TPU v7x, 32 devices: a whole 2x2x4 slice. The times are simulated.
32 devices in a mesh: band: 2 (over x), tm: 16 (over z, y, core).
Axes of the slice: x: 2, y: 2, z: 4, core: 2. Of those that a mesh axis runs over, the one named last changes fastest.
Arguments:
- voltages: bfloat16 [65536, 2048], P(('band', 'tm')), parts along dimension 0, may hold values from -6 to 6
- panel_map: int32 [2048], replicated, may hold values from 0 to 2047, each once
- block_list: int32 [16, 2], replicated, may hold values from 0 to 15, as said below
Outputs:
- visibilities: float32 [32, 2, 256, 128, 128], P('band', None, 'tm'), parts along dimension 0
There are 2 independent parts, one for each index of `band`. A program takes and returns all parts, laid end to end along the dimension named above; an argument that names none is the same for every part. Nothing has to cross between parts.
Inputs may be any that keep to these rules, and one draw needn't show every extreme that they name: `block_list`: each row is a pair of panel numbers; the list names exactly 8 distinct panels, among them panel 0 and panel 16 - 1, every one of them in its first column.
All inputs are finite; a program needn't handle non-finite values.
Results may differ from a plain program's by a relative error of at most 0.0064.
Values may be sent and summed in bfloat16 or wider, within the bound.
No kernel may reach another device: no remote copies, remote signals or barrier semaphores. Data moves between devices by JAX's collectives and lax.ppermute only.
A program may use at most 128 MiB of HBM per device.

v0:
```python
import jax
import jax.numpy as jnp
from jax import lax
from jax.sharding import PartitionSpec as P

CHANNELS = 256
TAPS = 4
PANEL = 128


def from_behind(block, axis, distance):
    devices = range(lax.axis_size(axis))
    route = [(i - distance, i) for i in devices if i - distance in devices]
    return lax.ppermute(block, axis, route)


def filter_taps(taps, frame):
    length = taps * frame
    place = jnp.arange(length).astype(jnp.float32)
    middle = (length - 1) / 2.0
    window = 0.5 - 0.5 * jnp.cos(2.0 * jnp.pi * (place + 0.5) / length)
    shape_h = jnp.sinc((place - middle) / frame) * window
    shape_h = shape_h / jnp.sqrt(jnp.sum(shape_h * shape_h))
    return shape_h.reshape(taps, frame).astype(jnp.float32)


def dft_table(channels):
    frame = 2 * channels
    rows_k = jnp.arange(channels, dtype=jnp.int32)[:, None]
    cols_n = jnp.arange(frame, dtype=jnp.int32)[None, :]
    phase = (rows_k * cols_n % frame).astype(jnp.float32) * (2.0 * jnp.pi / frame)
    return jnp.concatenate([jnp.cos(phase), -jnp.sin(phase)], axis=0).astype(jnp.bfloat16)


def body(voltages, panel_map, block_list):
    frame = 2 * CHANNELS
    spec_dev = voltages.shape[0] // frame
    groups = lax.axis_size("tm")
    band_dev = CHANNELS // groups
    panel_rows = panel_map.reshape(-1, PANEL)
    columns = panel_rows[block_list]
    width = voltages.shape[1]
    frames = voltages.reshape(spec_dev, frame, width)
    earlier = from_behind(frames[spec_dev - (TAPS - 1) :], "tm", 1)
    padded = jnp.concatenate([earlier, frames], axis=0)
    coeff = filter_taps(TAPS, frame)
    filtered = jnp.zeros((spec_dev, frame, width), jnp.float32)
    for tap in range(TAPS):
        filtered = filtered + coeff[tap][None, :, None] * padded[tap : tap + spec_dev].astype(
            jnp.float32
        )
    filtered = filtered.astype(jnp.bfloat16)
    table = dft_table(CHANNELS)
    spectra = jnp.einsum("kn,sni->ski", table, filtered, preferred_element_type=jnp.float32)
    spectra = spectra.astype(jnp.bfloat16).reshape(spec_dev, 2, groups, band_dev, width)
    data = lax.all_to_all(spectra, "tm", split_axis=2, concat_axis=0, tiled=True)[:, :, 0]
    total = data.shape[0]
    first = data[:, :, :, columns[:, 0]]
    second = data[:, :, :, columns[:, 1]]
    flipped = jnp.stack([first[:, 1], -first[:, 0]], axis=1)
    real_part = jnp.einsum("sckbi,sckbj->bkij", first, second, preferred_element_type=jnp.float32)
    imag_part = jnp.einsum("sckbi,sckbj->bkij", flipped, second, preferred_element_type=jnp.float32)
    return jnp.stack([real_part, imag_part], axis=1) / total


def solution(mesh):
    in_specs = (P(("band", "tm"), None), P(), P())
    out_specs = P("band", None, "tm", None, None)
    return jax.shard_map(body, mesh=mesh, in_specs=in_specs, out_specs=out_specs, check_vma=False)
```

profile of v0, /device:TPU:15, one launch (start us, length us, event | category | flops | bytes accessed | tf_op | source)
XLA Modules:
  0.0 472.7 jit_solution(12410593673535821267)
XLA Ops:
  0.0 0.0 copy-start
  0.0 6.6 %slice.44 = bf16[1536,2048]{1,0:T(8,128)(2,1)} slice(bf16[2048,2048]{1,0:T(8,128)(2,1)} %param.3), slice={[512:2048], [0:2048]} | slice | bytes 12582912 | tf_op jit(solution)/shard_map/slice | solution.py:44
  6.6 3.7 collective-permute-start
  10.3 0.6 multiply_reduce_fusion
  11.6 0.1 broadcast_divide_fusion
  11.6 2.2 negate_convert_fusion
  13.8 64.7 %collective-permute-done = bf16[3,512,2048]{2,1,0:T(8,128)(2,1)} collective-permute-done((bf16[3,512,2048]{2,1,0:T(8,128)(2,1)}, bf16[3,512,2048]{2,1,0:T(8,128)(2,1)}, u32[]{:S(2)}, u32[]{:S(2)}) %collective-permute-start) | collective-permute-done | bytes 6291488 | tf_op jit(solution)/shard_map/ppermute | solution.py:14
  78.5 17.1 %fusion.6 = bf16[4,2048,512]{1,2,0:T(8,128)(2,1)} fusion(bf16[4,512,2048]{2,1,0:T(8,128)(2,1)} %bitcast.51, bf16[3,512,2048]{2,1,0:T(8,128)(2,1)} %collective-permute-done, f32[512]{0:T(512)S(1)} %get-tuple-element.10, f32[512]{0:T(512)S(1)} %get-tuple-element.11, f32[512]{0:T(512)S(1)} %get-tuple-element.12, f32[512]{0:T(512)S(1)} %get-tuple-element.9, ...), kind=kOutput, calls=%fused_computation.18 | convolution fusion | flops 4388290560 | bytes 23601152 | tf_op jit(solution)/shard_map/kn,sni->ski/dot_general | solution.py:54
  95.6 0.0 copy-start.2
  95.6 8.3 %copy.7 = bf16[4,2,16,16,2048]{4,3,1,0,2:T(8,128)(2,1)} copy(bf16[4,2,16,16,2048]{4,3,2,1,0:T(8,128)(2,1)} %bitcast.50) | data formatting | bytes 16777216 | tf_op jit(solution)/shard_map/reshape | solution.py:55
  103.9 7.2 %all-to-all-start = ((bf16[4,2,16,16,2048]{4,3,1,0,2:T(8,128)(2,1)}), bf16[4,2,16,16,2048]{4,3,1,0,2:T(8,128)(2,1)}, u32[]{:S(2)}, u32[]{:S(2)}) async-start(bf16[4,2,16,16,2048]{4,3,1,0,2:T(8,128)(2,1)} %copy.7), calls=%async_computation | async-start | bytes 16777216 | tf_op jit(solution)/shard_map/all_to_all | solution.py:56
  111.1 0.0 copy-done.2
  111.1 0.1 copy.8
  111.2 0.1 reshape.85
  111.3 0.0 copy-done
  111.3 0.6 gather_fusion
  112.0 181.5 %all-to-all-done = bf16[4,2,16,16,2048]{4,3,1,0,2:T(8,128)(2,1)} async-done(((bf16[4,2,16,16,2048]{4,3,1,0,2:T(8,128)(2,1)}), bf16[4,2,16,16,2048]{4,3,1,0,2:T(8,128)(2,1)}, u32[]{:S(2)}, u32[]{:S(2)}) %all-to-all-start) | async-done | bytes 8388640 | tf_op jit(solution)/shard_map/all_to_all | solution.py:56
  293.5 26.8 %copy.9 = bf16[64,2,16,2048]{0,2,3,1:T(8,128)(2,1)} copy(bf16[64,2,16,2048]{3,2,1,0:T(8,128)(2,1)} %bitcast.7) | data formatting | bytes 16777216 | tf_op jit(solution)/shard_map/squeeze | solution.py:56
  320.3 25.9 %gather_fusion.2 = bf16[2048,64,2,16]{1,3,2,0:T(8,128)(2,1)} fusion(bf16[64,2,16,2048]{0,2,3,1:T(8,128)(2,1)} %copy.9, s32[2048]{0:T(1024)S(1)} %fusion.26), kind=kCustom, calls=%fused_computation.2 | custom fusion | bytes 16785408 | tf_op jit(solution)/shard_map/gather | solution.py:59
  346.2 25.9 %gather_fusion.1 = bf16[2048,64,2,16]{1,3,2,0:T(8,128)(2,1)} fusion(bf16[64,2,16,2048]{0,2,3,1:T(8,128)(2,1)} %copy.9, s32[2048]{0:T(1024)S(1)} %fusion.24), kind=kCustom, calls=%fused_computation.1 | custom fusion | bytes 16785408 | tf_op jit(solution)/shard_map/gather | solution.py:58
  372.0 21.0 %copy.11 = bf16[16,128,64,2,16]{1,2,3,4,0:T(8,128)(2,1)} copy(bf16[16,128,64,2,16]{2,4,3,1,0:T(8,128)(2,1)} %bitcast.49) | data formatting | bytes 16777216 | tf_op jit(solution)/shard_map/gather | solution.py:58
  393.1 21.1 %copy.15 = bf16[64,2,16,16,128]{4,0,1,2,3:T(8,128)(2,1)} copy(bf16[64,2,16,16,128]{0,2,1,4,3:T(8,128)(2,1)} %bitcast.48) | data formatting | bytes 16777216 | tf_op jit(solution)/shard_map/gather | solution.py:59
  414.1 5.8 %fusion.35 = (bf16[64,1,16,16,128]{4,0,1,2,3:T(8,128)(2,1)}, bf16[64,1,16,16,128]{4,0,1,2,3:T(8,128)(2,1)}) fusion(bf16[64,2,16,16,128]{4,0,1,2,3:T(8,128)(2,1)} %bitcast.47), kind=kLoop, calls=%fused_computation.71 | loop fusion | flops 2097152 | bytes 16777216 | tf_op jit(solution)/shard_map/slice | solution.py:60
  420.0 14.4 %convolution_bitcast_fusion.1 = f32[16,1,16,128,128]{4,3,2,0,1:T(8,128)} fusion(bf16[64,2,16,16,128]{4,0,1,2,3:T(8,128)(2,1)} %copy.15, bf16[16,128,64,2,16]{1,2,3,4,0:T(8,128)(2,1)} %copy.11), kind=kOutput, calls=%fused_computation.10 | convolution fusion | flops 1073741824 | bytes 33554432 | tf_op jit(solution)/shard_map/sckbi,sckbj->bkij/dot_general | solution.py:61
  434.3 14.9 %convolution_bitcast_fusion = f32[16,1,16,128,128]{4,3,2,0,1:T(8,128)} fusion(bf16[64,2,16,16,128]{4,0,1,2,3:T(8,128)(2,1)} %copy.15, bf16[64,1,16,16,128]{4,0,1,2,3:T(8,128)(2,1)} %get-tuple-element.6, bf16[64,1,16,16,128]{4,0,1,2,3:T(8,128)(2,1)} %get-tuple-element.5), kind=kOutput, calls=%fused_computation.9 | convolution fusion | flops 1077936128 | bytes 33554432 | tf_op jit(solution)/shard_map/sckbi,sckbj->bkij/dot_general | solution.py:62
  449.2 12.2 %maximum_multiply_fusion = f32[16,2,16,128,128]{4,3,2,0,1:T(8,128)S(1)} fusion(f32[16,1,16,128,128]{4,3,2,0,1:T(8,128)} %convolution_bitcast_fusion, f32[16,1,16,128,128]{4,3,2,0,1:T(8,128)} %convolution_bitcast_fusion.1), kind=kLoop, calls=%fused_computation.3 | loop fusion | flops 16777216 | bytes 67108864 | tf_op jit(solution)/shard_map/div | solution.py:63
  461.4 0.0 copy-start.1
  461.4 11.3 %copy.17 = f32[16,2,16,128,128]{4,3,2,1,0:T(8,128)} copy(f32[16,2,16,128,128]{4,3,2,0,1:T(8,128)S(1)} %maximum_multiply_fusion) | data formatting | bytes 67108864 | tf_op jit(solution)/shard_map/div | solution.py:63
  472.7 0.0 copy-done.1
  (6 shorter events, 0.0 us)
Async XLA Ops:
  0.0 111.3 %copy-start = (s32[2048]{0:T(1024)S(1)}, s32[2048]{0:T(1024)}, u32[]{:S(2)}) copy-start(s32[2048]{0:T(1024)} %param.4) | copy-start | bytes 24580
  6.6 71.9 %collective-permute-start = (bf16[3,512,2048]{2,1,0:T(8,128)(2,1)}, bf16[3,512,2048]{2,1,0:T(8,128)(2,1)}, u32[]{:S(2)}, u32[]{:S(2)}) collective-permute-start(bf16[3,512,2048]{2,1,0:T(8,128)(2,1)} %bitcast), channel_id=1, source_target_pairs={{0,1},{1,2},{2,3},{3,4},{4,5},{5,6},{6,7},{7,8},{8,9},{9,10},{10,1... | collective-permute-start | bytes 18874376 | tf_op jit(solution)/shard_map/ppermute | solution.py:14
  95.6 15.5 %copy-start.2 = (s32[16,2]{0,1:T(2,128)S(1)}, s32[16,2]{0,1:T(2,128)}, u32[]{:S(2)}) copy-start(s32[16,2]{0,1:T(2,128)} %param.5) | copy-start | bytes 388
  103.9 189.6 %all-to-all-start = ((bf16[4,2,16,16,2048]{4,3,1,0,2:T(8,128)(2,1)}), bf16[4,2,16,16,2048]{4,3,1,0,2:T(8,128)(2,1)}, u32[]{:S(2)}, u32[]{:S(2)}) async-start(bf16[4,2,16,16,2048]{4,3,1,0,2:T(8,128)(2,1)} %copy.7), calls=%async_computation | async-start | bytes 16777216 | tf_op jit(solution)/shard_map/all_to_all | solution.py:56
  461.4 11.3 %copy-start.1 = (s32[2048]{0:T(1024)S(1)}, s32[2048]{0:T(1024)}, u32[]{:S(2)}) copy-start(s32[2048]{0:T(1024)} %param.4) | copy-start | bytes 24580
where the time goes:
time: 474 us; the launch traced here: 473 us
  waiting for transfers between devices  246 us (52%)
  local copies, waits for them, and re-layouts  148 us (31%)
  matrix products  46.3 us (10%)
  other arithmetic  20.9 us (4%)
  starting transfers between devices  10.9 us (2%)
    all_to_all x1, waiting for transfers between devices, body(): lax.all_to_all(spectra, 'tm', split_axis=2, concat_axis=0, tiled=True)  182 us
    ppermute x1, waiting for transfers between devices, from_behind(): return lax.ppermute(block, axis, route)  64.7 us
    gather x2, local copies, waits for them, and re-layouts, body(): second = data[:, :, :, columns[:, 1]]  46.9 us
    gather x2, local copies, waits for them, and re-layouts, body(): first = data[:, :, :, columns[:, 0]]  46.9 us
    squeeze x1, local copies, waits for them, and re-layouts, body(): lax.all_to_all(spectra, 'tm', split_axis=2, concat_axis=0, tiled=True)  26.8 us
    dot_general x1, matrix products, body(): jnp.einsum('kn,sni->ski', table, filtered, preferred_element_type=jnp.flo...  17.1 us
    dot_general x1, matrix products, body(): jnp.einsum('sckbi,sckbj->bkij', flipped, second, preferred_element_type=j...  14.9 us
    dot_general x1, matrix products, body(): jnp.einsum('sckbi,sckbj->bkij', first, second, preferred_element_type=jnp...  14.4 us
  transfers between devices with their start and end apart: 2, of which 2 were waited for; matrix products, arithmetic and copies ran while one was open for 1% of the time, Pallas kernels for 0%

commit v1 on v0

v1 whole, which is shorter than its diff:
```python
import functools

import jax
import jax.numpy as jnp
import numpy as np
from jax import lax
from jax.experimental import pallas as pl
from jax.experimental.pallas import tpu as pltpu
from jax.sharding import PartitionSpec as P

CHANNELS = 256
TAPS = 4
PANEL = 128
USED = 8
FRAME = 2 * CHANNELS
WIDTH = USED * PANEL
ROWS = 16
LANES = 256


def from_behind(block, axis, distance):
    devices = range(lax.axis_size(axis))
    route = [(i - distance, i) for i in devices if i - distance in devices]
    return lax.ppermute(block, axis, route)


def filter_taps():
    length = TAPS * FRAME
    place = np.arange(length, dtype=np.float64)
    middle = (length - 1) / 2.0
    window = 0.5 - 0.5 * np.cos(2.0 * np.pi * (place + 0.5) / length)
    shape_h = np.sinc((place - middle) / FRAME) * window
    shape_h = shape_h / np.sqrt(np.sum(shape_h * shape_h))
    taps = shape_h.reshape(TAPS, FRAME, 1).astype(np.float32)
    return np.broadcast_to(taps, (TAPS, FRAME, PANEL)).copy()


def dft_table(groups, parts):
    own = CHANNELS // groups
    per = own // parts
    q, g, f, c = np.meshgrid(
        np.arange(parts), np.arange(groups), np.arange(per), np.arange(2), indexing="ij"
    )
    channel = (g * own + q * per + f).reshape(-1)
    imaginary = c.reshape(-1)
    phase = (channel[:, None] * np.arange(FRAME)[None, :] % FRAME) * (2.0 * np.pi / FRAME)
    table = np.where(imaginary[:, None] == 1, -np.sin(phase), np.cos(phase))
    return table.astype(np.float32).astype(jnp.bfloat16)


def row_orders():
    pairs = 256 // ROWS
    half = ROWS // 2
    table = np.zeros((512, 256), np.float32)
    for j in range(pairs):
        for f in range(half):
            row, col = f * pairs * 2 + j * 2, j * ROWS + f * 2
            table[row, col] = 1.0
            table[row + 1, col + 1] = 1.0
            table[256 + row, col + 1] = -1.0
            table[256 + row + 1, col] = 1.0
    return table.astype(jnp.bfloat16)


def named_panels(blocks):
    bits = jnp.int32(0)
    for b in range(blocks.shape[0]):
        bits = bits | (jnp.int32(1) << blocks[b, 0])
    return bits


def filtered_frame(taps_ref, frames, cols):
    total = None
    taps = [jnp.tile(taps_ref[t], (1, cols // PANEL)) for t in range(TAPS)]
    for t in range(TAPS):
        term = taps[t] * frames[t].astype(jnp.float32)
        total = term if total is None else total + term
    return total.astype(jnp.bfloat16)


def select_kernel(blocks, volts, inputs, taps, table, chosen, first, hot, panels):
    step = pl.program_id(0)
    groups, parts = first.shape[0], first.shape[1]

    @pl.when(step == 0)
    def _():
        bits = named_panels(blocks)
        count = jnp.int32(0)
        for p in range(inputs.shape[0]):
            panels[count] = p
            count = count + ((bits >> p) & 1)
        for j in range(USED):
            wanted = inputs[pl.ds(panels[j], 1), :]
            rows = lax.broadcasted_iota(jnp.int32, (volts.shape[2], PANEL), 0)
            hot[:, j * PANEL : (j + 1) * PANEL] = (rows == wanted).astype(jnp.float32).astype(
                jnp.bfloat16
            )

    @pl.loop(0, WIDTH // LANES)
    def _(k):
        cols = pl.ds(pl.multiple_of(k * LANES, LANES), LANES)
        chosen[step, :, cols] = jnp.dot(
            volts[0], hot[:, cols], preferred_element_type=jnp.float32
        ).astype(jnp.bfloat16)

    @pl.when(step == TAPS - 1)
    def _():
        @pl.loop(0, WIDTH // LANES)
        def _(k):
            cols = pl.ds(pl.multiple_of(k * LANES, LANES), LANES)
            frames = [chosen[t, :, cols] for t in range(TAPS)]
            spectrum = jnp.dot(
                table[...],
                filtered_frame(taps, frames, LANES),
                preferred_element_type=jnp.float32,
            ).astype(jnp.bfloat16)
            for q in range(parts):
                for g in range(groups):
                    at = (q * groups + g) * ROWS
                    first[g, q, :, cols] = spectrum[at : at + ROWS]


def select(block_list, panel_map, frames, taps, table, groups, parts):
    count, frame, width = frames.shape
    return pl.pallas_call(
        select_kernel,
        grid_spec=pltpu.PrefetchScalarGridSpec(
            num_scalar_prefetch=1,
            grid=(count,),
            in_specs=[
                pl.BlockSpec((1, frame, width), lambda s, blocks: (s, 0, 0)),
                pl.BlockSpec((width // PANEL, PANEL), lambda s, blocks: (0, 0)),
                pl.BlockSpec((TAPS, frame, PANEL), lambda s, blocks: (0, 0, 0)),
                pl.BlockSpec((frame, frame), lambda s, blocks: (0, 0)),
            ],
            out_specs=[
                pl.BlockSpec((count, frame, WIDTH), lambda s, blocks: (0, 0, 0)),
                pl.BlockSpec((groups, parts, ROWS, WIDTH), lambda s, blocks: (0, 0, 0, 0)),
            ],
            scratch_shapes=[
                pltpu.VMEM((width, WIDTH), jnp.bfloat16),
                pltpu.SMEM((width // PANEL + 1,), jnp.int32),
            ],
        ),
        out_shape=[
            jax.ShapeDtypeStruct((count, frame, WIDTH), jnp.bfloat16),
            jax.ShapeDtypeStruct((groups, parts, ROWS, WIDTH), jnp.bfloat16),
        ],
        compiler_params=pltpu.CompilerParams(vmem_limit_bytes=48 << 20),
        cost_estimate=pl.CostEstimate(
            flops=2 * count * frame * width * WIDTH, bytes_accessed=14 << 20, transcendentals=0
        ),
        name="select",
    )(block_list, frames, panel_map.reshape(-1, PANEL), taps, table)


def spectra_kernel(earlier, own, taps, table, *out):
    groups = out[0].shape[0]
    depth = TAPS - 1
    cols = earlier.shape[2]
    pool = [earlier[t] for t in range(depth)] + [own[t] for t in range(depth)]
    for s in range(depth):
        spectrum = jnp.dot(
            table[...],
            filtered_frame(taps, pool[s : s + TAPS], cols),
            preferred_element_type=jnp.float32,
        ).astype(jnp.bfloat16)
        for q, part in enumerate(out):
            for g in range(groups):
                at = (q * groups + g) * ROWS
                part[g, s] = spectrum[at : at + ROWS]


def later_spectra(earlier, chosen, taps, table, groups, parts):
    depth = TAPS - 1
    frame = chosen.shape[1]
    return pl.pallas_call(
        spectra_kernel,
        grid=(WIDTH // LANES,),
        in_specs=[
            pl.BlockSpec((depth, frame, LANES), lambda k: (0, 0, k)),
            pl.BlockSpec((depth, frame, LANES), lambda k: (0, 0, k)),
            pl.BlockSpec((TAPS, frame, PANEL), lambda k: (0, 0, 0)),
            pl.BlockSpec((frame, frame), lambda k: (0, 0)),
        ],
        out_specs=[pl.BlockSpec((groups, depth, ROWS, LANES), lambda k: (0, 0, 0, k))] * parts,
        out_shape=[jax.ShapeDtypeStruct((groups, depth, ROWS, WIDTH), jnp.bfloat16)] * parts,
        compiler_params=pltpu.CompilerParams(vmem_limit_bytes=32 << 20),
        cost_estimate=pl.CostEstimate(
            flops=2 * depth * frame * frame * WIDTH, bytes_accessed=10 << 20, transcendentals=0
        ),
        name="later_spectra",
    )(earlier, chosen, taps, table)


def correlate_kernel(scale, blocks, first, rest, orders, *refs):
    out, plain, turned, across = refs[-4:]
    step = pl.program_id(0)
    per = ROWS // 2
    keys = 512 // per
    lead = first.shape[0] * ROWS // 256
    total = lead + rest.shape[0] // 256

    @pl.when(step == 0)
    def _():
        for n in range(total):
            rows = (
                first[pl.ds(n * 256 // ROWS, 256 // ROWS), 0].reshape(256, WIDTH)
                if n < lead
                else rest[pl.ds((n - lead) * 256, 256)]
            )
            moved = jnp.dot(orders[...], rows, preferred_element_type=jnp.float32).astype(
                jnp.bfloat16
            )
            width = 256 // per
            for f in range(per):
                plain[f, n * width : (n + 1) * width] = moved[f * width : (f + 1) * width]
                turned[f, n * width : (n + 1) * width] = moved[
                    256 + f * width : 256 + (f + 1) * width
                ]

    across[...] = plain[step].T
    bits = named_panels(blocks)

    def place(panel):
        below = bits & ((jnp.int32(1) << panel) - 1)
        count = jnp.int32(0)
        for p in range(16):
            count = count + ((below >> p) & 1)
        return pl.multiple_of(count * PANEL, PANEL)

    for b in range(blocks.shape[0]):
        a, w = place(blocks[b, 0]), place(blocks[b, 1])
        left = across[pl.ds(a, PANEL), :]
        right = jnp.concatenate(
            [plain[step, :, pl.ds(w, PANEL)], turned[step, :, pl.ds(w, PANEL)]], axis=1
        )
        product = jnp.dot(left, right, preferred_element_type=jnp.float32) * scale
        out[b, 0, 0] = product[:, :PANEL]
        out[b, 1, 0] = product[:, PANEL:]


def correlate(block_list, first, rest, orders, part, shape, so_far):
    groups, parts = first.shape[0], first.shape[1]
    per = ROWS // 2
    keys = 2 * groups * TAPS
    rest = rest.reshape(-1, WIDTH)
    blocks = shape[0]
    operands = [block_list, first, rest, orders]
    in_specs = [
        pl.BlockSpec((groups, 1, ROWS, WIDTH), lambda s, blocks: (0, part, 0, 0)),
        pl.BlockSpec(rest.shape, lambda s, blocks: (0, 0)),
        pl.BlockSpec(orders.shape, lambda s, blocks: (0, 0)),
    ]
    aliases = {}
    if so_far is not None:
        aliases = {len(operands): 0}
        operands.append(so_far)
        in_specs.append(pl.BlockSpec(memory_space=pl.ANY))
    return pl.pallas_call(
        functools.partial(correlate_kernel, 1.0 / (groups * TAPS)),
        grid_spec=pltpu.PrefetchScalarGridSpec(
            num_scalar_prefetch=1,
            grid=(per,),
            in_specs=in_specs,
            out_specs=pl.BlockSpec(
                (blocks, 2, 1, PANEL, PANEL), lambda s, blocks: (0, 0, part * per + s, 0, 0)
            ),
            scratch_shapes=[
                pltpu.VMEM((per, keys, WIDTH), jnp.bfloat16),
                pltpu.VMEM((per, keys, WIDTH), jnp.bfloat16),
                pltpu.VMEM((WIDTH, keys), jnp.bfloat16),
            ],
        ),
        out_shape=jax.ShapeDtypeStruct(shape, jnp.float32),
        input_output_aliases=aliases,
        compiler_params=pltpu.CompilerParams(vmem_limit_bytes=48 << 20),
        cost_estimate=pl.CostEstimate(
            flops=4 * per * keys * PANEL * PANEL * blocks,
            bytes_accessed=18 << 20,
            transcendentals=0,
        ),
        name="correlate",
    )(*operands)


def body(voltages, panel_map, block_list):
    groups = lax.axis_size("tm")
    own = CHANNELS // groups
    parts = own * 2 // ROWS
    frames = voltages.reshape(-1, FRAME, voltages.shape[1])
    taps = filter_taps()
    table = dft_table(groups, parts)
    chosen, first = select(block_list, panel_map, frames, taps, table, groups, parts)
    earlier = from_behind(chosen[1:], "tm", 1)
    exchange = functools.partial(
        lax.all_to_all, axis_name="tm", split_axis=0, concat_axis=0, tiled=True
    )
    first = exchange(first)
    rest = later_spectra(earlier, chosen, taps, table, groups, parts)
    rest = [exchange(part) for part in rest]
    shape = (block_list.shape[0], 2, own, PANEL, PANEL)
    out = None
    for q in range(parts):
        out = correlate(block_list, first, rest[q], row_orders(), q, shape, out)
    return out


def solution(mesh):
    in_specs = (P(("band", "tm"), None), P(), P())
    out_specs = P("band", None, "tm", None, None)
    return jax.shard_map(body, mesh=mesh, in_specs=in_specs, out_specs=out_specs, check_vma=False)
```

time: 474 us -> 186 us (0.39)
  waiting for transfers between devices: 246 us -> 69.1 us
  local copies, waits for them, and re-layouts: 148 us -> 12.2 us
  Pallas kernels: 0 us -> 47.9 us
  matrix products: 46.3 us -> 0 us
  blocking collectives: 0 us -> 42.3 us
  other arithmetic: 20.9 us -> 0 us
    all_to_all x1 -> x2, waiting for transfers between devices: 182 us -> 25.5 us  [the longest x1 25.5 us: body(): rest = [exchange(part) for part in rest]]
    gather x5 -> x0, local copies, waits for them, and re-layouts: 94.4 us -> none  [the longest x2 46.9 us: body(): second = data[:, :, :, columns[:, 1]]]
    pallas_call x0 -> x4, Pallas kernels: none -> 47.9 us  [the longest x2 23 us: correlate(): pl.pallas_call(functools.partial(correlate_kernel, 1.0 / (groups * TAPS))...]
    dot_general x3 -> x0, matrix products: 46.3 us -> none  [the longest x1 17.1 us: body(): jnp.einsum('kn,sni->ski', table, filtered, preferred_element_type=jnp.flo...]
    all_to_all x0 -> x1, blocking collectives: none -> 42.3 us  [body(): rest = [exchange(part) for part in rest]]
    squeeze x1 -> x0, local copies, waits for them, and re-layouts: 26.8 us -> none  [body(): lax.all_to_all(spectra, 'tm', split_axis=2, concat_axis=0, tiled=True)]
    ppermute x1, waiting for transfers between devices: 64.7 us -> 43.5 us  [from_behind(): return lax.ppermute(block, axis, route)]
    div x2 -> x0, other arithmetic: 12.2 us -> none  [the longest x1 12.2 us: body(): return jnp.stack([real_part, imag_part], axis=1) / total]
  transfers between devices with their start and end apart: 2 -> 3, of which waited for: 2 -> 2; matrix products, arithmetic and copies ran while one was open for 1% -> 0% of each run, Pallas kernels for 0% -> 9%
where the time goes in v1:
time: 186 us; the launch traced here: 185 us
  waiting for transfers between devices  69.1 us (37%)
  Pallas kernels  47.9 us (26%)
  blocking collectives  42.3 us (23%)
  starting transfers between devices  13.8 us (7%)
  local copies, waits for them, and re-layouts  12.2 us (7%)
    ppermute x1, waiting for transfers between devices, from_behind(): return lax.ppermute(block, axis, route)  43.5 us
    all_to_all x1, blocking collectives, body(): rest = [exchange(part) for part in rest]  42.3 us
    all_to_all x1, waiting for transfers between devices, body(): rest = [exchange(part) for part in rest]  25.5 us
    pallas_call x2, Pallas kernels, correlate(): pl.pallas_call(functools.partial(correlate_kernel, 1.0 / (groups * TAPS))...  23 us
    pallas_call x1, Pallas kernels, select(): pl.pallas_call(select_kernel, grid_spec=pltpu.PrefetchScalarGridSpec(num_...  19.8 us
    unnamed x19, local copies, waits for them, and re-layouts  8.21 us
    pallas_call x1, Pallas kernels, later_spectra(): pl.pallas_call(spectra_kernel, grid=(WIDTH // LANES,), in_specs=[pl.Block...  5.14 us
    all_to_all x1, starting transfers between devices, body(): first = exchange(first)  5.05 us
  transfers between devices with their start and end apart: 3, of which 2 were waited for; matrix products, arithmetic and copies ran while one was open for 0% of the time, Pallas kernels for 9%

profile of v1, /device:TPU:15, one launch (start us, length us, event | category | flops | bytes accessed | tf_op | source)
XLA Modules:
  0.0 185.3 jit_solution(14176893001999425700)
XLA Ops:
  0.0 0.8 copy.11.blocks
  0.8 0.0 copy-start.4
  0.8 1.2 copy-done.4
  2.0 0.0 copy-start.6
  2.0 1.0 copy-done.6
  3.0 0.0 copy-start.8
  3.0 0.7 copy-done.8
  3.7 19.8 %select.1 = (bf16[4,512,1024]{2,1,0:T(8,128)(2,1)}, bf16[16,2,16,1024]{3,2,1,0:T(8,128)(2,1)}) custom-call(s32[16,2]{1,0:T(8,128)S(1)} %copy.11.blocks, bf16[4,512,2048]{2,1,0:T(8,128)(2,1)} %bitcast.6, s32[16,128]{1,0:T(8,128)S(1)} %bitcast.5, f32[4,512,128]{2,1,0:T(8,128)S(1)} %copy-done.4, bf16[512,512]{1,0:T(8,128)(2,1)S(1)} %copy-done.6), custom_call_target="tpu_custom_call" | custom-call | flops 8589934592 | bytes 14680064 | tf_op jit(solution)/shard_map/select/pallas_call | solution.py:125
  23.5 0.0 copy-start.5
  23.5 0.0 copy-start.7
  23.5 4.0 %slice.3 = bf16[3,512,1024]{2,1,0:T(8,128)(2,1)} slice(bf16[4,512,1024]{2,1,0:T(8,128)(2,1)} %get-tuple-element.10.own), slice={[1:4], [0:512], [0:1024]} | slice | bytes 6291456 | tf_op jit(solution)/shard_map/slice | solution.py:295
  27.5 3.7 %collective-permute-start = (bf16[3,512,1024]{2,1,0:T(8,128)(2,1)}, bf16[3,512,1024]{2,1,0:T(8,128)(2,1)}, u32[]{:S(2)}, u32[]{:S(2)}) collective-permute-start(bf16[3,512,1024]{2,1,0:T(8,128)(2,1)} %slice.3), channel_id=1, source_target_pairs={{0,1},{1,2},{2,3},{3,4},{4,5},{5,6},{6,7},{7,8},{8,9},{9,10},{10,1... | collective-permute-start | bytes 9437192 | tf_op jit(solution)/shard_map/ppermute | solution.py:24
  31.2 5.1 %all-to-all-start = ((bf16[16,2,16,1024]{3,2,1,0:T(8,128)(2,1)}), bf16[16,2,16,1024]{3,2,1,0:T(8,128)(2,1)S(1)}, u32[]{:S(2)}, u32[]{:S(2)}) async-start(bf16[16,2,16,1024]{3,2,1,0:T(8,128)(2,1)} %get-tuple-element.9), calls=%async_computation | async-start | bytes 2097152 | tf_op jit(solution)/shard_map/all_to_all | solution.py:299
  36.2 43.5 %collective-permute-done.earlier = bf16[3,512,1024]{2,1,0:T(8,128)(2,1)} collective-permute-done((bf16[3,512,1024]{2,1,0:T(8,128)(2,1)}, bf16[3,512,1024]{2,1,0:T(8,128)(2,1)}, u32[]{:S(2)}, u32[]{:S(2)}) %collective-permute-start) | collective-permute-done | bytes 3145760 | tf_op jit(solution)/shard_map/ppermute | solution.py:24
  79.8 0.0 copy-done.5
  79.8 0.0 copy-done.7
  79.8 0.0 copy-start
  79.8 2.2 %copy-done = bf16[4,512,1024]{2,1,0:T(8,128)(2,1)S(1)} copy-done((bf16[4,512,1024]{2,1,0:T(8,128)(2,1)S(1)}, bf16[4,512,1024]{2,1,0:T(8,128)(2,1)}, u32[]{:S(2)}) %copy-start) | copy-done | bytes 4194328
  82.0 5.1 %later_spectra.1 = (bf16[16,3,16,1024]{3,2,1,0:T(8,128)(2,1)S(1)}, bf16[16,3,16,1024]{3,2,1,0:T(8,128)(2,1)S(1)}) custom-call(bf16[3,512,1024]{2,1,0:T(8,128)(2,1)} %collective-permute-done.earlier, bf16[4,512,1024]{2,1,0:T(8,128)(2,1)S(1)} %copy-done, f32[4,512,128]{2,1,0:T(8,128)S(1)} %copy-done.5, bf16[512,512]{1,0:T(8,128)(2,1)S(1)} %copy-done.7), custom_call_target="tpu_custom_call" | custom-call | flops 1610612736 | bytes 10485760 | tf_op jit(solution)/shard_map/later_spectra/pallas_call | solution.py:177
  87.1 0.0 copy-start.1
  87.1 1.2 copy-done.1
  88.3 0.0 copy-start.2
  88.3 1.1 copy-done.2
  89.4 0.0 all-to-all-done.first
  89.4 0.0 copy-start.3
  89.4 42.3 %all_to_all.15 = bf16[16,3,16,1024]{3,2,1,0:T(8,128)(2,1)S(1)} all-to-all(bf16[16,3,16,1024]{3,2,1,0:T(8,128)(2,1)} %copy-done.2), channel_id=1, replica_groups=mesh['band'=2,'tm'=16] {'tm'}, dimensions={0} | all-to-all | bytes 3145728 | tf_op jit(solution)/shard_map/all_to_all | solution.py:301
  131.8 5.0 %all-to-all-start.1 = ((bf16[16,3,16,1024]{3,2,1,0:T(8,128)(2,1)}), bf16[16,3,16,1024]{3,2,1,0:T(8,128)(2,1)}, u32[]{:S(2)}, u32[]{:S(2)}) async-start(bf16[16,3,16,1024]{3,2,1,0:T(8,128)(2,1)} %copy-done.1), calls=%async_computation.1 | async-start | bytes 3145728 | tf_op jit(solution)/shard_map/all_to_all | solution.py:301
  136.8 0.0 copy-done.3
  136.8 10.8 %correlate.2.refs_0_ = f32[16,2,16,128,128]{4,3,2,1,0:T(8,128)} custom-call(s32[16,2]{1,0:T(8,128)S(1)} %copy.11.blocks, bf16[16,2,16,1024]{3,2,1,0:T(8,128)(2,1)S(1)} %all-to-all-done.first, bf16[768,1024]{1,0:T(8,128)(2,1)S(1)} %bitcast.4, bf16[512,256]{1,0:T(8,128)(2,1)S(1)} %copy-done.3), custom_call_target="tpu_custom_call" | custom-call | flops 1073741824 | bytes 18874368 | tf_op jit(solution)/shard_map/correlate/pallas_call | solution.py:260
  147.6 25.5 %all-to-all-done.1 = bf16[16,3,16,1024]{3,2,1,0:T(8,128)(2,1)} async-done(((bf16[16,3,16,1024]{3,2,1,0:T(8,128)(2,1)}), bf16[16,3,16,1024]{3,2,1,0:T(8,128)(2,1)}, u32[]{:S(2)}, u32[]{:S(2)}) %all-to-all-start.1) | async-done | bytes 1572896 | tf_op jit(solution)/shard_map/all_to_all | solution.py:301
  173.1 12.2 %correlate.3 = f32[16,2,16,128,128]{4,3,2,1,0:T(8,128)} custom-call(s32[16,2]{1,0:T(8,128)S(1)} %copy.11.blocks, bf16[16,2,16,1024]{3,2,1,0:T(8,128)(2,1)S(1)} %all-to-all-done.first, bf16[768,1024]{1,0:T(8,128)(2,1)} %bitcast.2.rest, bf16[512,256]{1,0:T(8,128)(2,1)S(1)} %copy-done.3, ...), custom_call_target="tpu_custom_call", output_to_operand_aliasing={{}: (4, {})} | custom-call | flops 1073741824 | bytes 18874368 | tf_op jit(solution)/shard_map/correlate/pallas_call | solution.py:260
Async XLA Ops:
  0.8 1.2 copy-start.4
  2.0 1.0 copy-start.6
  3.0 0.7 copy-start.8
  23.5 56.3 %copy-start.5 = (f32[4,512,128]{2,1,0:T(8,128)S(1)}, f32[4,512,128]{2,1,0:T(8,128)}, u32[]{:S(2)}) copy-start(f32[4,512,128]{2,1,0:T(8,128)} %constant.6.clone.taps) | copy-start | bytes 3145732
  23.5 56.3 %copy-start.7 = (bf16[512,512]{1,0:T(8,128)(2,1)S(1)}, bf16[512,512]{1,0:T(8,128)(2,1)}, u32[]{:S(2)}) copy-start(bf16[512,512]{1,0:T(8,128)(2,1)} %constant.7.clone.table) | copy-start | bytes 1572868
  27.5 52.3 %collective-permute-start = (bf16[3,512,1024]{2,1,0:T(8,128)(2,1)}, bf16[3,512,1024]{2,1,0:T(8,128)(2,1)}, u32[]{:S(2)}, u32[]{:S(2)}) collective-permute-start(bf16[3,512,1024]{2,1,0:T(8,128)(2,1)} %slice.3), channel_id=1, source_target_pairs={{0,1},{1,2},{2,3},{3,4},{4,5},{5,6},{6,7},{7,8},{8,9},{9,10},{10,1... | collective-permute-start | bytes 9437192 | tf_op jit(solution)/shard_map/ppermute | solution.py:24
  31.2 58.2 %all-to-all-start = ((bf16[16,2,16,1024]{3,2,1,0:T(8,128)(2,1)}), bf16[16,2,16,1024]{3,2,1,0:T(8,128)(2,1)S(1)}, u32[]{:S(2)}, u32[]{:S(2)}) async-start(bf16[16,2,16,1024]{3,2,1,0:T(8,128)(2,1)} %get-tuple-element.9), calls=%async_computation | async-start | bytes 2097152 | tf_op jit(solution)/shard_map/all_to_all | solution.py:299
  79.8 2.2 %copy-start = (bf16[4,512,1024]{2,1,0:T(8,128)(2,1)S(1)}, bf16[4,512,1024]{2,1,0:T(8,128)(2,1)}, u32[]{:S(2)}) copy-start(bf16[4,512,1024]{2,1,0:T(8,128)(2,1)} %get-tuple-element.10.own) | copy-start | bytes 12582916
  87.1 1.2 copy-start.1
  88.3 1.1 copy-start.2
  89.4 47.4 %copy-start.3 = (bf16[512,256]{1,0:T(8,128)(2,1)S(1)}, bf16[512,256]{1,0:T(8,128)(2,1)}, u32[]{:S(2)}) copy-start(bf16[512,256]{1,0:T(8,128)(2,1)} %constant.8.clone.orders) | copy-start | bytes 786436
  131.8 41.3 %all-to-all-start.1 = ((bf16[16,3,16,1024]{3,2,1,0:T(8,128)(2,1)}), bf16[16,3,16,1024]{3,2,1,0:T(8,128)(2,1)}, u32[]{:S(2)}, u32[]{:S(2)}) async-start(bf16[16,3,16,1024]{3,2,1,0:T(8,128)(2,1)} %copy-done.1), calls=%async_computation.1 | async-start | bytes 3145728 | tf_op jit(solution)/shard_map/all_to_all | solution.py:301

commit v2 on v1

v2 whole, which is shorter than its diff:
```python
import functools

import jax
import jax.numpy as jnp
import numpy as np
from jax import lax
from jax.experimental import pallas as pl
from jax.experimental.pallas import tpu as pltpu
from jax.sharding import PartitionSpec as P

CHANNELS = 256
TAPS = 4
PANEL = 128
USED = 8
FRAME = 2 * CHANNELS
WIDTH = USED * PANEL
ROWS = 16
LANES = 256
VMEM = 60 << 20


def pin(*arrays):
    return [pltpu.with_memory_space_constraint(array, pltpu.HBM) for array in arrays]


def shifted(block, axis, distance, around):
    count = lax.axis_size(axis)
    route = [(i, (i + distance) % count) for i in range(count) if around or 0 <= i + distance < count]
    return lax.ppermute(block, axis, route)


def filter_taps():
    length = TAPS * FRAME
    place = np.arange(length, dtype=np.float64)
    middle = (length - 1) / 2.0
    window = 0.5 - 0.5 * np.cos(2.0 * np.pi * (place + 0.5) / length)
    shape_h = np.sinc((place - middle) / FRAME) * window
    shape_h = shape_h / np.sqrt(np.sum(shape_h * shape_h))
    taps = shape_h.reshape(TAPS, FRAME, 1).astype(np.float32)
    return np.broadcast_to(taps, (TAPS, FRAME, PANEL)).copy()


def dft_table(groups, parts):
    own = CHANNELS // groups
    per = own // parts
    q, g, f, c = np.meshgrid(
        np.arange(parts), np.arange(groups), np.arange(per), np.arange(2), indexing="ij"
    )
    channel = (g * own + q * per + f).reshape(-1)
    imaginary = c.reshape(-1)
    phase = (channel[:, None] * np.arange(FRAME)[None, :] % FRAME) * (2.0 * np.pi / FRAME)
    table = np.where(imaginary[:, None] == 1, -np.sin(phase), np.cos(phase))
    return table.astype(np.float32).astype(jnp.bfloat16)


def row_orders():
    pairs = 256 // ROWS
    half = ROWS // 2
    table = np.zeros((512, 256), np.float32)
    for j in range(pairs):
        for f in range(half):
            row, col = f * pairs * 2 + j * 2, j * ROWS + f * 2
            table[row, col] = 1.0
            table[row + 1, col + 1] = 1.0
            table[256 + row, col + 1] = -1.0
            table[256 + row + 1, col] = 1.0
    return table.astype(jnp.bfloat16)


def named_panels(blocks):
    bits = jnp.int32(0)
    for b in range(blocks.shape[1]):
        bits = bits | (jnp.int32(1) << blocks[0, b])
    return bits


def filtered_frame(taps_ref, frames, cols):
    total = None
    taps = [jnp.tile(taps_ref[t], (1, cols // PANEL)) for t in range(TAPS)]
    for t in range(TAPS):
        term = taps[t] * frames[t].astype(jnp.float32)
        total = term if total is None else total + term
    return total.astype(jnp.bfloat16)


def select_kernel(
    blocks, frames, inputs, up, down, hot_out, places, volts, names, hot, chosen, panels, come, go
):
    depth = TAPS - 1
    half = WIDTH // 2
    listed = pltpu.make_async_copy(inputs, names, come.at[TAPS])
    listed.start()
    order = list(range(1, TAPS)) + [0]
    arrive = {t: pltpu.make_async_copy(frames.at[t], volts.at[t], come.at[t]) for t in order}
    for t in order:
        arrive[t].start()
    bits = named_panels(blocks)
    count = jnp.int32(0)
    slots = TAPS * USED
    for p in range(inputs.shape[0]):
        panels[count] = p
        panels[slots + p] = count * PANEL
        count = count + ((bits >> p) & 1)
    listed.wait()
    sends = []

    def send(source, target):
        sends.append(pltpu.make_async_copy(source, target, go.at[len(sends)]))
        sends[-1].start()

    for side in range(2):
        for j in range(side * USED // 2, (side + 1) * USED // 2):
            wanted = names[pl.ds(panels[j], 1), :]
            rows = lax.broadcasted_iota(jnp.int32, (volts.shape[2], PANEL), 0)
            hot[:, j * PANEL : (j + 1) * PANEL] = (
                (rows == wanted).astype(jnp.float32).astype(jnp.bfloat16)
            )
        cols = slice(side * half, (side + 1) * half)
        send(hot.at[:, cols], hot_out.at[:, cols])
        for t in range(depth):
            source = t if side else t + 1
            if source in arrive:
                arrive.pop(source).wait()
            chosen[t, :, cols] = jnp.dot(
                volts[source], hot[:, cols], preferred_element_type=jnp.float32
            ).astype(jnp.bfloat16)
            send(chosen.at[t, :, cols], (down if side else up).at[t])
    for i in range(2):
        for b in range(blocks.shape[1]):
            places[i, b] = panels[slots + blocks[i, b]]
    for copy in sends:
        copy.wait()


def select(block_list, panel_map, frames):
    count, frame, width = frames.shape
    depth = TAPS - 1
    anywhere = pl.BlockSpec(memory_space=pl.ANY)
    return pl.pallas_call(
        select_kernel,
        grid_spec=pltpu.PrefetchScalarGridSpec(
            num_scalar_prefetch=1,
            grid=(1,),
            in_specs=[anywhere] * 2,
            out_specs=[anywhere] * 3 + [pl.BlockSpec(memory_space=pltpu.SMEM)],
            scratch_shapes=[
                pltpu.VMEM((count, frame, width), jnp.bfloat16),
                pltpu.VMEM((width // PANEL, PANEL), jnp.int32),
                pltpu.VMEM((width, WIDTH), jnp.bfloat16),
                pltpu.VMEM((depth, frame, WIDTH), jnp.bfloat16),
                pltpu.SMEM((TAPS * USED + width // PANEL,), jnp.int32),
                pltpu.SemaphoreType.DMA((1 + TAPS,)),
                pltpu.SemaphoreType.DMA((2 + 2 * depth,)),
            ],
        ),
        out_shape=[
            pltpu.HBM((depth, frame, WIDTH // 2), jnp.bfloat16),
            pltpu.HBM((depth, frame, WIDTH // 2), jnp.bfloat16),
            pltpu.HBM((width, WIDTH), jnp.bfloat16),
            jax.ShapeDtypeStruct(block_list.shape, jnp.int32),
        ],
        compiler_params=pltpu.CompilerParams(vmem_limit_bytes=VMEM),
        cost_estimate=pl.CostEstimate(
            flops=3 * frame * width * WIDTH * 2, bytes_accessed=15 << 20, transcendentals=0
        ),
        name="select",
    )(block_list, *pin(frames, panel_map.reshape(-1, PANEL)))


def first_kernel(frame, hot, up, down, taps, table, extra, first):
    groups, parts = first.shape[0], first.shape[1]
    depth = TAPS - 1
    chosen = jnp.dot(frame[0], hot[...], preferred_element_type=jnp.float32).astype(jnp.bfloat16)
    extra[...] = chosen

    def spectra(frames):
        spectrum = jnp.dot(
            table[...],
            filtered_frame(taps, frames, chosen.shape[1]),
            preferred_element_type=jnp.float32,
        ).astype(jnp.bfloat16)
        for q in range(parts):
            for g in range(groups):
                at = (q * groups + g) * ROWS
                first[g, q] = spectrum[at : at + ROWS]

    left = pl.program_id(0) < pl.num_programs(0) // 2

    @pl.when(left)
    def _():
        spectra([extra[...]] + [up[t] for t in range(depth)])

    @pl.when(jnp.logical_not(left))
    def _():
        spectra([down[t] for t in range(depth)] + [extra[...]])


def first_spectra(frames, hot, up, down, taps, table, groups, parts):
    count, frame, width = frames.shape
    depth = TAPS - 1
    tiles = WIDTH // LANES // 2
    return pl.pallas_call(
        first_kernel,
        grid=(2 * tiles,),
        in_specs=[
            pl.BlockSpec((1, frame, width), lambda k: (k // tiles * (TAPS - 1), 0, 0)),
            pl.BlockSpec((width, LANES), lambda k: (0, k)),
            pl.BlockSpec((depth, frame, LANES), lambda k: (0, 0, jnp.minimum(k, tiles - 1))),
            pl.BlockSpec((depth, frame, LANES), lambda k: (0, 0, jnp.maximum(k - tiles, 0))),
            pl.BlockSpec((TAPS, frame, PANEL), lambda k: (0, 0, 0)),
            pl.BlockSpec((frame, frame), lambda k: (0, 0)),
        ],
        out_specs=[
            pl.BlockSpec((frame, LANES), lambda k: (0, k)),
            pl.BlockSpec((groups, parts, ROWS, LANES), lambda k: (0, 0, 0, k)),
        ],
        out_shape=[
            pltpu.HBM((frame, WIDTH), jnp.bfloat16),
            pltpu.HBM((groups, parts, ROWS, WIDTH), jnp.bfloat16),
        ],
        compiler_params=pltpu.CompilerParams(vmem_limit_bytes=VMEM // 2),
        cost_estimate=pl.CostEstimate(
            flops=2 * frame * (width + frame) * WIDTH, bytes_accessed=14 << 20, transcendentals=0
        ),
        name="first_spectra",
    )(*pin(frames, hot, up, down, taps, table))


def spectra_kernel(earlier, later, up, down, extra, taps, table, *out):
    groups = out[0].shape[0]
    depth = TAPS - 1
    cols = extra.shape[1]

    def spectra(pool):
        for s in range(depth):
            spectrum = jnp.dot(
                table[...],
                filtered_frame(taps, pool[s : s + TAPS], cols),
                preferred_element_type=jnp.float32,
            ).astype(jnp.bfloat16)
            for q, part in enumerate(out):
                for g in range(groups):
                    at = (q * groups + g) * ROWS
                    part[g, s] = spectrum[at : at + ROWS]

    left = pl.program_id(0) < pl.num_programs(0) // 2

    @pl.when(left)
    def _():
        own = [extra[...]] + [up[t] for t in range(depth - 1)]
        spectra([earlier[t] for t in range(depth)] + own)

    @pl.when(jnp.logical_not(left))
    def _():
        last = lax.axis_index("tm") == lax.axis_size("tm") - 1
        own = [down[t] for t in range(1, depth)] + [extra[...]]
        own = [jnp.where(last, jnp.zeros_like(frame), frame) for frame in own]
        spectra(own + [later[t] for t in range(depth)])


def later_spectra(earlier, later, up, down, extra, taps, table, groups, parts):
    depth = TAPS - 1
    frame = extra.shape[0]
    tiles = WIDTH // LANES // 2
    before = pl.BlockSpec((depth, frame, LANES), lambda k: (0, 0, jnp.minimum(k, tiles - 1)))
    after = pl.BlockSpec((depth, frame, LANES), lambda k: (0, 0, jnp.maximum(k - tiles, 0)))
    return pl.pallas_call(
        spectra_kernel,
        grid=(2 * tiles,),
        in_specs=[
            before,
            after,
            before,
            after,
            pl.BlockSpec((frame, LANES), lambda k: (0, k)),
            pl.BlockSpec((TAPS, frame, PANEL), lambda k: (0, 0, 0)),
            pl.BlockSpec((frame, frame), lambda k: (0, 0)),
        ],
        out_specs=[pl.BlockSpec((groups, depth, ROWS, LANES), lambda k: (0, 0, 0, k))] * parts,
        out_shape=[pltpu.HBM((groups, depth, ROWS, WIDTH), jnp.bfloat16)] * parts,
        compiler_params=pltpu.CompilerParams(vmem_limit_bytes=VMEM // 2),
        cost_estimate=pl.CostEstimate(
            flops=200 * depth * frame * frame * WIDTH, bytes_accessed=10 << 20, transcendentals=0
        ),
        name="later_spectra",
    )(earlier, later, *pin(up, down, extra, taps, table))


def same_frames(rest, n):
    behind = (TAPS - 1) * ROWS
    half, at = WIDTH // 2, n * 256
    left = rest[at : at + 256, :half]
    if n == 0:
        right = jnp.concatenate(
            [rest[rest.shape[0] - behind :, half:], rest[: 256 - behind, half:]], axis=0
        )
    else:
        right = rest[at - behind : at + 256 - behind, half:]
    return jnp.concatenate([left, right], axis=1)


def correlate_kernel(scale, blocks, first, rest, orders, *refs):
    out, plain, turned, across = refs[-4:]
    step = pl.program_id(0)
    per = ROWS // 2
    keys = 512 // per
    lead = first.shape[0] * ROWS // 256
    total = lead + rest.shape[0] // 256

    @pl.when(step == 0)
    def _():
        for n in range(total):
            rows = (
                first[pl.ds(n * 256 // ROWS, 256 // ROWS), 0].reshape(256, WIDTH)
                if n < lead
                else same_frames(rest, n - lead)
            )
            moved = jnp.dot(orders[...], rows, preferred_element_type=jnp.float32).astype(
                jnp.bfloat16
            )
            width = 256 // per
            for f in range(per):
                plain[f, n * width : (n + 1) * width] = moved[f * width : (f + 1) * width]
                turned[f, n * width : (n + 1) * width] = moved[
                    256 + f * width : 256 + (f + 1) * width
                ]

    across[...] = plain[step].T
    for b in range(blocks.shape[1]):
        a, w = (pl.multiple_of(blocks[i, b], PANEL) for i in range(2))
        left = across[pl.ds(a, PANEL), :]
        right = jnp.concatenate(
            [plain[step, :, pl.ds(w, PANEL)], turned[step, :, pl.ds(w, PANEL)]], axis=1
        )
        product = jnp.dot(left, right, preferred_element_type=jnp.float32) * scale
        out[b, 0, 0] = product[:, :PANEL]
        out[b, 1, 0] = product[:, PANEL:]


def correlate(places, first, rest, orders, part, shape, so_far):
    groups, parts = first.shape[0], first.shape[1]
    per = ROWS // 2
    keys = 2 * groups * TAPS
    rest = rest.reshape(-1, WIDTH)
    blocks = shape[0]
    operands = [places, first, rest, orders]
    in_specs = [
        pl.BlockSpec((groups, 1, ROWS, WIDTH), lambda s, blocks: (0, part, 0, 0)),
        pl.BlockSpec(rest.shape, lambda s, blocks: (0, 0)),
        pl.BlockSpec(orders.shape, lambda s, blocks: (0, 0)),
    ]
    aliases = {}
    if so_far is not None:
        aliases = {len(operands): 0}
        operands.append(so_far)
        in_specs.append(pl.BlockSpec(memory_space=pl.ANY))
    return pl.pallas_call(
        functools.partial(correlate_kernel, 1.0 / (groups * TAPS)),
        grid_spec=pltpu.PrefetchScalarGridSpec(
            num_scalar_prefetch=1,
            grid=(per,),
            in_specs=in_specs,
            out_specs=pl.BlockSpec(
                (blocks, 2, 1, PANEL, PANEL), lambda s, blocks: (0, 0, part * per + s, 0, 0)
            ),
            scratch_shapes=[
                pltpu.VMEM((per, keys, WIDTH), jnp.bfloat16),
                pltpu.VMEM((per, keys, WIDTH), jnp.bfloat16),
                pltpu.VMEM((WIDTH, keys), jnp.bfloat16),
            ],
        ),
        out_shape=jax.ShapeDtypeStruct(shape, jnp.float32),
        input_output_aliases=aliases,
        compiler_params=pltpu.CompilerParams(vmem_limit_bytes=VMEM // 2),
        cost_estimate=pl.CostEstimate(
            flops=4 * per * keys * PANEL * PANEL * blocks,
            bytes_accessed=18 << 20,
            transcendentals=0,
        ),
        name="correlate",
    )(*operands)


def body(voltages, panel_map, block_list):
    groups = lax.axis_size("tm")
    own = CHANNELS // groups
    parts = own * 2 // ROWS
    frames = voltages.reshape(-1, FRAME, voltages.shape[1])
    taps = filter_taps()
    table = dft_table(groups, parts)
    block_list = block_list.T
    up, down, hot, places = select(block_list, panel_map, frames)
    earlier = shifted(up, "tm", 1, False)
    later = shifted(down, "tm", -1, True)
    extra, first = first_spectra(frames, hot, up, down, taps, table, groups, parts)
    exchange = functools.partial(
        lax.all_to_all, axis_name="tm", split_axis=0, concat_axis=0, tiled=True
    )
    first = exchange(first)
    rest = later_spectra(earlier, later, up, down, extra, taps, table, groups, parts)
    rest = [exchange(part) for part in rest]
    shape = (block_list.shape[1], 2, own, PANEL, PANEL)
    out = None
    for q in range(parts):
        out = correlate(places, first, rest[q], row_orders(), q, shape, out)
    return out


def solution(mesh):
    in_specs = (P(("band", "tm"), None), P(), P())
    out_specs = P("band", None, "tm", None, None)
    return jax.shard_map(body, mesh=mesh, in_specs=in_specs, out_specs=out_specs, check_vma=False)
```

time: 186 us -> 163 us (0.88)
  waiting for transfers between devices: 69.1 us -> 48.2 us
  local copies, waits for them, and re-layouts: 12.2 us -> 0.01 us
  blocking collectives: 42.3 us -> 48.2 us
  Pallas kernels: 47.9 us -> 51 us
    ppermute x1 -> x2, waiting for transfers between devices: 43.5 us -> 12.1 us  [shifted(): return lax.ppermute(block, axis, route)]
    pallas_call x1 -> x2, Pallas kernels: 5.14 us -> 16.7 us  [the longest x1 9.7 us: first_spectra(): pl.pallas_call(first_kernel, grid=(2 * tiles,), in_specs=[pl.BlockSpec((1...]
    all_to_all x1, waiting for transfers between devices: 0.01 us -> 11.1 us  [body(): first = exchange(first)]
    unnamed x19 -> x4, local copies, waits for them, and re-layouts: 8.21 us -> 0.01 us
    pallas_call x1, Pallas kernels: 19.8 us -> 12.1 us  [select(): pl.pallas_call(select_kernel, grid_spec=pltpu.PrefetchScalarGridSpec(num_...]
    all_to_all x1, blocking collectives: 42.3 us -> 48.2 us  [body(): rest = [exchange(part) for part in rest]]
    slice x1 -> x0, local copies, waits for them, and re-layouts: 3.95 us -> none  [body(): earlier = from_behind(chosen[1:], 'tm', 1)]
    ppermute x1 -> x2, starting transfers between devices: 3.7 us -> 3.77 us  [shifted(): return lax.ppermute(block, axis, route)]
  transfers between devices with their start and end apart: 3 -> 4, of which waited for: 2 -> 4; matrix products, arithmetic and copies ran while one was open for 0% -> 0% of each run, Pallas kernels for 9% -> 17%
where the time goes in v2:
time: 163 us
  Pallas kernels  51 us (31%)
  waiting for transfers between devices  48.2 us (30%)
  blocking collectives  48.2 us (30%)
  starting transfers between devices  15.4 us (9%)
    all_to_all x1, blocking collectives, body(): rest = [exchange(part) for part in rest]  48.2 us
    all_to_all x1, waiting for transfers between devices, body(): rest = [exchange(part) for part in rest]  25.1 us
    pallas_call x2, Pallas kernels, correlate(): pl.pallas_call(functools.partial(correlate_kernel, 1.0 / (groups * TAPS))...  22.2 us
    pallas_call x1, Pallas kernels, select(): pl.pallas_call(select_kernel, grid_spec=pltpu.PrefetchScalarGridSpec(num_...  12.1 us
    ppermute x2, waiting for transfers between devices, shifted(): return lax.ppermute(block, axis, route)  12.1 us
    all_to_all x1, waiting for transfers between devices, body(): first = exchange(first)  11.1 us
    pallas_call x1, Pallas kernels, first_spectra(): pl.pallas_call(first_kernel, grid=(2 * tiles,), in_specs=[pl.BlockSpec((1...  9.7 us
    pallas_call x1, Pallas kernels, later_spectra(): pl.pallas_call(spectra_kernel, grid=(2 * tiles,), in_specs=[before, after...  7.02 us
  transfers between devices with their start and end apart: 4, of which 4 were waited for; matrix products, arithmetic and copies ran while one was open for 0% of the time, Pallas kernels for 17%

profile of v2, /device:TPU:15, one launch (start us, length us, event | category | flops | bytes accessed | tf_op | source)
XLA Modules:
  0.0 162.9 jit_solution(10215649492880439085)
XLA Ops:
  0.0 12.1 %select.1 = (bf16[3,512,512]{2,1,0:T(8,128)(2,1)}, bf16[3,512,512]{2,1,0:T(8,128)(2,1)}, bf16[2048,1024]{1,0:T(8,128)(2,1)}, s32[2,16]{1,0:T(2,128)}) custom-call(s32[2,16]{1,0:T(2,128)} %bitcast.10, bf16[4,512,2048]{2,1,0:T(8,128)(2,1)} %bitcast.7, s32[16,128]{1,0:T(8,128)} %bitcast.9), custom_call_target="tpu_custom_call" | custom-call | flops 6442450944 | bytes 15728640 | tf_op jit(solution)/shard_map/select/pallas_call | solution.py:139
  12.1 3.7 %collective-permute-start = (bf16[3,512,512]{2,1,0:T(8,128)(2,1)}, bf16[3,512,512]{2,1,0:T(8,128)(2,1)S(1)}, u32[]{:S(2)}, u32[]{:S(2)}) collective-permute-start(bf16[3,512,512]{2,1,0:T(8,128)(2,1)} %get-tuple-element.15.up), channel_id=1, source_target_pairs={{0,1},{1,2},{2,3},{3,4},{4,5},{5,6},{6,7},{7,8},{8,9},{9,10},{10,1... | collective-permute-start | bytes 4718600 | tf_op jit(solution)/shard_map/ppermute | solution.py:29
  15.9 0.1 collective-permute-start.1
  15.9 9.7 %first_spectra.1 = (bf16[512,1024]{1,0:T(8,128)(2,1)}, bf16[16,2,16,1024]{3,2,1,0:T(8,128)(2,1)}) custom-call(bf16[4,512,2048]{2,1,0:T(8,128)(2,1)} %bitcast.8, bf16[2048,1024]{1,0:T(8,128)(2,1)} %get-tuple-element.14.hot, bf16[3,512,512]{2,1,0:T(8,128)(2,1)} %get-tuple-element.15.up, bf16[3,512,512]{2,1,0:T(8,128)(2,1)} %get-tuple-element.16.down, ...), custom_call_target="tpu_custom_call" | custom-call | flops 2684354560 | bytes 14680064 | tf_op jit(solution)/shard_map/first_spectra/pallas_call | solution.py:202
  25.6 6.5 %all-to-all-start = ((bf16[16,2,16,1024]{3,2,1,0:T(8,128)(2,1)}), bf16[16,2,16,1024]{3,2,1,0:T(8,128)(2,1)}, u32[]{:S(2)}, u32[]{:S(2)}) async-start(bf16[16,2,16,1024]{3,2,1,0:T(8,128)(2,1)} %get-tuple-element.17), calls=%async_computation | async-start | bytes 2097152 | tf_op jit(solution)/shard_map/all_to_all | solution.py:399
  32.1 1.5 collective-permute-done.earlier
  33.6 10.6 %collective-permute-done.1.later = bf16[3,512,512]{2,1,0:T(8,128)(2,1)S(1)} collective-permute-done((bf16[3,512,512]{2,1,0:T(8,128)(2,1)}, bf16[3,512,512]{2,1,0:T(8,128)(2,1)S(1)}, u32[]{:S(2)}, u32[]{:S(2)}) %collective-permute-start.1) | collective-permute-done | bytes 1572896 | tf_op jit(solution)/shard_map/ppermute | solution.py:29
  44.2 7.0 %later_spectra.1 = (bf16[16,3,16,1024]{3,2,1,0:T(8,128)(2,1)}, bf16[16,3,16,1024]{3,2,1,0:T(8,128)(2,1)}) custom-call(bf16[3,512,512]{2,1,0:T(8,128)(2,1)S(1)} %collective-permute-done.earlier, bf16[3,512,512]{2,1,0:T(8,128)(2,1)S(1)} %collective-permute-done.1.later, bf16[3,512,512]{2,1,0:T(8,128)(2,1)} %get-tuple-element.15.up, ...), custom_call_target="tpu_custom_call" | custom-call | flops 161061273600 | bytes 10485760 | tf_op jit(solution)/shard_map/later_spectra/pallas_call | solution.py:267
  51.2 11.1 %all-to-all-done.first = bf16[16,2,16,1024]{3,2,1,0:T(8,128)(2,1)} async-done(((bf16[16,2,16,1024]{3,2,1,0:T(8,128)(2,1)}), bf16[16,2,16,1024]{3,2,1,0:T(8,128)(2,1)}, u32[]{:S(2)}, u32[]{:S(2)}) %all-to-all-start) | async-done | bytes 1048608 | tf_op jit(solution)/shard_map/all_to_all | solution.py:399
  62.3 48.2 %all_to_all.15 = bf16[16,3,16,1024]{3,2,1,0:T(8,128)(2,1)S(1)} all-to-all(bf16[16,3,16,1024]{3,2,1,0:T(8,128)(2,1)} %get-tuple-element.20), channel_id=1, replica_groups=mesh['band'=2,'tm'=16] {'tm'}, dimensions={0} | all-to-all | bytes 3145728 | tf_op jit(solution)/shard_map/all_to_all | solution.py:401
  110.5 0.0 copy-start
  110.5 0.0 copy-start.1
  110.5 5.2 %all-to-all-start.1 = ((bf16[16,3,16,1024]{3,2,1,0:T(8,128)(2,1)}), bf16[16,3,16,1024]{3,2,1,0:T(8,128)(2,1)S(1)}, u32[]{:S(2)}, u32[]{:S(2)}) async-start(bf16[16,3,16,1024]{3,2,1,0:T(8,128)(2,1)} %get-tuple-element.19), calls=%async_computation.1 | async-start | bytes 3145728 | tf_op jit(solution)/shard_map/all_to_all | solution.py:401
  115.6 0.0 copy-done
  115.6 0.0 copy-done.1
  115.6 11.1 %correlate.2.refs_0_ = f32[16,2,16,128,128]{4,3,2,1,0:T(8,128)} custom-call(s32[2,16]{1,0:T(2,128)S(1)} %copy-done.1, bf16[16,2,16,1024]{3,2,1,0:T(8,128)(2,1)} %all-to-all-done.first, bf16[768,1024]{1,0:T(8,128)(2,1)S(1)} %bitcast.6, bf16[512,256]{1,0:T(8,128)(2,1)S(1)} %copy-done), custom_call_target="tpu_custom_call" | custom-call | flops 1073741824 | bytes 18874368 | tf_op jit(solution)/shard_map/correlate/pallas_call | solution.py:357
  126.7 25.1 %all-to-all-done.1 = bf16[16,3,16,1024]{3,2,1,0:T(8,128)(2,1)S(1)} async-done(((bf16[16,3,16,1024]{3,2,1,0:T(8,128)(2,1)}), bf16[16,3,16,1024]{3,2,1,0:T(8,128)(2,1)S(1)}, u32[]{:S(2)}, u32[]{:S(2)}) %all-to-all-start.1) | async-done | bytes 1572896 | tf_op jit(solution)/shard_map/all_to_all | solution.py:401
  151.8 11.1 %correlate.3 = f32[16,2,16,128,128]{4,3,2,1,0:T(8,128)} custom-call(s32[2,16]{1,0:T(2,128)S(1)} %copy-done.1, bf16[16,2,16,1024]{3,2,1,0:T(8,128)(2,1)} %all-to-all-done.first, bf16[768,1024]{1,0:T(8,128)(2,1)S(1)} %bitcast.5, bf16[512,256]{1,0:T(8,128)(2,1)S(1)} %copy-done, f32[16,2,16,128,128]{4,3,2,1,0:T(8,128)} %correlate.2.refs_0_), custom_call_target="tpu_custom_call", output_to_operand_aliasing={{}: (4, {})} | custom-call | flops 1073741824 | bytes 18874368 | tf_op jit(solution)/shard_map/correlate/pallas_call | solution.py:357
Async XLA Ops:
  12.1 21.4 %collective-permute-start = (bf16[3,512,512]{2,1,0:T(8,128)(2,1)}, bf16[3,512,512]{2,1,0:T(8,128)(2,1)S(1)}, u32[]{:S(2)}, u32[]{:S(2)}) collective-permute-start(bf16[3,512,512]{2,1,0:T(8,128)(2,1)} %get-tuple-element.15.up), channel_id=1, source_target_pairs={{0,1},{1,2},{2,3},{3,4},{4,5},{5,6},{6,7},{7,8},{8,9},{9,10},{10,1... | collective-permute-start | bytes 4718600 | tf_op jit(solution)/shard_map/ppermute | solution.py:29
  15.9 28.3 %collective-permute-start.1 = (bf16[3,512,512]{2,1,0:T(8,128)(2,1)}, bf16[3,512,512]{2,1,0:T(8,128)(2,1)S(1)}, u32[]{:S(2)}, u32[]{:S(2)}) collective-permute-start(bf16[3,512,512]{2,1,0:T(8,128)(2,1)} %get-tuple-element.16.down), channel_id=1, source_target_pairs={{0,15},{1,0},{2,1},{3,2},{4,3},{5,4},{6,5},{7,6},{8,7},{9,8},{10,9... | collective-permute-start | bytes 4718600 | tf_op jit(solution)/shard_map/ppermute | solution.py:29
  25.6 36.6 %all-to-all-start = ((bf16[16,2,16,1024]{3,2,1,0:T(8,128)(2,1)}), bf16[16,2,16,1024]{3,2,1,0:T(8,128)(2,1)}, u32[]{:S(2)}, u32[]{:S(2)}) async-start(bf16[16,2,16,1024]{3,2,1,0:T(8,128)(2,1)} %get-tuple-element.17), calls=%async_computation | async-start | bytes 2097152 | tf_op jit(solution)/shard_map/all_to_all | solution.py:399
  110.5 5.2 %copy-start = (bf16[512,256]{1,0:T(8,128)(2,1)S(1)}, bf16[512,256]{1,0:T(8,128)(2,1)}, u32[]{:S(2)}) copy-start(bf16[512,256]{1,0:T(8,128)(2,1)} %constant.8.clone.orders) | copy-start | bytes 786436
  110.5 5.2 %copy-start.1 = (s32[2,16]{1,0:T(2,128)S(1)}, s32[2,16]{1,0:T(2,128)}, u32[]{:S(2)}) copy-start(s32[2,16]{1,0:T(2,128)} %get-tuple-element.13.blocks) | copy-start | bytes 388
  110.5 41.4 %all-to-all-start.1 = ((bf16[16,3,16,1024]{3,2,1,0:T(8,128)(2,1)}), bf16[16,3,16,1024]{3,2,1,0:T(8,128)(2,1)S(1)}, u32[]{:S(2)}, u32[]{:S(2)}) async-start(bf16[16,3,16,1024]{3,2,1,0:T(8,128)(2,1)} %get-tuple-element.19), calls=%async_computation.1 | async-start | bytes 3145728 | tf_op jit(solution)/shard_map/all_to_all | solution.py:401

commit v3 on v2

v3 whole, which is shorter than its diff:
```python
import functools

import jax
import jax.numpy as jnp
import numpy as np
from jax import lax
from jax.experimental import pallas as pl
from jax.experimental.pallas import tpu as pltpu
from jax.sharding import PartitionSpec as P

CHANNELS = 256
TAPS = 4
PANEL = 128
USED = 8
FRAME = 2 * CHANNELS
WIDTH = USED * PANEL
ROWS = 16
LANES = 256
VMEM = 60 << 20


def pin(*arrays):
    return [pltpu.with_memory_space_constraint(array, pltpu.HBM) for array in arrays]


def shifted(block, axis, distance, around):
    count = lax.axis_size(axis)
    route = [(i, (i + distance) % count) for i in range(count) if around or 0 <= i + distance < count]
    return lax.ppermute(block, axis, route)


def filter_taps():
    length = TAPS * FRAME
    place = np.arange(length, dtype=np.float64)
    middle = (length - 1) / 2.0
    window = 0.5 - 0.5 * np.cos(2.0 * np.pi * (place + 0.5) / length)
    shape_h = np.sinc((place - middle) / FRAME) * window
    shape_h = shape_h / np.sqrt(np.sum(shape_h * shape_h))
    taps = shape_h.reshape(TAPS, FRAME, 1).astype(np.float32)
    return np.broadcast_to(taps, (TAPS, FRAME, PANEL)).copy()


def dft_table(groups, parts):
    own = CHANNELS // groups
    per = own // parts
    q, g, f, c = np.meshgrid(
        np.arange(parts), np.arange(groups), np.arange(per), np.arange(2), indexing="ij"
    )
    channel = (g * own + q * per + f).reshape(-1)
    imaginary = c.reshape(-1)
    phase = (channel[:, None] * np.arange(FRAME)[None, :] % FRAME) * (2.0 * np.pi / FRAME)
    table = np.where(imaginary[:, None] == 1, -np.sin(phase), np.cos(phase))
    return table.astype(np.float32).astype(jnp.bfloat16)


def row_orders():
    pairs = 256 // ROWS
    half = ROWS // 2
    table = np.zeros((512, 256), np.float32)
    for j in range(pairs):
        for f in range(half):
            row, col = f * pairs * 2 + j * 2, j * ROWS + f * 2
            table[row, col] = 1.0
            table[row + 1, col + 1] = 1.0
            table[256 + row, col + 1] = -1.0
            table[256 + row + 1, col] = 1.0
    return table.astype(jnp.bfloat16)


def named_panels(blocks):
    bits = jnp.int32(0)
    for b in range(blocks.shape[1]):
        bits = bits | (jnp.int32(1) << blocks[0, b])
    return bits


def filtered_frame(taps_ref, frames, cols):
    total = None
    taps = [jnp.tile(taps_ref[t], (1, cols // PANEL)) for t in range(TAPS)]
    for t in range(TAPS):
        term = taps[t] * frames[t].astype(jnp.float32)
        total = term if total is None else total + term
    return total.astype(jnp.bfloat16)


def select_kernel(side, blocks, frames, inputs, taps, table, *refs):
    halo, extra, first, places = refs[-14:-10]
    volts, names, weights, matrix, hot, chosen, spectra, panels, come, go = refs[-10:]
    groups, parts = first.shape[0], first.shape[1]
    half = WIDTH // 2
    order = [(t + 1 - side) % TAPS for t in range(TAPS)]
    listed = pltpu.make_async_copy(inputs, names, come.at[TAPS])
    listed.start()
    arrive = [pltpu.make_async_copy(frames.at[t], volts.at[t], come.at[t]) for t in order]
    arrive.append(pltpu.make_async_copy(taps, weights, come.at[TAPS + 1]))
    arrive.append(pltpu.make_async_copy(table, matrix, come.at[TAPS + 2]))
    for copy in arrive:
        copy.start()
    bits = named_panels(blocks)
    count = jnp.int32(0)
    slots = TAPS * USED
    for p in range(inputs.shape[0]):
        panels[count] = p
        panels[slots + p] = count * PANEL
        count = count + ((bits >> p) & 1)
    listed.wait()
    for j in range(USED // 2):
        wanted = names[pl.ds(panels[side * USED // 2 + j], 1), :]
        rows = lax.broadcasted_iota(jnp.int32, (volts.shape[2], PANEL), 0)
        hot[:, j * PANEL : (j + 1) * PANEL] = (
            (rows == wanted).astype(jnp.float32).astype(jnp.bfloat16)
        )
    sends = []

    def send(source, target):
        sends.append(pltpu.make_async_copy(source, target, go.at[len(sends)]))
        sends[-1].start()

    for k, t in enumerate(order):
        arrive[k].wait()
        chosen[t] = jnp.dot(volts[t], hot[...], preferred_element_type=jnp.float32).astype(
            jnp.bfloat16
        )
        send(chosen.at[t], halo.at[k] if k < TAPS - 1 else extra)
    arrive[TAPS].wait()
    arrive[TAPS + 1].wait()
    for k in range(half // LANES):
        cols = slice(k * LANES, (k + 1) * LANES)
        spectrum = jnp.dot(
            matrix[...],
            filtered_frame(weights, [chosen[t, :, cols] for t in range(TAPS)], LANES),
            preferred_element_type=jnp.float32,
        ).astype(jnp.bfloat16)
        for q in range(parts):
            for g in range(groups):
                at = (q * groups + g) * ROWS
                spectra[g, q, :, cols] = spectrum[at : at + ROWS]
    send(spectra, first.at[:, :, :, side * half : (side + 1) * half])
    for i in range(2):
        for b in range(blocks.shape[1]):
            places[i, b] = panels[slots + blocks[i, b]]
    for copy in sends:
        copy.wait()


def select(side, block_list, panel_map, frames, taps, table, groups, parts, so_far):
    count, frame, width = frames.shape
    depth = TAPS - 1
    half = WIDTH // 2
    anywhere = pl.BlockSpec(memory_space=pl.ANY)
    operands = [block_list, *pin(frames, panel_map.reshape(-1, PANEL), taps, table)]
    aliases = {}
    if so_far is not None:
        aliases = {len(operands): 2}
        operands.append(so_far)
    return pl.pallas_call(
        functools.partial(select_kernel, side),
        grid_spec=pltpu.PrefetchScalarGridSpec(
            num_scalar_prefetch=1,
            grid=(1,),
            in_specs=[anywhere] * (len(operands) - 1),
            out_specs=[anywhere] * 3 + [pl.BlockSpec(memory_space=pltpu.SMEM)],
            scratch_shapes=[
                pltpu.VMEM((count, frame, width), jnp.bfloat16),
                pltpu.VMEM((width // PANEL, PANEL), jnp.int32),
                pltpu.VMEM(taps.shape, jnp.float32),
                pltpu.VMEM(table.shape, jnp.bfloat16),
                pltpu.VMEM((width, half), jnp.bfloat16),
                pltpu.VMEM((count, frame, half), jnp.bfloat16),
                pltpu.VMEM((groups, parts, ROWS, half), jnp.bfloat16),
                pltpu.SMEM((TAPS * USED + width // PANEL,), jnp.int32),
                pltpu.SemaphoreType.DMA((3 + TAPS,)),
                pltpu.SemaphoreType.DMA((1 + TAPS,)),
            ],
        ),
        out_shape=[
            pltpu.HBM((depth, frame, half), jnp.bfloat16),
            pltpu.HBM((frame, half), jnp.bfloat16),
            pltpu.HBM((groups, parts, ROWS, WIDTH), jnp.bfloat16),
            jax.ShapeDtypeStruct(block_list.shape, jnp.int32),
        ],
        input_output_aliases=aliases,
        compiler_params=pltpu.CompilerParams(vmem_limit_bytes=VMEM),
        cost_estimate=pl.CostEstimate(
            flops=count * frame * width * WIDTH, bytes_accessed=12 << 20, transcendentals=0
        ),
        name="select",
    )(*operands)


def spectra_kernel(earlier, later, up, down, first, last, taps, table, *out):
    groups = out[0].shape[0]
    depth = TAPS - 1
    cols = first.shape[1]

    def spectra(pool):
        for s in range(depth):
            spectrum = jnp.dot(
                table[...],
                filtered_frame(taps, pool[s : s + TAPS], cols),
                preferred_element_type=jnp.float32,
            ).astype(jnp.bfloat16)
            for q, part in enumerate(out):
                for g in range(groups):
                    at = (q * groups + g) * ROWS
                    part[g, s] = spectrum[at : at + ROWS]

    left = pl.program_id(0) < pl.num_programs(0) // 2

    @pl.when(left)
    def _():
        own = [first[...]] + [up[t] for t in range(depth - 1)]
        spectra([earlier[t] for t in range(depth)] + own)

    @pl.when(jnp.logical_not(left))
    def _():
        ends = lax.axis_index("tm") == lax.axis_size("tm") - 1
        own = [down[t] for t in range(1, depth)] + [last[...]]
        own = [jnp.where(ends, jnp.zeros_like(frame), frame) for frame in own]
        spectra(own + [later[t] for t in range(depth)])


def later_spectra(earlier, later, up, down, first, last, taps, table, groups, parts):
    depth = TAPS - 1
    frame = first.shape[0]
    tiles = WIDTH // LANES // 2
    before = pl.BlockSpec((depth, frame, LANES), lambda k: (0, 0, jnp.minimum(k, tiles - 1)))
    after = pl.BlockSpec((depth, frame, LANES), lambda k: (0, 0, jnp.maximum(k - tiles, 0)))
    return pl.pallas_call(
        spectra_kernel,
        grid=(2 * tiles,),
        in_specs=[
            before,
            after,
            before,
            after,
            pl.BlockSpec((frame, LANES), lambda k: (0, jnp.minimum(k, tiles - 1))),
            pl.BlockSpec((frame, LANES), lambda k: (0, jnp.maximum(k - tiles, 0))),
            pl.BlockSpec((TAPS, frame, PANEL), lambda k: (0, 0, 0)),
            pl.BlockSpec((frame, frame), lambda k: (0, 0)),
        ],
        out_specs=[pl.BlockSpec((groups, depth, ROWS, LANES), lambda k: (0, 0, 0, k))] * parts,
        out_shape=[pltpu.HBM((groups, depth, ROWS, WIDTH), jnp.bfloat16)] * parts,
        compiler_params=pltpu.CompilerParams(vmem_limit_bytes=VMEM // 2),
        cost_estimate=pl.CostEstimate(
            flops=200 * depth * frame * frame * WIDTH, bytes_accessed=10 << 20, transcendentals=0
        ),
        name="later_spectra",
    )(earlier, later, *pin(up, down, first, last, taps, table))


def same_frames(rest, n, cols):
    behind = (TAPS - 1) * ROWS
    at = n * 256
    if cols.start < WIDTH // 2:
        return rest[at : at + 256, cols]
    if n == 0:
        return jnp.concatenate(
            [rest[rest.shape[0] - behind :, cols], rest[: 256 - behind, cols]], axis=0
        )
    return rest[at - behind : at + 256 - behind, cols]


def correlate_kernel(scale, part, blocks, first, rest, orders, *refs):
    out, plain, turned, across, made, go = refs[-6:]
    per = ROWS // 2
    lead = first.shape[0] * ROWS // 256
    total = lead + rest.shape[0] // 256
    width = 256 // per
    for n in range(total):
        for k in range(WIDTH // LANES):
            cols = slice(k * LANES, (k + 1) * LANES)
            if n < lead:
                rows = first[n * 256 // ROWS : (n + 1) * 256 // ROWS, part, :, cols]
                rows = rows.reshape(256, LANES)
            else:
                rows = same_frames(rest, n - lead, cols)
            moved = jnp.dot(orders[...], rows, preferred_element_type=jnp.float32)
            moved = moved.astype(jnp.bfloat16)
            for f in range(per):
                at = f * width
                plain[f, n * width : (n + 1) * width, cols] = moved[at : at + width]
                turned[f, n * width : (n + 1) * width, cols] = moved[256 + at : 256 + at + width]

    def sending(f):
        return pltpu.make_async_copy(made.at[f], out.at[:, :, part * per + f], go.at[f])

    @pl.loop(0, per)
    def _(f):
        across[...] = plain[f].T
        for b in range(blocks.shape[1]):
            a, w = (pl.multiple_of(blocks[i, b], PANEL) for i in range(2))
            left = across[pl.ds(a, PANEL), :]
            right = jnp.concatenate(
                [plain[f, :, pl.ds(w, PANEL)], turned[f, :, pl.ds(w, PANEL)]], axis=1
            )
            product = jnp.dot(left, right, preferred_element_type=jnp.float32) * scale
            made[f, b, 0] = product[:, :PANEL]
            made[f, b, 1] = product[:, PANEL:]
        sending(f).start()

    @pl.loop(0, per)
    def _(f):
        sending(f).wait()


def correlate(places, first, rest, orders, part, shape, so_far):
    groups = first.shape[0]
    per = ROWS // 2
    keys = 2 * groups * TAPS
    rest = rest.reshape(-1, WIDTH)
    blocks = shape[0]
    operands = [places, first, rest, *pin(orders)]
    in_specs = [
        pl.BlockSpec(memory_space=pltpu.VMEM),
        pl.BlockSpec(memory_space=pltpu.VMEM),
        pl.BlockSpec(orders.shape, lambda s, blocks: (0, 0)),
    ]
    aliases = {}
    if so_far is not None:
        aliases = {len(operands): 0}
        operands.append(so_far)
        in_specs.append(pl.BlockSpec(memory_space=pl.ANY))
    return pl.pallas_call(
        functools.partial(correlate_kernel, 1.0 / (groups * TAPS), part),
        grid_spec=pltpu.PrefetchScalarGridSpec(
            num_scalar_prefetch=1,
            grid=(1,),
            in_specs=in_specs,
            out_specs=pl.BlockSpec(memory_space=pl.ANY),
            scratch_shapes=[
                pltpu.VMEM((per, keys, WIDTH), jnp.bfloat16),
                pltpu.VMEM((per, keys, WIDTH), jnp.bfloat16),
                pltpu.VMEM((WIDTH, keys), jnp.bfloat16),
                pltpu.VMEM((per, blocks, 2, PANEL, PANEL), jnp.float32),
                pltpu.SemaphoreType.DMA((per,)),
            ],
        ),
        out_shape=pltpu.HBM(shape, jnp.float32),
        input_output_aliases=aliases,
        compiler_params=pltpu.CompilerParams(vmem_limit_bytes=VMEM // 2),
        cost_estimate=pl.CostEstimate(
            flops=4 * per * keys * PANEL * PANEL * blocks,
            bytes_accessed=18 << 20,
            transcendentals=0,
        ),
        name="correlate",
    )(*operands)


def body(voltages, panel_map, block_list):
    groups = lax.axis_size("tm")
    own = CHANNELS // groups
    parts = own * 2 // ROWS
    frames = voltages.reshape(-1, FRAME, voltages.shape[1])
    taps = filter_taps()
    table = dft_table(groups, parts)
    block_list = block_list.T
    half = functools.partial(
        select, block_list=block_list, panel_map=panel_map, frames=frames, taps=taps,
        table=table, groups=groups, parts=parts,
    )
    up, left, first, places = half(0, so_far=None)
    earlier = shifted(up, "tm", 1, False)
    down, right, first, _ = half(1, so_far=first)
    later = shifted(down, "tm", -1, True)
    exchange = functools.partial(
        lax.all_to_all, axis_name="tm", split_axis=0, concat_axis=0, tiled=True
    )
    first = exchange(first)
    rest = later_spectra(earlier, later, up, down, left, right, taps, table, groups, parts)
    rest = [exchange(part) for part in rest]
    shape = (block_list.shape[1], 2, own, PANEL, PANEL)
    out = None
    for q in range(parts):
        out = correlate(places, first, rest[q], row_orders(), q, shape, out)
    return out


def solution(mesh):
    in_specs = (P(("band", "tm"), None), P(), P())
    out_specs = P("band", None, "tm", None, None)
    return jax.shard_map(body, mesh=mesh, in_specs=in_specs, out_specs=out_specs, check_vma=False)
```

time: 163 us -> 160 us (0.982)
  waiting for transfers between devices: 48.2 us -> 58 us
  blocking collectives: 48.2 us -> 40.4 us
  Pallas kernels: 51 us -> 45.2 us
    ppermute x2, waiting for transfers between devices: 12.1 us -> 31.4 us  [shifted(): return lax.ppermute(block, axis, route)]
    all_to_all x1, waiting for transfers between devices: 11.1 us -> 0.01 us  [body(): first = exchange(first)]
    all_to_all x1, blocking collectives: 48.2 us -> 40.4 us  [body(): rest = [exchange(part) for part in rest]]
    pallas_call x4, Pallas kernels: 44 us -> 38.1 us  [the longest x2 19.1 us: correlate(): pl.pallas_call(functools.partial(correlate_kernel, 1.0 / (groups * TAPS),...]
  transfers between devices with their start and end apart: 4 -> 4, of which waited for: 4 -> 3; matrix products, arithmetic and copies ran while one was open for 0% -> 0% of each run, Pallas kernels for 17% -> 16%
where the time goes in v3:
time: 160 us; the launch traced here: 159 us
  waiting for transfers between devices  58 us (36%)
  Pallas kernels  45.2 us (28%)
  blocking collectives  40.4 us (25%)
  starting transfers between devices  15.4 us (10%)
    all_to_all x1, blocking collectives, body(): rest = [exchange(part) for part in rest]  40.4 us
    ppermute x2, waiting for transfers between devices, shifted(): return lax.ppermute(block, axis, route)  31.4 us
    all_to_all x1, waiting for transfers between devices, body(): rest = [exchange(part) for part in rest]  26.6 us
    pallas_call x2, Pallas kernels, correlate(): pl.pallas_call(functools.partial(correlate_kernel, 1.0 / (groups * TAPS),...  19.1 us
    pallas_call x2, Pallas kernels, select(): pl.pallas_call(functools.partial(select_kernel, side), grid_spec=pltpu.Pr...  19 us
    pallas_call x1, Pallas kernels, later_spectra(): pl.pallas_call(spectra_kernel, grid=(2 * tiles,), in_specs=[before, after...  7.09 us
    all_to_all x1, starting transfers between devices, body(): first = exchange(first)  6.48 us
    all_to_all x1, starting transfers between devices, body(): rest = [exchange(part) for part in rest]  5.18 us
  transfers between devices with their start and end apart: 4, of which 3 were waited for; matrix products, arithmetic and copies ran while one was open for 0% of the time, Pallas kernels for 16%

profile of v3, /device:TPU:15, one launch (start us, length us, event | category | flops | bytes accessed | tf_op | source)
XLA Modules:
  0.0 159.2 jit_solution(14708593950029949600)
XLA Ops:
  0.0 9.5 %select.2 = (bf16[3,512,512]{2,1,0:T(8,128)(2,1)}, bf16[512,512]{1,0:T(8,128)(2,1)}, bf16[16,2,16,1024]{3,2,1,0:T(8,128)(2,1)}, s32[2,16]{1,0:T(2,128)}) custom-call(s32[2,16]{1,0:T(2,128)} %bitcast.11, bf16[4,512,2048]{2,1,0:T(8,128)(2,1)} %bitcast.7, s32[16,128]{1,0:T(8,128)} %bitcast.9, f32[4,512,128]{2,1,0:T(8,128)} %constant.6.clone.taps, ...), custom_call_target="tpu_custom_call" | custom-call | flops 4294967296 | bytes 12582912 | tf_op jit(solution)/shard_map/select/pallas_call | solution.py:156
  9.5 3.7 %collective-permute-start = (bf16[3,512,512]{2,1,0:T(8,128)(2,1)}, bf16[3,512,512]{2,1,0:T(8,128)(2,1)S(1)}, u32[]{:S(2)}, u32[]{:S(2)}) collective-permute-start(bf16[3,512,512]{2,1,0:T(8,128)(2,1)} %get-tuple-element.17.up), channel_id=1, source_target_pairs={{0,1},{1,2},{2,3},{3,4},{4,5},{5,6},{6,7},{7,8},{8,9},{9,10},{10,1... | collective-permute-start | bytes 4718600 | tf_op jit(solution)/shard_map/ppermute | solution.py:29
  13.2 9.5 %select.3 = (bf16[3,512,512]{2,1,0:T(8,128)(2,1)}, bf16[512,512]{1,0:T(8,128)(2,1)}, bf16[16,2,16,1024]{3,2,1,0:T(8,128)(2,1)}, s32[2,16]{1,0:T(2,128)}) custom-call(s32[2,16]{1,0:T(2,128)} %bitcast.12, bf16[4,512,2048]{2,1,0:T(8,128)(2,1)} %bitcast.8, s32[16,128]{1,0:T(8,128)} %bitcast.10, ...), custom_call_target="tpu_custom_call", output_to_operand_aliasing={{2}: (5, {})} | custom-call | flops 4294967296 | bytes 12582912 | tf_op jit(solution)/shard_map/select/pallas_call | solution.py:156
  22.7 0.1 collective-permute-start.1
  22.8 6.5 %all-to-all-start = ((bf16[16,2,16,1024]{3,2,1,0:T(8,128)(2,1)}), bf16[16,2,16,1024]{3,2,1,0:T(8,128)(2,1)}, u32[]{:S(2)}, u32[]{:S(2)}) async-start(bf16[16,2,16,1024]{3,2,1,0:T(8,128)(2,1)} %get-tuple-element.16), calls=%async_computation | async-start | bytes 2097152 | tf_op jit(solution)/shard_map/all_to_all | solution.py:370
  29.3 1.8 %collective-permute-done.earlier = bf16[3,512,512]{2,1,0:T(8,128)(2,1)S(1)} collective-permute-done((bf16[3,512,512]{2,1,0:T(8,128)(2,1)}, bf16[3,512,512]{2,1,0:T(8,128)(2,1)S(1)}, u32[]{:S(2)}, u32[]{:S(2)}) %collective-permute-start) | collective-permute-done | bytes 1572896 | tf_op jit(solution)/shard_map/ppermute | solution.py:29
  31.1 29.5 %collective-permute-done.1.later = bf16[3,512,512]{2,1,0:T(8,128)(2,1)S(1)} collective-permute-done((bf16[3,512,512]{2,1,0:T(8,128)(2,1)}, bf16[3,512,512]{2,1,0:T(8,128)(2,1)S(1)}, u32[]{:S(2)}, u32[]{:S(2)}) %collective-permute-start.1) | collective-permute-done | bytes 1572896 | tf_op jit(solution)/shard_map/ppermute | solution.py:29
  60.6 7.1 %later_spectra.1 = (bf16[16,3,16,1024]{3,2,1,0:T(8,128)(2,1)}, bf16[16,3,16,1024]{3,2,1,0:T(8,128)(2,1)}) custom-call(bf16[3,512,512]{2,1,0:T(8,128)(2,1)S(1)} %collective-permute-done.earlier, bf16[3,512,512]{2,1,0:T(8,128)(2,1)S(1)} %collective-permute-done.1.later, bf16[3,512,512]{2,1,0:T(8,128)(2,1)} %get-tuple-element.17.up, ...), custom_call_target="tpu_custom_call" | custom-call | flops 161061273600 | bytes 10485760 | tf_op jit(solution)/shard_map/later_spectra/pallas_call | solution.py:229
  67.7 0.0 all-to-all-done.first
  67.7 40.4 %all_to_all.15 = bf16[16,3,16,1024]{3,2,1,0:T(8,128)(2,1)S(1)} all-to-all(bf16[16,3,16,1024]{3,2,1,0:T(8,128)(2,1)} %get-tuple-element.22), channel_id=1, replica_groups=mesh['band'=2,'tm'=16] {'tm'}, dimensions={0} | all-to-all | bytes 3145728 | tf_op jit(solution)/shard_map/all_to_all | solution.py:372
  108.1 0.0 copy-start
  108.1 5.2 %all-to-all-start.1 = ((bf16[16,3,16,1024]{3,2,1,0:T(8,128)(2,1)}), bf16[16,3,16,1024]{3,2,1,0:T(8,128)(2,1)S(1)}, u32[]{:S(2)}, u32[]{:S(2)}) async-start(bf16[16,3,16,1024]{3,2,1,0:T(8,128)(2,1)} %get-tuple-element.21), calls=%async_computation.1 | async-start | bytes 3145728 | tf_op jit(solution)/shard_map/all_to_all | solution.py:372
  113.3 0.0 copy-done
  113.3 9.6 %correlate.2.refs_0_ = f32[16,2,16,128,128]{4,3,2,1,0:T(8,128)} custom-call(s32[2,16]{1,0:T(2,128)S(1)} %copy-done, bf16[16,2,16,1024]{3,2,1,0:T(8,128)(2,1)} %all-to-all-done.first, bf16[768,1024]{1,0:T(8,128)(2,1)S(1)} %bitcast.6, bf16[512,256]{1,0:T(8,128)(2,1)} %constant.8.clone.orders), custom_call_target="tpu_custom_call" | custom-call | flops 1073741824 | bytes 18874368 | tf_op jit(solution)/shard_map/correlate/pallas_call | solution.py:324
  122.9 26.6 %all-to-all-done.1 = bf16[16,3,16,1024]{3,2,1,0:T(8,128)(2,1)S(1)} async-done(((bf16[16,3,16,1024]{3,2,1,0:T(8,128)(2,1)}), bf16[16,3,16,1024]{3,2,1,0:T(8,128)(2,1)S(1)}, u32[]{:S(2)}, u32[]{:S(2)}) %all-to-all-start.1) | async-done | bytes 1572896 | tf_op jit(solution)/shard_map/all_to_all | solution.py:372
  149.5 9.6 %correlate.3 = f32[16,2,16,128,128]{4,3,2,1,0:T(8,128)} custom-call(s32[2,16]{1,0:T(2,128)S(1)} %copy-done, bf16[16,2,16,1024]{3,2,1,0:T(8,128)(2,1)} %all-to-all-done.first, bf16[768,1024]{1,0:T(8,128)(2,1)S(1)} %bitcast.5, bf16[512,256]{1,0:T(8,128)(2,1)} %constant.8.clone.orders, ...), custom_call_target="tpu_custom_call", output_to_operand_aliasing={{}: (4, {})} | custom-call | flops 1073741824 | bytes 18874368 | tf_op jit(solution)/shard_map/correlate/pallas_call | solution.py:324
Async XLA Ops:
  9.5 21.6 %collective-permute-start = (bf16[3,512,512]{2,1,0:T(8,128)(2,1)}, bf16[3,512,512]{2,1,0:T(8,128)(2,1)S(1)}, u32[]{:S(2)}, u32[]{:S(2)}) collective-permute-start(bf16[3,512,512]{2,1,0:T(8,128)(2,1)} %get-tuple-element.17.up), channel_id=1, source_target_pairs={{0,1},{1,2},{2,3},{3,4},{4,5},{5,6},{6,7},{7,8},{8,9},{9,10},{10,1... | collective-permute-start | bytes 4718600 | tf_op jit(solution)/shard_map/ppermute | solution.py:29
  22.7 37.9 %collective-permute-start.1 = (bf16[3,512,512]{2,1,0:T(8,128)(2,1)}, bf16[3,512,512]{2,1,0:T(8,128)(2,1)S(1)}, u32[]{:S(2)}, u32[]{:S(2)}) collective-permute-start(bf16[3,512,512]{2,1,0:T(8,128)(2,1)} %get-tuple-element.18.down), channel_id=1, source_target_pairs={{0,15},{1,0},{2,1},{3,2},{4,3},{5,4},{6,5},{7,6},{8,7},{9,8},{10,9... | collective-permute-start | bytes 4718600 | tf_op jit(solution)/shard_map/ppermute | solution.py:29
  22.8 44.9 %all-to-all-start = ((bf16[16,2,16,1024]{3,2,1,0:T(8,128)(2,1)}), bf16[16,2,16,1024]{3,2,1,0:T(8,128)(2,1)}, u32[]{:S(2)}, u32[]{:S(2)}) async-start(bf16[16,2,16,1024]{3,2,1,0:T(8,128)(2,1)} %get-tuple-element.16), calls=%async_computation | async-start | bytes 2097152 | tf_op jit(solution)/shard_map/all_to_all | solution.py:370
  108.1 5.2 %copy-start = (s32[2,16]{1,0:T(2,128)S(1)}, s32[2,16]{1,0:T(2,128)}, u32[]{:S(2)}) copy-start(s32[2,16]{1,0:T(2,128)} %get-tuple-element.14.blocks) | copy-start | bytes 388
  108.1 41.4 %all-to-all-start.1 = ((bf16[16,3,16,1024]{3,2,1,0:T(8,128)(2,1)}), bf16[16,3,16,1024]{3,2,1,0:T(8,128)(2,1)S(1)}, u32[]{:S(2)}, u32[]{:S(2)}) async-start(bf16[16,3,16,1024]{3,2,1,0:T(8,128)(2,1)} %get-tuple-element.21), calls=%async_computation.1 | async-start | bytes 3145728 | tf_op jit(solution)/shard_map/all_to_all | solution.py:372

commit v4 on v3

v4 whole, which is shorter than its diff:
```python
import functools

import jax
import jax.numpy as jnp
import numpy as np
from jax import lax
from jax.experimental import pallas as pl
from jax.experimental.pallas import tpu as pltpu
from jax.sharding import PartitionSpec as P

CHANNELS = 256
TAPS = 4
PANEL = 128
USED = 8
FRAME = 2 * CHANNELS
WIDTH = USED * PANEL
ROWS = 16
PLANE = 4
LANES = 256
VMEM = 60 << 20


def pin(*arrays):
    return [pltpu.with_memory_space_constraint(array, pltpu.HBM) for array in arrays]


def shifted(block, axis, distance, around):
    count = lax.axis_size(axis)
    route = [(i, (i + distance) % count) for i in range(count) if around or 0 <= i + distance < count]
    return lax.ppermute(block, axis, route)


def filter_taps():
    length = TAPS * FRAME
    place = np.arange(length, dtype=np.float64)
    middle = (length - 1) / 2.0
    window = 0.5 - 0.5 * np.cos(2.0 * np.pi * (place + 0.5) / length)
    shape_h = np.sinc((place - middle) / FRAME) * window
    shape_h = shape_h / np.sqrt(np.sum(shape_h * shape_h))
    taps = shape_h.reshape(TAPS, FRAME, 1).astype(np.float32)
    return np.broadcast_to(taps, (TAPS, FRAME, PANEL)).copy()


def dft_table(groups, parts):
    own = CHANNELS // groups
    per = own // parts
    q, g, f, c = np.meshgrid(
        np.arange(parts), np.arange(groups), np.arange(per), np.arange(2), indexing="ij"
    )
    channel = (g * own + q * per + f).reshape(-1)
    imaginary = c.reshape(-1)
    phase = (channel[:, None] * np.arange(FRAME)[None, :] % FRAME) * (2.0 * np.pi / FRAME)
    table = np.where(imaginary[:, None] == 1, -np.sin(phase), np.cos(phase))
    return table.astype(np.float32).astype(jnp.bfloat16)


def row_orders():
    pairs = 256 // ROWS
    half = ROWS // 2
    table = np.zeros((512, 256), np.float32)
    for j in range(pairs):
        for f in range(half):
            row, col = f * pairs * 2 + j * 2, j * ROWS + f * 2
            table[row, col] = 1.0
            table[row + 1, col + 1] = 1.0
            table[256 + row, col + 1] = -1.0
            table[256 + row + 1, col] = 1.0
    return table.astype(jnp.bfloat16)


def named_panels(blocks):
    bits = jnp.int32(0)
    for b in range(blocks.shape[1]):
        bits = bits | (jnp.int32(1) << blocks[0, b])
    return bits


def filtered_frame(taps_ref, frames, cols):
    total = None
    taps = [jnp.tile(taps_ref[t], (1, cols // PANEL)) for t in range(TAPS)]
    for t in range(TAPS):
        term = taps[t] * frames[t].astype(jnp.float32)
        total = term if total is None else total + term
    return total.astype(jnp.bfloat16)


def select_kernel(side, blocks, frames, inputs, *refs):
    halo, hot_out, places, volts, names, hot, chosen, panels, come, go = refs
    depth = TAPS - 1
    order = [(t + 1 - side) % TAPS for t in range(depth)]
    listed = pltpu.make_async_copy(inputs, names, come.at[depth])
    listed.start()
    arrive = [pltpu.make_async_copy(frames.at[t], volts.at[k], come.at[k]) for k, t in enumerate(order)]
    for copy in arrive:
        copy.start()
    bits = named_panels(blocks)
    slot = jnp.int32(0)
    slots = TAPS * USED
    for p in range(inputs.shape[0]):
        panels[slot] = p
        panels[slots + p] = slot * PANEL
        slot = slot + ((bits >> p) & 1)
    listed.wait()
    for j in range(USED // 2):
        wanted = names[pl.ds(panels[side * USED // 2 + j], 1), :]
        rows = lax.broadcasted_iota(jnp.int32, (volts.shape[2], PANEL), 0)
        hot[:, j * PANEL : (j + 1) * PANEL] = (
            (rows == wanted).astype(jnp.float32).astype(jnp.bfloat16)
        )
    sends = []

    def send(source, target):
        sends.append(pltpu.make_async_copy(source, target, go.at[len(sends)]))
        sends[-1].start()

    send(hot, hot_out)
    for k in range(depth):
        arrive[k].wait()
        chosen[k] = jnp.dot(volts[k], hot[...], preferred_element_type=jnp.float32).astype(
            jnp.bfloat16
        )
        send(chosen.at[k], halo.at[k])
    for i in range(2):
        for b in range(blocks.shape[1]):
            places[i, b] = panels[slots + blocks[i, b]]
    for copy in sends:
        copy.wait()


def select(side, block_list, panel_map, frames):
    count, frame, width = frames.shape
    depth = TAPS - 1
    half = WIDTH // 2
    anywhere = pl.BlockSpec(memory_space=pl.ANY)
    return pl.pallas_call(
        functools.partial(select_kernel, side),
        grid_spec=pltpu.PrefetchScalarGridSpec(
            num_scalar_prefetch=1,
            grid=(1,),
            in_specs=[anywhere] * 2,
            out_specs=[anywhere] * 2 + [pl.BlockSpec(memory_space=pltpu.SMEM)],
            scratch_shapes=[
                pltpu.VMEM((depth, frame, width), jnp.bfloat16),
                pltpu.VMEM((width // PANEL, PANEL), jnp.int32),
                pltpu.VMEM((width, half), jnp.bfloat16),
                pltpu.VMEM((depth, frame, half), jnp.bfloat16),
                pltpu.SMEM((TAPS * USED + width // PANEL,), jnp.int32),
                pltpu.SemaphoreType.DMA((TAPS,)),
                pltpu.SemaphoreType.DMA((TAPS,)),
            ],
        ),
        out_shape=[
            pltpu.HBM((depth, frame, half), jnp.bfloat16),
            pltpu.HBM((width, half), jnp.bfloat16),
            jax.ShapeDtypeStruct(block_list.shape, jnp.int32),
        ],
        compiler_params=pltpu.CompilerParams(vmem_limit_bytes=VMEM),
        cost_estimate=pl.CostEstimate(
            flops=depth * frame * width * WIDTH, bytes_accessed=10 << 20, transcendentals=0
        ),
        name="select",
    )(block_list, *pin(frames, panel_map.reshape(-1, PANEL)))


def first_kernel(count, frames, hot0, hot1, up, down, taps, table, *refs):
    kept_out, planes = refs[:2], refs[2 : 2 + count]
    volts, hots, held, kept, spectra, weights, matrix, come, go = refs[2 + count :]
    groups, parts = spectra.shape[0], spectra.shape[1]
    half = WIDTH // 2
    arrive = []

    def fetch(source, target):
        arrive.append(pltpu.make_async_copy(source, target, come.at[len(arrive)]))
        arrive[-1].start()

    for side, (hot, halo) in enumerate(((hot0, up), (hot1, down))):
        fetch(hot, hots.at[side])
        fetch(frames.at[side * (TAPS - 1)], volts.at[side])
        fetch(halo, held.at[side])
        if side == 0:
            fetch(taps, weights)
            fetch(table, matrix)
    sends = []

    def send(source, target):
        sends.append(pltpu.make_async_copy(source, target, go.at[len(sends)]))
        sends[-1].start()

    for side in range(2):
        for copy in arrive[5 * side : 5 * side + 2]:
            copy.wait()
        kept[side] = jnp.dot(
            volts[side], hots[side], preferred_element_type=jnp.float32
        ).astype(jnp.bfloat16)
        send(kept.at[side], kept_out[side])
        for copy in arrive[5 * side + 2 : 5 * side + 5]:
            copy.wait()
        for k in range(half // LANES):
            cols = slice(k * LANES, (k + 1) * LANES)
            pool = [held[side, t, :, cols] for t in range(TAPS - 1)]
            pool.insert(side * (TAPS - 1), kept[side, :, cols])
            spectrum = jnp.dot(
                matrix[...],
                filtered_frame(weights, pool, LANES),
                preferred_element_type=jnp.float32,
            ).astype(jnp.bfloat16)
            at_cols = slice(side * half + k * LANES, side * half + (k + 1) * LANES)
            for q in range(parts):
                for g in range(groups):
                    at = (q * groups + g) * ROWS
                    spectra[g, q, :, at_cols] = spectrum[at : at + ROWS]
    mine = lax.axis_index("tm") // PLANE
    for r, plane in enumerate(planes):
        send(spectra.at[pl.ds((mine ^ r) * PLANE, PLANE)], plane)
    for copy in sends:
        copy.wait()


def first_spectra(frames, hots, up, down, taps, table, groups, parts):
    count, frame, width = frames.shape
    depth = TAPS - 1
    half = WIDTH // 2
    planes = groups // PLANE
    anywhere = pl.BlockSpec(memory_space=pl.ANY)
    return pl.pallas_call(
        functools.partial(first_kernel, planes),
        in_specs=[anywhere] * 7,
        out_specs=[anywhere] * (2 + planes),
        scratch_shapes=[
            pltpu.VMEM((2, frame, width), jnp.bfloat16),
            pltpu.VMEM((2, width, half), jnp.bfloat16),
            pltpu.VMEM((2, depth, frame, half), jnp.bfloat16),
            pltpu.VMEM((2, frame, half), jnp.bfloat16),
            pltpu.VMEM((groups, parts, ROWS, WIDTH), jnp.bfloat16),
            pltpu.VMEM(taps.shape, jnp.float32),
            pltpu.VMEM(table.shape, jnp.bfloat16),
            pltpu.SemaphoreType.DMA((8,)),
            pltpu.SemaphoreType.DMA((2 + planes,)),
        ],
        out_shape=[pltpu.HBM((frame, half), jnp.bfloat16)] * 2
        + [pltpu.HBM((PLANE, parts, ROWS, WIDTH), jnp.bfloat16)] * planes,
        compiler_params=pltpu.CompilerParams(vmem_limit_bytes=VMEM),
        cost_estimate=pl.CostEstimate(
            flops=2 * frame * (width + frame) * WIDTH, bytes_accessed=16 << 20, transcendentals=0
        ),
        name="first_spectra",
    )(*pin(frames, *hots, up, down, taps, table))


def regroup_kernel(*refs):
    planes = len(refs) - 3 - PLANE
    came, left, (held, come, go) = refs[:planes], refs[planes:-3], refs[-3:]
    mine = lax.axis_index("tm") % PLANE
    arrive = [
        [
            pltpu.make_async_copy(plane.at[mine ^ q], held.at[q, r], come.at[q, r])
            for r, plane in enumerate(came)
        ]
        for q in range(PLANE)
    ]
    leave = [pltpu.make_async_copy(held.at[q], left[q], go.at[q]) for q in range(PLANE)]
    for copies in arrive:
        for copy in copies:
            copy.start()
    for copies, copy in zip(arrive, leave):
        for part in copies:
            part.wait()
        copy.start()
    for copy in leave:
        copy.wait()


def regroup(came):
    planes = len(came)
    shape = (planes, *came[0].shape[1:])
    anywhere = pl.BlockSpec(memory_space=pl.ANY)
    return pl.pallas_call(
        regroup_kernel,
        in_specs=[anywhere] * planes,
        out_specs=[anywhere] * PLANE,
        scratch_shapes=[
            pltpu.VMEM((PLANE, *shape), jnp.bfloat16),
            pltpu.SemaphoreType.DMA((PLANE, planes)),
            pltpu.SemaphoreType.DMA((PLANE,)),
        ],
        out_shape=[pltpu.HBM(shape, jnp.bfloat16)] * PLANE,
        cost_estimate=pl.CostEstimate(flops=0, bytes_accessed=2 << 20, transcendentals=0),
        name="regroup",
    )(*came)


def across_planes(planes):
    count = len(planes) * PLANE
    return [planes[0]] + [
        lax.ppermute(plane, "tm", [(i, i ^ (r * PLANE)) for i in range(count)])
        for r, plane in enumerate(planes)
        if r
    ]


def within_plane(came):
    count = len(came) * PLANE
    left = regroup(came)
    return [left[0]] + [
        lax.ppermute(block, "tm", [(i, i ^ q) for i in range(count)])
        for q, block in enumerate(left)
        if q
    ]


def spectra_kernel(side, halo, own, kept, taps, table, *refs):
    out = refs[-1]
    groups, parts = out.shape[0], out.shape[2]
    depth = TAPS - 1
    halos = [halo[t] for t in range(depth)]
    if side:
        ends = lax.axis_index("tm") == lax.axis_size("tm") - 1
        frames = [own[t] for t in range(1, depth)] + [kept[...]]
        pool = [jnp.where(ends, jnp.zeros_like(frame), frame) for frame in frames] + halos
    else:
        pool = halos + [kept[...]] + [own[t] for t in range(depth - 1)]
    for s in range(depth):
        spectrum = jnp.dot(
            table[...],
            filtered_frame(taps, pool[s : s + TAPS], kept.shape[1]),
            preferred_element_type=jnp.float32,
        ).astype(jnp.bfloat16)
        for q in range(parts):
            for g in range(groups):
                at = (q * groups + g) * ROWS
                out[g, s, q] = spectrum[at : at + ROWS]


def later_spectra(side, halo, own, kept, taps, table, groups, parts, so_far):
    depth = TAPS - 1
    frame, cols = kept.shape
    three = pl.BlockSpec((depth, frame, LANES), lambda k: (0, 0, k))
    tiles = cols // LANES
    more = [] if so_far is None else [so_far]
    return pl.pallas_call(
        functools.partial(spectra_kernel, side),
        grid=(cols // LANES,),
        in_specs=[
            three,
            three,
            pl.BlockSpec((frame, LANES), lambda k: (0, k)),
            pl.BlockSpec((TAPS, frame, PANEL), lambda k: (0, 0, 0)),
            pl.BlockSpec((frame, frame), lambda k: (0, 0)),
        ]
        + [pl.BlockSpec(memory_space=pl.ANY)] * len(more),
        out_specs=pl.BlockSpec(
            (groups, depth, parts, ROWS, LANES), lambda k: (0, 0, 0, 0, side * tiles + k)
        ),
        out_shape=pltpu.HBM((groups, depth, parts, ROWS, WIDTH), jnp.bfloat16),
        input_output_aliases={5: 0} if more else {},
        compiler_params=pltpu.CompilerParams(vmem_limit_bytes=VMEM // 2),
        cost_estimate=pl.CostEstimate(
            flops=200 * depth * frame * frame * cols, bytes_accessed=6 << 20, transcendentals=0
        ),
        name="later_spectra",
    )(halo, *pin(own, kept, taps, table), *more)


def correlate_kernel(scale, blocks, *refs):
    sources, rest, orders = refs[:PLANE], refs[PLANE], refs[PLANE + 1]
    out, plain, turned, across, made, first, go, come = refs[-8:]
    groups, depth, parts = rest.shape[0], rest.shape[1], rest.shape[2]
    half = WIDTH // 2
    per = ROWS // 2
    pairs = 256 // ROWS
    width = 256 // per
    arrive = [
        pltpu.make_async_copy(source, first.at[q], come.at[q]) for q, source in enumerate(sources)
    ]
    for copy in arrive:
        copy.start()
    here = [(q, r) for q in range(PLANE) for r in range(groups // PLANE)]
    there = [(g, t) for g in range(groups) for t in range(depth)]
    lead = len(here) // pairs
    total = lead + len(there) // pairs

    def sending(part, f):
        return pltpu.make_async_copy(
            made.at[part, f], out.at[:, :, part * per + f], go.at[part, f]
        )

    for part in range(parts):
        for n in list(range(lead, total)) + list(range(lead)):
            if n == 0 and part == 0:
                for copy in arrive:
                    copy.wait()
            for k in range(WIDTH // LANES):
                cols = slice(k * LANES, (k + 1) * LANES)
                if n < lead:
                    rows = [
                        first[q, r, part, :, cols] for q, r in here[n * pairs : (n + 1) * pairs]
                    ]
                else:
                    some = there[(n - lead) * pairs : (n - lead + 1) * pairs]
                    behind = int(cols.start >= half)
                    rows = [rest[(g - behind) % groups, t, part, :, cols] for g, t in some]
                moved = jnp.dot(
                    orders[...], jnp.concatenate(rows, axis=0), preferred_element_type=jnp.float32
                ).astype(jnp.bfloat16)
                for f in range(per):
                    at = f * width
                    plain[f, n * width : (n + 1) * width, cols] = moved[at : at + width]
                    turned[f, n * width : (n + 1) * width, cols] = moved[
                        256 + at : 256 + at + width
                    ]

        @pl.loop(0, per)
        def _(f):
            across[...] = plain[f].T
            for b in range(blocks.shape[1]):
                a, w = (pl.multiple_of(blocks[i, b], PANEL) for i in range(2))
                product = jnp.dot(
                    across[pl.ds(a, PANEL), :],
                    jnp.concatenate(
                        [plain[f, :, pl.ds(w, PANEL)], turned[f, :, pl.ds(w, PANEL)]], axis=1
                    ),
                    preferred_element_type=jnp.float32,
                )
                made[part, f, b, 0] = product[:, :PANEL] * scale
                made[part, f, b, 1] = product[:, PANEL:] * scale
            sending(part, f).start()

    for part in range(parts):

        @pl.loop(0, per)
        def _(f):
            sending(part, f).wait()


def correlate(places, first, rest, orders, blocks):
    groups, depth, parts = rest.shape[0], rest.shape[1], rest.shape[2]
    per = ROWS // 2
    keys = 2 * groups * TAPS
    shape = (blocks, 2, parts * per, PANEL, PANEL)
    anywhere = pl.BlockSpec(memory_space=pl.ANY)
    inside = pl.BlockSpec(memory_space=pltpu.VMEM)
    return pl.pallas_call(
        functools.partial(correlate_kernel, 1.0 / (groups * TAPS)),
        grid_spec=pltpu.PrefetchScalarGridSpec(
            num_scalar_prefetch=1,
            grid=(1,),
            in_specs=[anywhere] * PLANE
            + [inside, pl.BlockSpec(orders.shape, lambda s, blocks: (0, 0))],
            out_specs=anywhere,
            scratch_shapes=[
                pltpu.VMEM((per, keys, WIDTH), jnp.bfloat16),
                pltpu.VMEM((per, keys, WIDTH), jnp.bfloat16),
                pltpu.VMEM((WIDTH, keys), jnp.bfloat16),
                pltpu.VMEM((parts, per, blocks, 2, PANEL, PANEL), jnp.float32),
                pltpu.VMEM((PLANE, *first[0].shape), jnp.bfloat16),
                pltpu.SemaphoreType.DMA((parts, per)),
                pltpu.SemaphoreType.DMA((PLANE,)),
            ],
        ),
        out_shape=pltpu.HBM(shape, jnp.float32),
        compiler_params=pltpu.CompilerParams(vmem_limit_bytes=VMEM * 5 // 6),
        cost_estimate=pl.CostEstimate(
            flops=4 * parts * per * keys * PANEL * PANEL * blocks,
            bytes_accessed=36 << 20,
            transcendentals=0,
        ),
        name="correlate",
    )(places, *pin(*first), rest, *pin(orders))


def body(voltages, panel_map, block_list):
    groups = lax.axis_size("tm")
    own = CHANNELS // groups
    parts = own * 2 // ROWS
    frames = voltages.reshape(-1, FRAME, voltages.shape[1])
    taps = filter_taps()
    table = dft_table(groups, parts)
    block_list = block_list.T
    up, hot0, places = select(0, block_list, panel_map, frames)
    earlier = shifted(up, "tm", 1, False)
    down, hot1, _ = select(1, block_list, panel_map, frames)
    later = shifted(down, "tm", -1, True)
    left, right, *planes = first_spectra(
        frames, (hot0, hot1), up, down, taps, table, groups, parts
    )
    came = across_planes(planes)
    later_half = functools.partial(
        later_spectra, taps=taps, table=table, groups=groups, parts=parts
    )
    rest = later_half(0, earlier, up, left, so_far=None)
    rest = later_half(1, later, down, right, so_far=rest)
    rest, came = lax.optimization_barrier((rest, came))
    first = within_plane(came)
    rest = lax.all_to_all(rest, "tm", split_axis=0, concat_axis=0, tiled=True)
    return correlate(places, first, rest, row_orders(), block_list.shape[1])


def solution(mesh):
    in_specs = (P(("band", "tm"), None), P(), P())
    out_specs = P("band", None, "tm", None, None)
    return jax.shard_map(body, mesh=mesh, in_specs=in_specs, out_specs=out_specs, check_vma=False)
```

time: 160 us -> 153 us (0.956)
  blocking collectives: 40.4 us -> 0 us
  waiting for transfers between devices: 58 us -> 82.6 us
  starting transfers between devices: 15.4 us -> 20.6 us
  Pallas kernels: 45.2 us -> 48.5 us
    all_to_all x1 -> x0, blocking collectives: 40.4 us -> none  [body(): rest = [exchange(part) for part in rest]]
    ppermute x0 -> x6, waiting for transfers between devices: none -> 24.7 us  [the longest x3 24.7 us: within_plane(): lax.ppermute(block, 'tm', [(i, i ^ q) for i in range(count)])]
    ppermute x2, waiting for transfers between devices: 31.4 us -> 17.8 us  [shifted(): return lax.ppermute(block, axis, route)]
    all_to_all x2 -> x1, waiting for transfers between devices: 26.6 us -> 40.1 us  [body(): rest = lax.all_to_all(rest, 'tm', split_axis=0, concat_axis=0, tiled=True)]
    pallas_call x3 -> x5, Pallas kernels: 26.2 us -> 33.5 us  [the longest x1 15.3 us: correlate(): pl.pallas_call(functools.partial(correlate_kernel, 1.0 / (groups * TAPS))...]
    ppermute x0 -> x6, starting transfers between devices: none -> 4.93 us  [the longest x3 2.71 us: across_planes(): lax.ppermute(plane, 'tm', [(i, i ^ r * PLANE) for i in range(count)])]
    pallas_call x2, Pallas kernels: 19 us -> 15 us  [select(): pl.pallas_call(functools.partial(select_kernel, side), grid_spec=pltpu.Pr...]
    all_to_all x2 -> x1, starting transfers between devices: 11.7 us -> 11.9 us  [body(): rest = lax.all_to_all(rest, 'tm', split_axis=0, concat_axis=0, tiled=True)]
  transfers between devices with their start and end apart: 4 -> 9, of which waited for: 3 -> 4; matrix products, arithmetic and copies ran while one was open for 0% -> 0% of each run, Pallas kernels for 16% -> 17%
where the time goes in v4:
time: 153 us
  waiting for transfers between devices  82.6 us (54%)
  Pallas kernels  48.5 us (32%)
  starting transfers between devices  20.6 us (13%)
    all_to_all x1, waiting for transfers between devices, body(): rest = lax.all_to_all(rest, 'tm', split_axis=0, concat_axis=0, tiled=True)  40.1 us
    ppermute x3, waiting for transfers between devices, within_plane(): lax.ppermute(block, 'tm', [(i, i ^ q) for i in range(count)])  24.7 us
    ppermute x2, waiting for transfers between devices, shifted(): return lax.ppermute(block, axis, route)  17.8 us
    pallas_call x1, Pallas kernels, correlate(): pl.pallas_call(functools.partial(correlate_kernel, 1.0 / (groups * TAPS))...  15.3 us
    pallas_call x2, Pallas kernels, select(): pl.pallas_call(functools.partial(select_kernel, side), grid_spec=pltpu.Pr...  15 us
    all_to_all x1, starting transfers between devices, body(): rest = lax.all_to_all(rest, 'tm', split_axis=0, concat_axis=0, tiled=True)  11.9 us
    pallas_call x2, Pallas kernels, later_spectra(): pl.pallas_call(functools.partial(spectra_kernel, side), grid=(cols // LAN...  8.57 us
    pallas_call x1, Pallas kernels, first_spectra(): pl.pallas_call(functools.partial(first_kernel, planes), in_specs=[anywher...  7.42 us
  transfers between devices with their start and end apart: 9, of which 4 were waited for; matrix products, arithmetic and copies ran while one was open for 0% of the time, Pallas kernels for 17%

profile of v4, /device:TPU:15, one launch (start us, length us, event | category | flops | bytes accessed | tf_op | source)
XLA Modules:
  0.0 152.6 jit_solution(7178762844441099503)
XLA Ops:
  0.0 7.5 %select.2 = (bf16[3,512,512]{2,1,0:T(8,128)(2,1)}, bf16[2048,512]{1,0:T(8,128)(2,1)}, s32[2,16]{1,0:T(2,128)}) custom-call(s32[2,16]{1,0:T(2,128)} %bitcast.8, bf16[4,512,2048]{2,1,0:T(8,128)(2,1)} %bitcast.3, s32[16,128]{1,0:T(8,128)} %bitcast.6), custom_call_target="tpu_custom_call" | custom-call | flops 3221225472 | bytes 10485760 | tf_op jit(solution)/shard_map/select/pallas_call | solution.py:135
  7.5 3.7 %collective-permute-start.1 = (bf16[3,512,512]{2,1,0:T(8,128)(2,1)}, bf16[3,512,512]{2,1,0:T(8,128)(2,1)S(1)}, u32[]{:S(2)}, u32[]{:S(2)}) collective-permute-start(bf16[3,512,512]{2,1,0:T(8,128)(2,1)} %get-tuple-element.29.up.own), channel_id=1, source_target_pairs={{0,1},{1,2},{2,3},{3,4},{4,5},{5,6},{6,7},{7,8},{8,9},{9,10},{10,1... | collective-permute-start | bytes 4718600 | tf_op jit(solution)/shard_map/ppermute | solution.py:30
  11.2 7.5 %select.3 = (bf16[3,512,512]{2,1,0:T(8,128)(2,1)}, bf16[2048,512]{1,0:T(8,128)(2,1)}, s32[2,16]{1,0:T(2,128)}) custom-call(s32[2,16]{1,0:T(2,128)} %bitcast.9, bf16[4,512,2048]{2,1,0:T(8,128)(2,1)} %bitcast.4, s32[16,128]{1,0:T(8,128)} %bitcast.7), custom_call_target="tpu_custom_call" | custom-call | flops 3221225472 | bytes 10485760 | tf_op jit(solution)/shard_map/select/pallas_call | solution.py:135
  18.7 0.1 collective-permute-start
  18.8 7.4 %first_spectra.1 = (bf16[512,512]{1,0:T(8,128)(2,1)}, bf16[512,512]{1,0:T(8,128)(2,1)}, bf16[4,2,16,1024]{3,2,1,0:T(8,128)(2,1)}, bf16[4,2,16,1024]{3,2,1,0:T(8,...) custom-call(bf16[4,512,2048]{2,1,0:T(8,128)(2,1)} %bitcast.5, ...), custom_call_target="tpu_custom_call" | custom-call | flops 2684354560 | bytes 16777216 | tf_op jit(solution)/shard_map/first_spectra/pallas_call | solution.py:225
  26.2 0.2 collective-permute-start.2
  26.4 2.3 %collective-permute-start.3 = (bf16[4,2,16,1024]{3,2,1,0:T(8,128)(2,1)}, bf16[4,2,16,1024]{3,2,1,0:T(8,128)(2,1)}, u32[]{:S(2)}, u32[]{:S(2)}) collective-permute-start(bf16[4,2,16,1024]{3,2,1,0:T(8,128)(2,1)} %get-tuple-element.34), channel_id=1, source_target_pairs={{0,8},{1,9},{2,10},{3,11},{4,12},{5,13},{6,14},{7,15},{8,0},{9,1},... | collective-permute-start | bytes 786440 | tf_op jit(solution)/shard_map/ppermute | solution.py:295
  28.7 0.2 collective-permute-start.4
  28.9 0.0 collective-permute-done.1.halo
  28.9 4.3 %later_spectra.2.refs_0_ = bf16[16,3,2,16,1024]{4,3,2,1,0:T(8,128)(2,1)} custom-call(bf16[3,512,512]{2,1,0:T(8,128)(2,1)S(1)} %collective-permute-done.1.halo, bf16[3,512,512]{2,1,0:T(8,128)(2,1)} %get-tuple-element.29.up.own, bf16[512,512]{1,0:T(8,128)(2,1)} %get-tuple-element.31.kept, f32[4,512,128]{2,1,0:T(8,128)} %constant.6.clone.taps, ...), custom_call_target="tpu_custom_call" | custom-call | flops 80530636800 | bytes 6291456 | tf_op jit(solution)/shard_map/later_spectra/pallas_call | solution.py:340
  33.2 17.8 %collective-permute-done.halo = bf16[3,512,512]{2,1,0:T(8,128)(2,1)S(1)} collective-permute-done((bf16[3,512,512]{2,1,0:T(8,128)(2,1)}, bf16[3,512,512]{2,1,0:T(8,128)(2,1)S(1)}, u32[]{:S(2)}, u32[]{:S(2)}) %collective-permute-start) | collective-permute-done | bytes 1572896 | tf_op jit(solution)/shard_map/ppermute | solution.py:30
  51.0 4.3 %later_spectra.3 = bf16[16,3,2,16,1024]{4,3,2,1,0:T(8,128)(2,1)} custom-call(bf16[3,512,512]{2,1,0:T(8,128)(2,1)S(1)} %collective-permute-done.halo, bf16[3,512,512]{2,1,0:T(8,128)(2,1)} %get-tuple-element.26.down.own, bf16[512,512]{1,0:T(8,128)(2,1)} %get-tuple-element.30.kept, f32[4,512,128]{2,1,0:T(8,128)} %constant.6.clone.taps, ...), custom_call_target="tpu_custom_call", output_to_operand_aliasing={{}: (5, {})} | custom-call | flops 80530636800 | bytes 6291456 | tf_op jit(solution)/shard_map/later_spectra/pallas_call | solution.py:340
  55.3 0.0 collective-permute-done.2.refs_1_
  55.3 0.0 collective-permute-done.3.refs_2_
  55.3 0.0 collective-permute-done.4.refs_3_
  55.3 0.0 copy-start
  55.3 11.9 %all-to-all-start = ((bf16[16,3,2,16,1024]{4,3,2,1,0:T(8,128)(2,1)}), bf16[16,3,2,16,1024]{4,3,2,1,0:T(8,128)(2,1)S(1)}, u32[]{:S(2)}, u32[]{:S(2)}) async-start(bf16[16,3,2,16,1024]{4,3,2,1,0:T(8,128)(2,1)} %later_spectra.3), calls=%async_computation | async-start | bytes 6291456 | tf_op jit(solution)/shard_map/all_to_all | solution.py:494
  67.2 2.2 %regroup.1 = (bf16[4,2,16,1024]{3,2,1,0:T(8,128)(2,1)}, bf16[4,2,16,1024]{3,2,1,0:T(8,128)(2,1)}, bf16[4,2,16,1024]{3,2,1,0:T(8,128)(2,1)}, bf16[4,2,16,1024]{3,2,1,0:T(8,128)(2,1)}) custom-call(bf16[4,2,16,1024]{3,2,1,0:T(8,128)(2,1)} %get-tuple-element.36.refs_0_, bf16[4,2,16,1024]{3,2,1,0:T(8,128)(2,1)} %collective-permute-done.2.refs_1_, ...), custom_call_target="tpu_custom_call" | custom-call | bytes 2097152 | tf_op jit(solution)/shard_map/regroup/pallas_call | solution.py:277
  69.4 0.4 collective-permute-start.5
  69.8 0.3 collective-permute-start.6
  70.1 1.5 collective-permute-start.7
  71.6 0.0 collective-permute-done.5.refs_1_
  71.6 0.0 copy-start.1
  71.6 19.3 %collective-permute-done.6.refs_2_ = bf16[4,2,16,1024]{3,2,1,0:T(8,128)(2,1)S(1)} collective-permute-done((bf16[4,2,16,1024]{3,2,1,0:T(8,128)(2,1)}, bf16[4,2,16,1024]{3,2,1,0:T(8,128)(2,1)S(1)}, u32[]{:S(2)}, u32[]{:S(2)}) %collective-permute-start.6) | collective-permute-done | bytes 262176 | tf_op jit(solution)/shard_map/ppermute | solution.py:305
  90.9 0.0 copy-start.2
  90.9 0.7 copy-done.2
  91.6 5.4 %collective-permute-done.7.refs_3_ = bf16[4,2,16,1024]{3,2,1,0:T(8,128)(2,1)} collective-permute-done((bf16[4,2,16,1024]{3,2,1,0:T(8,128)(2,1)}, bf16[4,2,16,1024]{3,2,1,0:T(8,128)(2,1)}, u32[]{:S(2)}, u32[]{:S(2)}) %collective-permute-start.7) | collective-permute-done | bytes 262176 | tf_op jit(solution)/shard_map/ppermute | solution.py:305
  97.0 40.1 %all-to-all-done.refs_4_ = bf16[16,3,2,16,1024]{4,3,2,1,0:T(8,128)(2,1)S(1)} async-done(((bf16[16,3,2,16,1024]{4,3,2,1,0:T(8,128)(2,1)}), bf16[16,3,2,16,1024]{4,3,2,1,0:T(8,128)(2,1)S(1)}, u32[]{:S(2)}, u32[]{:S(2)}) %all-to-all-start) | async-done | bytes 3145760 | tf_op jit(solution)/shard_map/all_to_all | solution.py:494
  137.2 0.0 copy-done.1
  137.2 0.0 copy-done
  137.2 15.3 %correlate.1 = f32[16,2,16,128,128]{4,3,2,1,0:T(8,128)} custom-call(s32[2,16]{1,0:T(2,128)S(1)} %copy-done, bf16[4,2,16,1024]{3,2,1,0:T(8,128)(2,1)} %get-tuple-element.40.refs_0_, bf16[4,2,16,1024]{3,2,1,0:T(8,128)(2,1)} %copy-done.1, bf16[4,2,16,1024]{3,2,1,0:T(8,128)(2,1)} %copy-done.2, bf16[4,2,16,1024]{3,2,1,0:T(8,128)(2,1)} %collective-permute-done.7.refs_3_, ...), custom_call_target="tpu_custom_call" | custom-call | flops 2147483648 | bytes 37748736 | tf_op jit(solution)/shard_map/correlate/pallas_call | solution.py:442
Async XLA Ops:
  7.5 21.4 %collective-permute-start.1 = (bf16[3,512,512]{2,1,0:T(8,128)(2,1)}, bf16[3,512,512]{2,1,0:T(8,128)(2,1)S(1)}, u32[]{:S(2)}, u32[]{:S(2)}) collective-permute-start(bf16[3,512,512]{2,1,0:T(8,128)(2,1)} %get-tuple-element.29.up.own), channel_id=1, source_target_pairs={{0,1},{1,2},{2,3},{3,4},{4,5},{5,6},{6,7},{7,8},{8,9},{9,10},{10,1... | collective-permute-start | bytes 4718600 | tf_op jit(solution)/shard_map/ppermute | solution.py:30
  18.7 32.3 %collective-permute-start = (bf16[3,512,512]{2,1,0:T(8,128)(2,1)}, bf16[3,512,512]{2,1,0:T(8,128)(2,1)S(1)}, u32[]{:S(2)}, u32[]{:S(2)}) collective-permute-start(bf16[3,512,512]{2,1,0:T(8,128)(2,1)} %get-tuple-element.26.down.own), channel_id=1, source_target_pairs={{0,15},{1,0},{2,1},{3,2},{4,3},{5,4},{6,5},{7,6},{8,7},{9,8},{10,9... | collective-permute-start | bytes 4718600 | tf_op jit(solution)/shard_map/ppermute | solution.py:30
  26.2 29.1 %collective-permute-start.2 = (bf16[4,2,16,1024]{3,2,1,0:T(8,128)(2,1)}, bf16[4,2,16,1024]{3,2,1,0:T(8,128)(2,1)}, u32[]{:S(2)}, u32[]{:S(2)}) collective-permute-start(bf16[4,2,16,1024]{3,2,1,0:T(8,128)(2,1)} %get-tuple-element.33), channel_id=1, source_target_pairs={{0,4},{1,5},{2,6},{3,7},{4,0},{5,1},{6,2},{7,3},{8,12},{9,13},{10,... | collective-permute-start | bytes 786440 | tf_op jit(solution)/shard_map/ppermute | solution.py:295
  26.4 28.9 %collective-permute-start.3 = (bf16[4,2,16,1024]{3,2,1,0:T(8,128)(2,1)}, bf16[4,2,16,1024]{3,2,1,0:T(8,128)(2,1)}, u32[]{:S(2)}, u32[]{:S(2)}) collective-permute-start(bf16[4,2,16,1024]{3,2,1,0:T(8,128)(2,1)} %get-tuple-element.34), channel_id=1, source_target_pairs={{0,8},{1,9},{2,10},{3,11},{4,12},{5,13},{6,14},{7,15},{8,0},{9,1},... | collective-permute-start | bytes 786440 | tf_op jit(solution)/shard_map/ppermute | solution.py:295
  28.7 26.6 %collective-permute-start.4 = (bf16[4,2,16,1024]{3,2,1,0:T(8,128)(2,1)}, bf16[4,2,16,1024]{3,2,1,0:T(8,128)(2,1)}, u32[]{:S(2)}, u32[]{:S(2)}) collective-permute-start(bf16[4,2,16,1024]{3,2,1,0:T(8,128)(2,1)} %get-tuple-element.35), channel_id=1, source_target_pairs={{0,12},{1,13},{2,14},{3,15},{4,8},{5,9},{6,10},{7,11},{8,4},{9,5},... | collective-permute-start | bytes 786440 | tf_op jit(solution)/shard_map/ppermute | solution.py:295
  55.3 81.9 %copy-start = (s32[2,16]{1,0:T(2,128)S(1)}, s32[2,16]{1,0:T(2,128)}, u32[]{:S(2)}) copy-start(s32[2,16]{1,0:T(2,128)} %get-tuple-element.25.blocks) | copy-start | bytes 388
  55.3 81.9 %all-to-all-start = ((bf16[16,3,2,16,1024]{4,3,2,1,0:T(8,128)(2,1)}), bf16[16,3,2,16,1024]{4,3,2,1,0:T(8,128)(2,1)S(1)}, u32[]{:S(2)}, u32[]{:S(2)}) async-start(bf16[16,3,2,16,1024]{4,3,2,1,0:T(8,128)(2,1)} %later_spectra.3), calls=%async_computation | async-start | bytes 6291456 | tf_op jit(solution)/shard_map/all_to_all | solution.py:494
  69.4 2.2 %collective-permute-start.5 = (bf16[4,2,16,1024]{3,2,1,0:T(8,128)(2,1)}, bf16[4,2,16,1024]{3,2,1,0:T(8,128)(2,1)S(1)}, u32[]{:S(2)}, u32[]{:S(2)}) collective-permute-start(bf16[4,2,16,1024]{3,2,1,0:T(8,128)(2,1)} %get-tuple-element.41), channel_id=1, source_target_pairs={{0,1},{1,0},{2,3},{3,2},{4,5},{5,4},{6,7},{7,6},{8,9},{9,8},{10,11... | collective-permute-start | bytes 786440 | tf_op jit(solution)/shard_map/ppermute | solution.py:305
  69.8 21.1 %collective-permute-start.6 = (bf16[4,2,16,1024]{3,2,1,0:T(8,128)(2,1)}, bf16[4,2,16,1024]{3,2,1,0:T(8,128)(2,1)S(1)}, u32[]{:S(2)}, u32[]{:S(2)}) collective-permute-start(bf16[4,2,16,1024]{3,2,1,0:T(8,128)(2,1)} %get-tuple-element.42), channel_id=1, source_target_pairs={{0,2},{1,3},{2,0},{3,1},{4,6},{5,7},{6,4},{7,5},{8,10},{9,11},{10,... | collective-permute-start | bytes 786440 | tf_op jit(solution)/shard_map/ppermute | solution.py:305
  70.1 26.9 %collective-permute-start.7 = (bf16[4,2,16,1024]{3,2,1,0:T(8,128)(2,1)}, bf16[4,2,16,1024]{3,2,1,0:T(8,128)(2,1)}, u32[]{:S(2)}, u32[]{:S(2)}) collective-permute-start(bf16[4,2,16,1024]{3,2,1,0:T(8,128)(2,1)} %get-tuple-element.43), channel_id=1, source_target_pairs={{0,3},{1,2},{2,1},{3,0},{4,7},{5,6},{6,5},{7,4},{8,11},{9,10},{10,... | collective-permute-start | bytes 786440 | tf_op jit(solution)/shard_map/ppermute | solution.py:305
  71.6 65.5 %copy-start.1 = (bf16[4,2,16,1024]{3,2,1,0:T(8,128)(2,1)}, bf16[4,2,16,1024]{3,2,1,0:T(8,128)(2,1)S(1)}, u32[]{:S(2)}) copy-start(bf16[4,2,16,1024]{3,2,1,0:T(8,128)(2,1)S(1)} %collective-permute-done.5.refs_1_) | copy-start | bytes 786436
  90.9 0.7 copy-start.2

commit v5 on v4

--- a/solution.py
+++ b/solution.py
@@ -84,121 +84,119 @@
     return total.astype(jnp.bfloat16)
 
 
-def select_kernel(side, blocks, frames, inputs, *refs):
-    halo, hot_out, places, volts, names, hot, chosen, panels, come, go = refs
-    depth = TAPS - 1
-    order = [(t + 1 - side) % TAPS for t in range(depth)]
-    listed = pltpu.make_async_copy(inputs, names, come.at[depth])
-    listed.start()
-    arrive = [pltpu.make_async_copy(frames.at[t], volts.at[k], come.at[k]) for k, t in enumerate(order)]
-    for copy in arrive:
-        copy.start()
+def choose(side, blocks, names, hot, panels):
     bits = named_panels(blocks)
     slot = jnp.int32(0)
     slots = TAPS * USED
-    for p in range(inputs.shape[0]):
+    for p in range(names.shape[0]):
         panels[slot] = p
         panels[slots + p] = slot * PANEL
         slot = slot + ((bits >> p) & 1)
-    listed.wait()
     for j in range(USED // 2):
         wanted = names[pl.ds(panels[side * USED // 2 + j], 1), :]
-        rows = lax.broadcasted_iota(jnp.int32, (volts.shape[2], PANEL), 0)
+        rows = lax.broadcasted_iota(jnp.int32, (hot.shape[0], PANEL), 0)
         hot[:, j * PANEL : (j + 1) * PANEL] = (
             (rows == wanted).astype(jnp.float32).astype(jnp.bfloat16)
         )
-    sends = []
-
-    def send(source, target):
-        sends.append(pltpu.make_async_copy(source, target, go.at[len(sends)]))
-        sends[-1].start()
-
-    send(hot, hot_out)
-    for k in range(depth):
+
+
+def left_kernel(blocks, frames, inputs, halo, hot, volts, places, names, panels, come):
+    listed = pltpu.make_async_copy(inputs, names, come.at[TAPS])
+    listed.start()
+    order = list(range(1, TAPS)) + [0]
+    arrive = [pltpu.make_async_copy(frames.at[t], volts.at[t], come.at[t]) for t in order]
+    for copy in arrive[:-1]:
+        copy.start()
+    listed.wait()
+    choose(0, blocks, names, hot, panels)
+    for k in range(TAPS - 1):
         arrive[k].wait()
-        chosen[k] = jnp.dot(volts[k], hot[...], preferred_element_type=jnp.float32).astype(
+        if k == 0:
+            arrive[-1].start()
+        halo[k] = jnp.dot(volts[k + 1], hot[...], preferred_element_type=jnp.float32).astype(
             jnp.bfloat16
         )
-        send(chosen.at[k], halo.at[k])
     for i in range(2):
         for b in range(blocks.shape[1]):
-            places[i, b] = panels[slots + blocks[i, b]]
-    for copy in sends:
-        copy.wait()
+            places[i, b] = panels[TAPS * USED + blocks[i, b]]
+    arrive[TAPS - 1].wait()
+
+
+def right_kernel(blocks, volts, inputs, halo, hot, names, panels, come):
+    listed = pltpu.make_async_copy(inputs, names, come.at[TAPS])
+    listed.start()
+    listed.wait()
+    choose(1, blocks, names, hot, panels)
+    for k in range(TAPS - 1):
+        halo[k] = jnp.dot(volts[k], hot[...], preferred_element_type=jnp.float32).astype(
+            jnp.bfloat16
+        )
+
+
+ANYWHERE = pl.BlockSpec(memory_space=pl.ANY)
+INSIDE = pl.BlockSpec(memory_space=pltpu.VMEM)
 
 
 def select(side, block_list, panel_map, frames):
     count, frame, width = frames.shape
     depth = TAPS - 1
     half = WIDTH // 2
-    anywhere = pl.BlockSpec(memory_space=pl.ANY)
+    out_specs = [INSIDE, INSIDE]
+    out_shape = [
+        pltpu.VMEM((depth, frame, half), jnp.bfloat16),
+        pltpu.VMEM((width, half), jnp.bfloat16),
+    ]
+    if side == 0:
+        out_specs += [INSIDE, pl.BlockSpec(memory_space=pltpu.SMEM)]
+        out_shape += [
+            pltpu.VMEM(frames.shape, jnp.bfloat16),
+            jax.ShapeDtypeStruct(block_list.shape, jnp.int32),
+        ]
     return pl.pallas_call(
-        functools.partial(select_kernel, side),
+        right_kernel if side else left_kernel,
         grid_spec=pltpu.PrefetchScalarGridSpec(
             num_scalar_prefetch=1,
             grid=(1,),
-            in_specs=[anywhere] * 2,
-            out_specs=[anywhere] * 2 + [pl.BlockSpec(memory_space=pltpu.SMEM)],
+            in_specs=[INSIDE if side else ANYWHERE, ANYWHERE],
+            out_specs=out_specs,
             scratch_shapes=[
-                pltpu.VMEM((depth, frame, width), jnp.bfloat16),
                 pltpu.VMEM((width // PANEL, PANEL), jnp.int32),
-                pltpu.VMEM((width, half), jnp.bfloat16),
-                pltpu.VMEM((depth, frame, half), jnp.bfloat16),
                 pltpu.SMEM((TAPS * USED + width // PANEL,), jnp.int32),
-                pltpu.SemaphoreType.DMA((TAPS,)),
-                pltpu.SemaphoreType.DMA((TAPS,)),
+                pltpu.SemaphoreType.DMA((1 + TAPS,)),
             ],
         ),
-        out_shape=[
-            pltpu.HBM((depth, frame, half), jnp.bfloat16),
-            pltpu.HBM((width, half), jnp.bfloat16),
-            jax.ShapeDtypeStruct(block_list.shape, jnp.int32),
-        ],
-        compiler_params=pltpu.CompilerParams(vmem_limit_bytes=VMEM),
+        out_shape=out_shape,
+        compiler_params=pltpu.CompilerParams(vmem_limit_bytes=VMEM // 2),
         cost_estimate=pl.CostEstimate(
             flops=depth * frame * width * WIDTH, bytes_accessed=10 << 20, transcendentals=0
         ),
         name="select",
-    )(block_list, *pin(frames, panel_map.reshape(-1, PANEL)))
-
-
-def first_kernel(count, frames, hot0, hot1, up, down, taps, table, *refs):
-    kept_out, planes = refs[:2], refs[2 : 2 + count]
-    volts, hots, held, kept, spectra, weights, matrix, come, go = refs[2 + count :]
+    )(block_list, *([frames] if side else pin(frames)), *pin(panel_map.reshape(-1, PANEL)))
+
+
+def first_kernel(count, volts, hot0, hot1, up, down, taps, table, orders, *refs):
+    kept, held, planes = refs[:2], refs[2:5], refs[5 : 5 + count]
+    spectra, come, go = refs[5 + count :]
+    weights, matrix, _ = held
     groups, parts = spectra.shape[0], spectra.shape[1]
     half = WIDTH // 2
-    arrive = []
-
-    def fetch(source, target):
-        arrive.append(pltpu.make_async_copy(source, target, come.at[len(arrive)]))
-        arrive[-1].start()
-
+    arrive = [
+        pltpu.make_async_copy(source, target, come.at[i])
+        for i, (source, target) in enumerate(zip((taps, table, orders), held))
+    ]
+    for copy in arrive:
+        copy.start()
     for side, (hot, halo) in enumerate(((hot0, up), (hot1, down))):
-        fetch(hot, hots.at[side])
-        fetch(frames.at[side * (TAPS - 1)], volts.at[side])
-        fetch(halo, held.at[side])
+        kept[side][...] = jnp.dot(
+            volts[side * (TAPS - 1)], hot[...], preferred_element_type=jnp.float32
+        ).astype(jnp.bfloat16)
         if side == 0:
-            fetch(taps, weights)
-            fetch(table, matrix)
-    sends = []
-
-    def send(source, target):
-        sends.append(pltpu.make_async_copy(source, target, go.at[len(sends)]))
-        sends[-1].start()
-
-    for side in range(2):
-        for copy in arrive[5 * side : 5 * side + 2]:
-            copy.wait()
-        kept[side] = jnp.dot(
-            volts[side], hots[side], preferred_element_type=jnp.float32
-        ).astype(jnp.bfloat16)
-        send(kept.at[side], kept_out[side])
-        for copy in arrive[5 * side + 2 : 5 * side + 5]:
-            copy.wait()
+            for copy in arrive:
+                copy.wait()
         for k in range(half // LANES):
             cols = slice(k * LANES, (k + 1) * LANES)
-            pool = [held[side, t, :, cols] for t in range(TAPS - 1)]
-            pool.insert(side * (TAPS - 1), kept[side, :, cols])
+            pool = [halo[t, :, cols] for t in range(TAPS - 1)]
+            pool.insert(side * (TAPS - 1), kept[side][:, cols])
             spectrum = jnp.dot(
                 matrix[...],
                 filtered_frame(weights, pool, LANES),
@@ -210,41 +208,38 @@
                     at = (q * groups + g) * ROWS
                     spectra[g, q, :, at_cols] = spectrum[at : at + ROWS]
     mine = lax.axis_index("tm") // PLANE
-    for r, plane in enumerate(planes):
-        send(spectra.at[pl.ds((mine ^ r) * PLANE, PLANE)], plane)
+    sends = [
+        pltpu.make_async_copy(spectra.at[pl.ds((mine ^ r) * PLANE, PLANE)], plane, go.at[r])
+        for r, plane in enumerate(planes)
+    ]
+    for copy in sends:
+        copy.start()
     for copy in sends:
         copy.wait()
 
 
-def first_spectra(frames, hots, up, down, taps, table, groups, parts):
-    count, frame, width = frames.shape
-    depth = TAPS - 1
+def first_spectra(volts, hots, up, down, taps, table, orders, groups, parts):
+    count, frame, width = volts.shape
     half = WIDTH // 2
     planes = groups // PLANE
-    anywhere = pl.BlockSpec(memory_space=pl.ANY)
     return pl.pallas_call(
         functools.partial(first_kernel, planes),
-        in_specs=[anywhere] * 7,
-        out_specs=[anywhere] * (2 + planes),
+        in_specs=[INSIDE] * 5 + [ANYWHERE] * 3,
+        out_specs=[INSIDE] * 5 + [ANYWHERE] * planes,
         scratch_shapes=[
-            pltpu.VMEM((2, frame, width), jnp.bfloat16),
-            pltpu.VMEM((2, width, half), jnp.bfloat16),
-            pltpu.VMEM((2, depth, frame, half), jnp.bfloat16),
-            pltpu.VMEM((2, frame, half), jnp.bfloat16),
             pltpu.VMEM((groups, parts, ROWS, WIDTH), jnp.bfloat16),
-            pltpu.VMEM(taps.shape, jnp.float32),
-            pltpu.VMEM(table.shape, jnp.bfloat16),
-            pltpu.SemaphoreType.DMA((8,)),
-            pltpu.SemaphoreType.DMA((2 + planes,)),
+            pltpu.SemaphoreType.DMA((3,)),
+            pltpu.SemaphoreType.DMA((planes,)),
         ],
-        out_shape=[pltpu.HBM((frame, half), jnp.bfloat16)] * 2
+        out_shape=[pltpu.VMEM((frame, half), jnp.bfloat16)] * 2
+        + [pltpu.VMEM(held.shape, held.dtype) for held in (taps, table, orders)]
         + [pltpu.HBM((PLANE, parts, ROWS, WIDTH), jnp.bfloat16)] * planes,
-        compiler_params=pltpu.CompilerParams(vmem_limit_bytes=VMEM),
+        compiler_params=pltpu.CompilerParams(vmem_limit_bytes=VMEM // 2),
         cost_estimate=pl.CostEstimate(
             flops=2 * frame * (width + frame) * WIDTH, bytes_accessed=16 << 20, transcendentals=0
         ),
         name="first_spectra",
-    )(*pin(frames, *hots, up, down, taps, table))
+    )(volts, *hots, up, down, *pin(taps, table, orders))
 
 
 def regroup_kernel(*refs):
@@ -284,7 +279,8 @@
             pltpu.SemaphoreType.DMA((PLANE,)),
         ],
         out_shape=[pltpu.HBM(shape, jnp.bfloat16)] * PLANE,
-        cost_estimate=pl.CostEstimate(flops=0, bytes_accessed=2 << 20, transcendentals=0),
+        compiler_params=pltpu.CompilerParams(vmem_limit_bytes=VMEM // 12),
+        cost_estimate=pl.CostEstimate(flops=1 << 38, bytes_accessed=2 << 20, transcendentals=0),
         name="regroup",
     )(*came)
 
@@ -309,56 +305,57 @@
 
 
 def spectra_kernel(side, halo, own, kept, taps, table, *refs):
-    out = refs[-1]
+    out, made, go = refs[-3:]
     groups, parts = out.shape[0], out.shape[2]
     depth = TAPS - 1
-    halos = [halo[t] for t in range(depth)]
-    if side:
-        ends = lax.axis_index("tm") == lax.axis_size("tm") - 1
-        frames = [own[t] for t in range(1, depth)] + [kept[...]]
-        pool = [jnp.where(ends, jnp.zeros_like(frame), frame) for frame in frames] + halos
-    else:
-        pool = halos + [kept[...]] + [own[t] for t in range(depth - 1)]
-    for s in range(depth):
-        spectrum = jnp.dot(
-            table[...],
-            filtered_frame(taps, pool[s : s + TAPS], kept.shape[1]),
-            preferred_element_type=jnp.float32,
-        ).astype(jnp.bfloat16)
-        for q in range(parts):
-            for g in range(groups):
-                at = (q * groups + g) * ROWS
-                out[g, s, q] = spectrum[at : at + ROWS]
+    half = WIDTH // 2
+    sends = []
+    for k in range(half // LANES):
+        cols = slice(k * LANES, (k + 1) * LANES)
+        halos = [halo[t, :, cols] for t in range(depth)]
+        if side:
+            ends = lax.axis_index("tm") == lax.axis_size("tm") - 1
+            frames = [own[t, :, cols] for t in range(1, depth)] + [kept[:, cols]]
+            pool = [jnp.where(ends, jnp.zeros_like(frame), frame) for frame in frames] + halos
+        else:
+            pool = halos + [kept[:, cols]] + [own[t, :, cols] for t in range(depth - 1)]
+        for s in range(depth):
+            spectrum = jnp.dot(
+                table[...],
+                filtered_frame(taps, pool[s : s + TAPS], LANES),
+                preferred_element_type=jnp.float32,
+            ).astype(jnp.bfloat16)
+            for q in range(parts):
+                for g in range(groups):
+                    at = (q * groups + g) * ROWS
+                    made[k, g, s, q] = spectrum[at : at + ROWS]
+        to = slice(side * half + k * LANES, side * half + (k + 1) * LANES)
+        sends.append(pltpu.make_async_copy(made.at[k], out.at[:, :, :, :, to], go.at[k]))
+        sends[-1].start()
+    for copy in sends:
+        copy.wait()
 
 
 def later_spectra(side, halo, own, kept, taps, table, groups, parts, so_far):
     depth = TAPS - 1
     frame, cols = kept.shape
-    three = pl.BlockSpec((depth, frame, LANES), lambda k: (0, 0, k))
-    tiles = cols // LANES
     more = [] if so_far is None else [so_far]
     return pl.pallas_call(
         functools.partial(spectra_kernel, side),
-        grid=(cols // LANES,),
-        in_specs=[
-            three,
-            three,
-            pl.BlockSpec((frame, LANES), lambda k: (0, k)),
-            pl.BlockSpec((TAPS, frame, PANEL), lambda k: (0, 0, 0)),
-            pl.BlockSpec((frame, frame), lambda k: (0, 0)),
-        ]
-        + [pl.BlockSpec(memory_space=pl.ANY)] * len(more),
-        out_specs=pl.BlockSpec(
-            (groups, depth, parts, ROWS, LANES), lambda k: (0, 0, 0, 0, side * tiles + k)
-        ),
+        in_specs=[INSIDE] * 5 + [ANYWHERE] * len(more),
+        out_specs=ANYWHERE,
         out_shape=pltpu.HBM((groups, depth, parts, ROWS, WIDTH), jnp.bfloat16),
+        scratch_shapes=[
+            pltpu.VMEM((cols // LANES, groups, depth, parts, ROWS, LANES), jnp.bfloat16),
+            pltpu.SemaphoreType.DMA((cols // LANES,)),
+        ],
         input_output_aliases={5: 0} if more else {},
-        compiler_params=pltpu.CompilerParams(vmem_limit_bytes=VMEM // 2),
+        compiler_params=pltpu.CompilerParams(vmem_limit_bytes=VMEM // 3),
         cost_estimate=pl.CostEstimate(
             flops=200 * depth * frame * frame * cols, bytes_accessed=6 << 20, transcendentals=0
         ),
         name="later_spectra",
-    )(halo, *pin(own, kept, taps, table), *more)
+    )(halo, own, kept, taps, table, *more)
 
 
 def correlate_kernel(scale, blocks, *refs):
@@ -445,7 +442,7 @@
             num_scalar_prefetch=1,
             grid=(1,),
             in_specs=[anywhere] * PLANE
-            + [inside, pl.BlockSpec(orders.shape, lambda s, blocks: (0, 0))],
+            + [inside, inside],
             out_specs=anywhere,
             scratch_shapes=[
                 pltpu.VMEM((per, keys, WIDTH), jnp.bfloat16),
@@ -458,14 +455,14 @@
             ],
         ),
         out_shape=pltpu.HBM(shape, jnp.float32),
-        compiler_params=pltpu.CompilerParams(vmem_limit_bytes=VMEM * 5 // 6),
+        compiler_params=pltpu.CompilerParams(vmem_limit_bytes=VMEM * 5//6),
         cost_estimate=pl.CostEstimate(
             flops=4 * parts * per * keys * PANEL * PANEL * blocks,
             bytes_accessed=36 << 20,
             transcendentals=0,
         ),
         name="correlate",
-    )(places, *pin(*first), rest, *pin(orders))
+    )(places, *first, rest, orders)
 
 
 def body(voltages, panel_map, block_list):
@@ -476,12 +473,12 @@
     taps = filter_taps()
     table = dft_table(groups, parts)
     block_list = block_list.T
-    up, hot0, places = select(0, block_list, panel_map, frames)
+    up, hot0, volts, places = select(0, block_list, panel_map, frames)
     earlier = shifted(up, "tm", 1, False)
-    down, hot1, _ = select(1, block_list, panel_map, frames)
+    down, hot1 = select(1, block_list, panel_map, volts)
     later = shifted(down, "tm", -1, True)
-    left, right, *planes = first_spectra(
-        frames, (hot0, hot1), up, down, taps, table, groups, parts
+    left, right, taps, table, orders, *planes = first_spectra(
+        volts, (hot0, hot1), up, down, taps, table, row_orders(), groups, parts
     )
     came = across_planes(planes)
     later_half = functools.partial(
@@ -489,10 +486,11 @@
     )
     rest = later_half(0, earlier, up, left, so_far=None)
     rest = later_half(1, later, down, right, so_far=rest)
-    rest, came = lax.optimization_barrier((rest, came))
+
+
     first = within_plane(came)
     rest = lax.all_to_all(rest, "tm", split_axis=0, concat_axis=0, tiled=True)
-    return correlate(places, first, rest, row_orders(), block_list.shape[1])
+    return correlate(places, first, rest, orders, block_list.shape[1])
 
 
 def solution(mesh):

time: 153 us -> 145 us (0.948)
  Pallas kernels: 48.5 us -> 39.4 us
  waiting for transfers between devices: 82.6 us -> 87 us
  starting transfers between devices: 20.6 us -> 16.4 us
    pallas_call x5, Pallas kernels: 31 us -> 21.1 us  [the longest x2 11.4 us: select(): pl.pallas_call(right_kernel if side else left_kernel, grid_spec=pltpu.Pre...]
    all_to_all x1, starting transfers between devices: 11.9 us -> 7.06 us  [body(): rest = lax.all_to_all(rest, 'tm', split_axis=0, concat_axis=0, tiled=True)]
    ppermute x2, waiting for transfers between devices: 17.8 us -> 22.1 us  [shifted(): return lax.ppermute(block, axis, route)]
  transfers between devices with their start and end apart: 9 -> 9, of which waited for: 4 -> 5; matrix products, arithmetic and copies ran while one was open for 0% -> 0% of each run, Pallas kernels for 17% -> 12%
where the time goes in v5:
time: 145 us
  waiting for transfers between devices  87 us (60%)
  Pallas kernels  39.4 us (27%)
  starting transfers between devices  16.4 us (11%)
  local copies, waits for them, and re-layouts  1.63 us (1%)
    all_to_all x1, waiting for transfers between devices, body(): rest = lax.all_to_all(rest, 'tm', split_axis=0, concat_axis=0, tiled=True)  40.1 us
    ppermute x3, waiting for transfers between devices, within_plane(): lax.ppermute(block, 'tm', [(i, i ^ q) for i in range(count)])  24.8 us
    ppermute x2, waiting for transfers between devices, shifted(): return lax.ppermute(block, axis, route)  22.1 us
    pallas_call x1, Pallas kernels, correlate(): pl.pallas_call(functools.partial(correlate_kernel, 1.0 / (groups * TAPS))...  16.1 us
    pallas_call x2, Pallas kernels, select(): pl.pallas_call(right_kernel if side else left_kernel, grid_spec=pltpu.Pre...  11.4 us
    all_to_all x1, starting transfers between devices, body(): rest = lax.all_to_all(rest, 'tm', split_axis=0, concat_axis=0, tiled=True)  7.06 us
    pallas_call x2, Pallas kernels, later_spectra(): pl.pallas_call(functools.partial(spectra_kernel, side), in_specs=[INSIDE]...  4.89 us
    pallas_call x1, Pallas kernels, first_spectra(): pl.pallas_call(functools.partial(first_kernel, planes), in_specs=[INSIDE]...  4.74 us
  transfers between devices with their start and end apart: 9, of which 5 were waited for; matrix products, arithmetic and copies ran while one was open for 0% of the time, Pallas kernels for 12%

profile of v5, /device:TPU:15, one launch (start us, length us, event | category | flops | bytes accessed | tf_op | source)
XLA Modules:
  0.0 144.7 jit_solution(16544761349718780287)
XLA Ops:
  0.0 0.0 copy-start.2
  0.0 0.7 copy-done.2
  0.7 6.5 %select.2 = (bf16[3,512,512]{2,1,0:T(8,128)(2,1)S(1)}, bf16[2048,512]{1,0:T(8,128)(2,1)S(1)}, bf16[4,512,2048]{2,1,0:T(8,128)(2,1)S(1)}, s32[2,16]{1,0:T(2,128)S(1)}) custom-call(s32[2,16]{1,0:T(2,128)S(1)} %bitcast.3, bf16[4,512,2048]{2,1,0:T(8,128)(2,1)} %bitcast.5, s32[16,128]{1,0:T(8,128)} %bitcast.6), custom_call_target="tpu_custom_call" | custom-call | flops 3221225472 | bytes 10485760 | tf_op jit(solution)/shard_map/select/pallas_call | solution.py:155
  7.2 3.7 %collective-permute-start.7 = (bf16[3,512,512]{2,1,0:T(8,128)(2,1)S(1)}, bf16[3,512,512]{2,1,0:T(8,128)(2,1)S(1)}, u32[]{:S(2)}, u32[]{:S(2)}) collective-permute-start(bf16[3,512,512]{2,1,0:T(8,128)(2,1)S(1)} %get-tuple-element.28.up.own), channel_id=1, source_target_pairs={{0,1},{1,2},{2,3},{3,4},{4,5},{5,6},{6,7},{7,8},{8,9},{9,10},{10,1... | collective-permute-start | bytes 4718600 | tf_op jit(solution)/shard_map/ppermute | solution.py:30
  11.0 4.9 %select.3 = (bf16[3,512,512]{2,1,0:T(8,128)(2,1)S(1)}, bf16[2048,512]{1,0:T(8,128)(2,1)S(1)}) custom-call(s32[2,16]{1,0:T(2,128)S(1)} %bitcast.4, bf16[4,512,2048]{2,1,0:T(8,128)(2,1)S(1)} %get-tuple-element.25.volts, s32[16,128]{1,0:T(8,128)} %bitcast.7), custom_call_target="tpu_custom_call" | custom-call | flops 3221225472 | bytes 10485760 | tf_op jit(solution)/shard_map/select/pallas_call | solution.py:155
  15.9 0.1 collective-permute-start.6
  15.9 4.7 %first_spectra.1 = (bf16[512,512]{1,0:T(8,128)(2,1)S(1)}, bf16[512,512]{1,0:T(8,128)(2,1)S(1)}, f32[4,512,128]{2,1,0:T(8,128)S(1)}, bf16[512,512]{1,0:T(8,128)(2...) custom-call(bf16[4,512,2048]{2,1,0:T(8,128)(2,1)S(1)} %get-tuple-ele, ...), custom_call_target="tpu_custom_call" | custom-call | flops 2684354560 | bytes 16777216 | tf_op jit(solution)/shard_map/first_spectra/pallas_call | solution.py:225
  20.7 0.2 collective-permute-start
  20.9 2.3 %collective-permute-start.1 = (bf16[4,2,16,1024]{3,2,1,0:T(8,128)(2,1)}, bf16[4,2,16,1024]{3,2,1,0:T(8,128)(2,1)}, u32[]{:S(2)}, u32[]{:S(2)}) collective-permute-start(bf16[4,2,16,1024]{3,2,1,0:T(8,128)(2,1)} %get-tuple-element.32), channel_id=1, source_target_pairs={{0,8},{1,9},{2,10},{3,11},{4,12},{5,13},{6,14},{7,15},{8,0},{9,1},... | collective-permute-start | bytes 786440 | tf_op jit(solution)/shard_map/ppermute | solution.py:291
  23.2 0.2 collective-permute-start.2
  23.4 9.4 %collective-permute-done.7.halo = bf16[3,512,512]{2,1,0:T(8,128)(2,1)S(1)} collective-permute-done((bf16[3,512,512]{2,1,0:T(8,128)(2,1)S(1)}, bf16[3,512,512]{2,1,0:T(8,128)(2,1)S(1)}, u32[]{:S(2)}, u32[]{:S(2)}) %collective-permute-start.7) | collective-permute-done | bytes 1572896 | tf_op jit(solution)/shard_map/ppermute | solution.py:30
  32.8 2.4 %later_spectra.2.refs_0_ = bf16[16,3,2,16,1024]{4,3,2,1,0:T(8,128)(2,1)} custom-call(bf16[3,512,512]{2,1,0:T(8,128)(2,1)S(1)} %collective-permute-done.7.halo, bf16[3,512,512]{2,1,0:T(8,128)(2,1)S(1)} %get-tuple-element.28.up.own, bf16[512,512]{1,0:T(8,128)(2,1)S(1)} %get-tuple-element.41.kept, f32[4,512,128]{2,1,0:T(8,128)S(1)} %get-tuple-element.39.taps, ...), custom_call_target="tpu_custom_call" | custom-call | flops 80530636800 | bytes 6291456 | tf_op jit(solution)/shard_map/later_spectra/pallas_call | solution.py:343
  35.2 12.7 %collective-permute-done.6.halo = bf16[3,512,512]{2,1,0:T(8,128)(2,1)S(1)} collective-permute-done((bf16[3,512,512]{2,1,0:T(8,128)(2,1)S(1)}, bf16[3,512,512]{2,1,0:T(8,128)(2,1)S(1)}, u32[]{:S(2)}, u32[]{:S(2)}) %collective-permute-start.6) | collective-permute-done | bytes 1572896 | tf_op jit(solution)/shard_map/ppermute | solution.py:30
  47.9 2.4 %later_spectra.3 = bf16[16,3,2,16,1024]{4,3,2,1,0:T(8,128)(2,1)} custom-call(bf16[3,512,512]{2,1,0:T(8,128)(2,1)S(1)} %collective-permute-done.6.halo, bf16[3,512,512]{2,1,0:T(8,128)(2,1)S(1)} %get-tuple-element.29.down.own, bf16[512,512]{1,0:T(8,128)(2,1)S(1)} %get-tuple-element.38.kept, ...), custom_call_target="tpu_custom_call", output_to_operand_aliasing={{}: (5, {})} | custom-call | flops 80530636800 | bytes 6291456 | tf_op jit(solution)/shard_map/later_spectra/pallas_call | solution.py:343
  50.4 0.0 copy-start.1
  50.4 7.1 %all-to-all-start = ((bf16[16,3,2,16,1024]{4,3,2,1,0:T(8,128)(2,1)}), bf16[16,3,2,16,1024]{4,3,2,1,0:T(8,128)(2,1)}, u32[]{:S(2)}, u32[]{:S(2)}) async-start(bf16[16,3,2,16,1024]{4,3,2,1,0:T(8,128)(2,1)} %later_spectra.3), calls=%async_computation | async-start | bytes 6291456 | tf_op jit(solution)/shard_map/all_to_all | solution.py:492
  57.5 0.0 collective-permute-done.refs_1_
  57.5 0.0 collective-permute-done.1.refs_2_
  57.5 0.0 collective-permute-done.2.refs_3_
  57.5 0.0 copy-done.1
  57.5 2.2 %regroup.1 = (bf16[4,2,16,1024]{3,2,1,0:T(8,128)(2,1)}, bf16[4,2,16,1024]{3,2,1,0:T(8,128)(2,1)}, bf16[4,2,16,1024]{3,2,1,0:T(8,128)(2,1)}, bf16[4,2,16,1024]{3,2,1,0:T(8,128)(2,1)}) custom-call(bf16[4,2,16,1024]{3,2,1,0:T(8,128)(2,1)S(1)} %copy-done.1, bf16[4,2,16,1024]{3,2,1,0:T(8,128)(2,1)} %collective-permute-done.refs_1_, ...), custom_call_target="tpu_custom_call" | custom-call | flops 274877906944 | bytes 2097152 | tf_op jit(solution)/shard_map/regroup/pallas_call | solution.py:272
  59.7 0.4 collective-permute-start.3
  60.1 2.4 %collective-permute-start.4 = (bf16[4,2,16,1024]{3,2,1,0:T(8,128)(2,1)}, bf16[4,2,16,1024]{3,2,1,0:T(8,128)(2,1)S(1)}, u32[]{:S(2)}, u32[]{:S(2)}) collective-permute-start(bf16[4,2,16,1024]{3,2,1,0:T(8,128)(2,1)} %get-tuple-element.36), channel_id=1, source_target_pairs={{0,2},{1,3},{2,0},{3,1},{4,6},{5,7},{6,4},{7,5},{8,10},{9,11},{10,... | collective-permute-start | bytes 786440 | tf_op jit(solution)/shard_map/ppermute | solution.py:301
  62.5 0.0 collective-permute-start.5
  62.6 0.0 collective-permute-done.3.refs_1_
  62.6 18.6 %collective-permute-done.4.refs_2_ = bf16[4,2,16,1024]{3,2,1,0:T(8,128)(2,1)S(1)} collective-permute-done((bf16[4,2,16,1024]{3,2,1,0:T(8,128)(2,1)}, bf16[4,2,16,1024]{3,2,1,0:T(8,128)(2,1)S(1)}, u32[]{:S(2)}, u32[]{:S(2)}) %collective-permute-start.4) | collective-permute-done | bytes 262176 | tf_op jit(solution)/shard_map/ppermute | solution.py:301
  81.2 6.2 %collective-permute-done.5.refs_3_ = bf16[4,2,16,1024]{3,2,1,0:T(8,128)(2,1)S(1)} collective-permute-done((bf16[4,2,16,1024]{3,2,1,0:T(8,128)(2,1)}, bf16[4,2,16,1024]{3,2,1,0:T(8,128)(2,1)S(1)}, u32[]{:S(2)}, u32[]{:S(2)}) %collective-permute-start.5) | collective-permute-done | bytes 262176 | tf_op jit(solution)/shard_map/ppermute | solution.py:301
  87.4 40.1 %all-to-all-done.refs_4_ = bf16[16,3,2,16,1024]{4,3,2,1,0:T(8,128)(2,1)} async-done(((bf16[16,3,2,16,1024]{4,3,2,1,0:T(8,128)(2,1)}), bf16[16,3,2,16,1024]{4,3,2,1,0:T(8,128)(2,1)}, u32[]{:S(2)}, u32[]{:S(2)}) %all-to-all-start) | async-done | bytes 3145760 | tf_op jit(solution)/shard_map/all_to_all | solution.py:492
  127.5 0.0 copy-start
  127.5 0.9 copy-done
  128.4 16.1 %correlate.1 = f32[16,2,16,128,128]{4,3,2,1,0:T(8,128)} custom-call(s32[2,16]{1,0:T(2,128)S(1)} %get-tuple-element.24.blocks, bf16[4,2,16,1024]{3,2,1,0:T(8,128)(2,1)S(1)} %copy-done, bf16[4,2,16,1024]{3,2,1,0:T(8,128)(2,1)S(1)} %collective-permute-done.3.refs_1_, bf16[4,2,16,1024]{3,2,1,0:T(8,128)(2,1)S(1)} %collective-permute-done.4.refs_2_, ...), custom_call_target="tpu_custom_call" | custom-call | flops 2147483648 | bytes 37748736 | tf_op jit(solution)/shard_map/correlate/pallas_call | solution.py:439
Async XLA Ops:
  0.0 0.7 copy-start.2
  7.2 25.5 %collective-permute-start.7 = (bf16[3,512,512]{2,1,0:T(8,128)(2,1)S(1)}, bf16[3,512,512]{2,1,0:T(8,128)(2,1)S(1)}, u32[]{:S(2)}, u32[]{:S(2)}) collective-permute-start(bf16[3,512,512]{2,1,0:T(8,128)(2,1)S(1)} %get-tuple-element.28.up.own), channel_id=1, source_target_pairs={{0,1},{1,2},{2,3},{3,4},{4,5},{5,6},{6,7},{7,8},{8,9},{9,10},{10,1... | collective-permute-start | bytes 4718600 | tf_op jit(solution)/shard_map/ppermute | solution.py:30
  15.9 32.1 %collective-permute-start.6 = (bf16[3,512,512]{2,1,0:T(8,128)(2,1)S(1)}, bf16[3,512,512]{2,1,0:T(8,128)(2,1)S(1)}, u32[]{:S(2)}, u32[]{:S(2)}) collective-permute-start(bf16[3,512,512]{2,1,0:T(8,128)(2,1)S(1)} %get-tuple-element.29.down.own), channel_id=1, source_target_pairs={{0,15},{1,0},{2,1},{3,2},{4,3},{5,4},{6,5},{7,6},{8,7},{9,8},{10,9... | collective-permute-start | bytes 4718600 | tf_op jit(solution)/shard_map/ppermute | solution.py:30
  20.7 36.8 %collective-permute-start = (bf16[4,2,16,1024]{3,2,1,0:T(8,128)(2,1)}, bf16[4,2,16,1024]{3,2,1,0:T(8,128)(2,1)}, u32[]{:S(2)}, u32[]{:S(2)}) collective-permute-start(bf16[4,2,16,1024]{3,2,1,0:T(8,128)(2,1)} %get-tuple-element.31), channel_id=1, source_target_pairs={{0,4},{1,5},{2,6},{3,7},{4,0},{5,1},{6,2},{7,3},{8,12},{9,13},{10,... | collective-permute-start | bytes 786440 | tf_op jit(solution)/shard_map/ppermute | solution.py:291
  20.9 36.5 %collective-permute-start.1 = (bf16[4,2,16,1024]{3,2,1,0:T(8,128)(2,1)}, bf16[4,2,16,1024]{3,2,1,0:T(8,128)(2,1)}, u32[]{:S(2)}, u32[]{:S(2)}) collective-permute-start(bf16[4,2,16,1024]{3,2,1,0:T(8,128)(2,1)} %get-tuple-element.32), channel_id=1, source_target_pairs={{0,8},{1,9},{2,10},{3,11},{4,12},{5,13},{6,14},{7,15},{8,0},{9,1},... | collective-permute-start | bytes 786440 | tf_op jit(solution)/shard_map/ppermute | solution.py:291
  23.2 34.3 %collective-permute-start.2 = (bf16[4,2,16,1024]{3,2,1,0:T(8,128)(2,1)}, bf16[4,2,16,1024]{3,2,1,0:T(8,128)(2,1)}, u32[]{:S(2)}, u32[]{:S(2)}) collective-permute-start(bf16[4,2,16,1024]{3,2,1,0:T(8,128)(2,1)} %get-tuple-element.33), channel_id=1, source_target_pairs={{0,12},{1,13},{2,14},{3,15},{4,8},{5,9},{6,10},{7,11},{8,4},{9,5},... | collective-permute-start | bytes 786440 | tf_op jit(solution)/shard_map/ppermute | solution.py:291
  50.4 7.1 %copy-start.1 = (bf16[4,2,16,1024]{3,2,1,0:T(8,128)(2,1)S(1)}, bf16[4,2,16,1024]{3,2,1,0:T(8,128)(2,1)}, u32[]{:S(2)}) copy-start(bf16[4,2,16,1024]{3,2,1,0:T(8,128)(2,1)} %get-tuple-element.30.refs_0_) | copy-start | bytes 786436
  50.4 77.1 %all-to-all-start = ((bf16[16,3,2,16,1024]{4,3,2,1,0:T(8,128)(2,1)}), bf16[16,3,2,16,1024]{4,3,2,1,0:T(8,128)(2,1)}, u32[]{:S(2)}, u32[]{:S(2)}) async-start(bf16[16,3,2,16,1024]{4,3,2,1,0:T(8,128)(2,1)} %later_spectra.3), calls=%async_computation | async-start | bytes 6291456 | tf_op jit(solution)/shard_map/all_to_all | solution.py:492
  59.7 2.8 %collective-permute-start.3 = (bf16[4,2,16,1024]{3,2,1,0:T(8,128)(2,1)}, bf16[4,2,16,1024]{3,2,1,0:T(8,128)(2,1)S(1)}, u32[]{:S(2)}, u32[]{:S(2)}) collective-permute-start(bf16[4,2,16,1024]{3,2,1,0:T(8,128)(2,1)} %get-tuple-element.35), channel_id=1, source_target_pairs={{0,1},{1,0},{2,3},{3,2},{4,5},{5,4},{6,7},{7,6},{8,9},{9,8},{10,11... | collective-permute-start | bytes 786440 | tf_op jit(solution)/shard_map/ppermute | solution.py:301
  60.1 21.0 %collective-permute-start.4 = (bf16[4,2,16,1024]{3,2,1,0:T(8,128)(2,1)}, bf16[4,2,16,1024]{3,2,1,0:T(8,128)(2,1)S(1)}, u32[]{:S(2)}, u32[]{:S(2)}) collective-permute-start(bf16[4,2,16,1024]{3,2,1,0:T(8,128)(2,1)} %get-tuple-element.36), channel_id=1, source_target_pairs={{0,2},{1,3},{2,0},{3,1},{4,6},{5,7},{6,4},{7,5},{8,10},{9,11},{10,... | collective-permute-start | bytes 786440 | tf_op jit(solution)/shard_map/ppermute | solution.py:301
  62.5 24.9 %collective-permute-start.5 = (bf16[4,2,16,1024]{3,2,1,0:T(8,128)(2,1)}, bf16[4,2,16,1024]{3,2,1,0:T(8,128)(2,1)S(1)}, u32[]{:S(2)}, u32[]{:S(2)}) collective-permute-start(bf16[4,2,16,1024]{3,2,1,0:T(8,128)(2,1)} %get-tuple-element.37), channel_id=1, source_target_pairs={{0,3},{1,2},{2,1},{3,0},{4,7},{5,6},{6,5},{7,4},{8,11},{9,10},{10,... | collective-permute-start | bytes 786440 | tf_op jit(solution)/shard_map/ppermute | solution.py:301
  127.5 1.0 copy-start

commit v6 on v5

--- a/solution.py
+++ b/solution.py
@@ -280,7 +280,7 @@
         ],
         out_shape=[pltpu.HBM(shape, jnp.bfloat16)] * PLANE,
         compiler_params=pltpu.CompilerParams(vmem_limit_bytes=VMEM // 12),
-        cost_estimate=pl.CostEstimate(flops=1 << 38, bytes_accessed=2 << 20, transcendentals=0),
+        cost_estimate=pl.CostEstimate(flops=1 << 37, bytes_accessed=2 << 20, transcendentals=0),
         name="regroup",
     )(*came)
 
@@ -350,7 +350,7 @@
             pltpu.SemaphoreType.DMA((cols // LANES,)),
         ],
         input_output_aliases={5: 0} if more else {},
-        compiler_params=pltpu.CompilerParams(vmem_limit_bytes=VMEM // 3),
+        compiler_params=pltpu.CompilerParams(vmem_limit_bytes=VMEM // 6),
         cost_estimate=pl.CostEstimate(
             flops=200 * depth * frame * frame * cols, bytes_accessed=6 << 20, transcendentals=0
         ),
@@ -462,7 +462,7 @@
             transcendentals=0,
         ),
         name="correlate",
-    )(places, *first, rest, orders)
+    )(places, *pin(*first), rest, orders)
 
 
 def body(voltages, panel_map, block_list):

time: 145 us -> 142 us (0.979)
  waiting for transfers between devices: 87 us -> 85.1 us
  Pallas kernels: 39.4 us -> 37.7 us
    ppermute x3, waiting for transfers between devices: 24.8 us -> 22.9 us  [within_plane(): lax.ppermute(block, 'tm', [(i, i ^ q) for i in range(count)])]
    pallas_call x1, Pallas kernels: 16.1 us -> 14.4 us  [correlate(): pl.pallas_call(functools.partial(correlate_kernel, 1.0 / (groups * TAPS))...]
where the time goes in v6:
time: 142 us
  waiting for transfers between devices  85.1 us (60%)
  Pallas kernels  37.7 us (27%)
  starting transfers between devices  16.4 us (12%)
  local copies, waits for them, and re-layouts  2.33 us (2%)
    all_to_all x1, waiting for transfers between devices, body(): rest = lax.all_to_all(rest, 'tm', split_axis=0, concat_axis=0, tiled=True)  40.1 us
    ppermute x3, waiting for transfers between devices, within_plane(): lax.ppermute(block, 'tm', [(i, i ^ q) for i in range(count)])  22.9 us
    ppermute x2, waiting for transfers between devices, shifted(): return lax.ppermute(block, axis, route)  22 us
    pallas_call x1, Pallas kernels, correlate(): pl.pallas_call(functools.partial(correlate_kernel, 1.0 / (groups * TAPS))...  14.4 us
    pallas_call x2, Pallas kernels, select(): pl.pallas_call(right_kernel if side else left_kernel, grid_spec=pltpu.Pre...  11.4 us
    all_to_all x1, starting transfers between devices, body(): rest = lax.all_to_all(rest, 'tm', split_axis=0, concat_axis=0, tiled=True)  6.93 us
    pallas_call x2, Pallas kernels, later_spectra(): pl.pallas_call(functools.partial(spectra_kernel, side), in_specs=[INSIDE]...  4.88 us
    pallas_call x1, Pallas kernels, first_spectra(): pl.pallas_call(functools.partial(first_kernel, planes), in_specs=[INSIDE]...  4.8 us
  transfers between devices with their start and end apart: 9, of which 5 were waited for; matrix products, arithmetic and copies ran while one was open for 0% of the time, Pallas kernels for 12%

profile of v6, /device:TPU:15, one launch (start us, length us, event | category | flops | bytes accessed | tf_op | source)
XLA Modules:
  0.0 141.8 jit_solution(17058696945178344479)
XLA Ops:
  0.0 0.0 copy-start.1
  0.0 0.7 copy-done.1
  0.7 6.5 %select.2 = (bf16[3,512,512]{2,1,0:T(8,128)(2,1)S(1)}, bf16[2048,512]{1,0:T(8,128)(2,1)S(1)}, bf16[4,512,2048]{2,1,0:T(8,128)(2,1)S(1)}, s32[2,16]{1,0:T(2,128)S(1)}) custom-call(s32[2,16]{1,0:T(2,128)S(1)} %bitcast.3, bf16[4,512,2048]{2,1,0:T(8,128)(2,1)} %bitcast.5, s32[16,128]{1,0:T(8,128)} %bitcast.6), custom_call_target="tpu_custom_call" | custom-call | flops 3221225472 | bytes 10485760 | tf_op jit(solution)/shard_map/select/pallas_call | solution.py:155
  7.2 3.7 %collective-permute-start.7 = (bf16[3,512,512]{2,1,0:T(8,128)(2,1)S(1)}, bf16[3,512,512]{2,1,0:T(8,128)(2,1)S(1)}, u32[]{:S(2)}, u32[]{:S(2)}) collective-permute-start(bf16[3,512,512]{2,1,0:T(8,128)(2,1)S(1)} %get-tuple-element.28.up.own), channel_id=1, source_target_pairs={{0,1},{1,2},{2,3},{3,4},{4,5},{5,6},{6,7},{7,8},{8,9},{9,10},{10,1... | collective-permute-start | bytes 4718600 | tf_op jit(solution)/shard_map/ppermute | solution.py:30
  11.0 4.9 %select.3 = (bf16[3,512,512]{2,1,0:T(8,128)(2,1)S(1)}, bf16[2048,512]{1,0:T(8,128)(2,1)S(1)}) custom-call(s32[2,16]{1,0:T(2,128)S(1)} %bitcast.4, bf16[4,512,2048]{2,1,0:T(8,128)(2,1)S(1)} %get-tuple-element.25.volts, s32[16,128]{1,0:T(8,128)} %bitcast.7), custom_call_target="tpu_custom_call" | custom-call | flops 3221225472 | bytes 10485760 | tf_op jit(solution)/shard_map/select/pallas_call | solution.py:155
  15.9 0.1 collective-permute-start.6
  15.9 4.8 %first_spectra.1 = (bf16[512,512]{1,0:T(8,128)(2,1)S(1)}, bf16[512,512]{1,0:T(8,128)(2,1)S(1)}, f32[4,512,128]{2,1,0:T(8,128)S(1)}, bf16[512,512]{1,0:T(8,128)(2...) custom-call(bf16[4,512,2048]{2,1,0:T(8,128)(2,1)S(1)} %get-tuple-ele, ...), custom_call_target="tpu_custom_call" | custom-call | flops 2684354560 | bytes 16777216 | tf_op jit(solution)/shard_map/first_spectra/pallas_call | solution.py:225
  20.7 0.2 collective-permute-start
  21.0 2.3 %collective-permute-start.1 = (bf16[4,2,16,1024]{3,2,1,0:T(8,128)(2,1)}, bf16[4,2,16,1024]{3,2,1,0:T(8,128)(2,1)}, u32[]{:S(2)}, u32[]{:S(2)}) collective-permute-start(bf16[4,2,16,1024]{3,2,1,0:T(8,128)(2,1)} %get-tuple-element.32), channel_id=1, source_target_pairs={{0,8},{1,9},{2,10},{3,11},{4,12},{5,13},{6,14},{7,15},{8,0},{9,1},... | collective-permute-start | bytes 786440 | tf_op jit(solution)/shard_map/ppermute | solution.py:291
  23.3 0.2 collective-permute-start.2
  23.4 9.1 %collective-permute-done.7.halo = bf16[3,512,512]{2,1,0:T(8,128)(2,1)S(1)} collective-permute-done((bf16[3,512,512]{2,1,0:T(8,128)(2,1)S(1)}, bf16[3,512,512]{2,1,0:T(8,128)(2,1)S(1)}, u32[]{:S(2)}, u32[]{:S(2)}) %collective-permute-start.7) | collective-permute-done | bytes 1572896 | tf_op jit(solution)/shard_map/ppermute | solution.py:30
  32.6 2.4 %later_spectra.2.refs_0_ = bf16[16,3,2,16,1024]{4,3,2,1,0:T(8,128)(2,1)} custom-call(bf16[3,512,512]{2,1,0:T(8,128)(2,1)S(1)} %collective-permute-done.7.halo, bf16[3,512,512]{2,1,0:T(8,128)(2,1)S(1)} %get-tuple-element.28.up.own, bf16[512,512]{1,0:T(8,128)(2,1)S(1)} %get-tuple-element.41.kept, f32[4,512,128]{2,1,0:T(8,128)S(1)} %get-tuple-element.39.taps, ...), custom_call_target="tpu_custom_call" | custom-call | flops 80530636800 | bytes 6291456 | tf_op jit(solution)/shard_map/later_spectra/pallas_call | solution.py:343
  35.0 12.9 %collective-permute-done.6.halo = bf16[3,512,512]{2,1,0:T(8,128)(2,1)S(1)} collective-permute-done((bf16[3,512,512]{2,1,0:T(8,128)(2,1)S(1)}, bf16[3,512,512]{2,1,0:T(8,128)(2,1)S(1)}, u32[]{:S(2)}, u32[]{:S(2)}) %collective-permute-start.6) | collective-permute-done | bytes 1572896 | tf_op jit(solution)/shard_map/ppermute | solution.py:30
  47.9 2.4 %later_spectra.3 = bf16[16,3,2,16,1024]{4,3,2,1,0:T(8,128)(2,1)} custom-call(bf16[3,512,512]{2,1,0:T(8,128)(2,1)S(1)} %collective-permute-done.6.halo, bf16[3,512,512]{2,1,0:T(8,128)(2,1)S(1)} %get-tuple-element.29.down.own, bf16[512,512]{1,0:T(8,128)(2,1)S(1)} %get-tuple-element.38.kept, ...), custom_call_target="tpu_custom_call", output_to_operand_aliasing={{}: (5, {})} | custom-call | flops 80530636800 | bytes 6291456 | tf_op jit(solution)/shard_map/later_spectra/pallas_call | solution.py:343
  50.4 6.9 %all-to-all-start = ((bf16[16,3,2,16,1024]{4,3,2,1,0:T(8,128)(2,1)}), bf16[16,3,2,16,1024]{4,3,2,1,0:T(8,128)(2,1)S(1)}, u32[]{:S(2)}, u32[]{:S(2)}) async-start(bf16[16,3,2,16,1024]{4,3,2,1,0:T(8,128)(2,1)} %later_spectra.3), calls=%async_computation | async-start | bytes 6291456 | tf_op jit(solution)/shard_map/all_to_all | solution.py:492
  57.3 0.0 collective-permute-done.refs_1_
  57.3 0.0 collective-permute-done.1.refs_2_
  57.3 0.0 collective-permute-done.2.refs_3_
  57.3 0.0 copy-start
  57.3 0.9 copy-done
  58.3 2.2 %regroup.1 = (bf16[4,2,16,1024]{3,2,1,0:T(8,128)(2,1)}, bf16[4,2,16,1024]{3,2,1,0:T(8,128)(2,1)}, bf16[4,2,16,1024]{3,2,1,0:T(8,128)(2,1)}, bf16[4,2,16,1024]{3,2,1,0:T(8,128)(2,1)}) custom-call(bf16[4,2,16,1024]{3,2,1,0:T(8,128)(2,1)S(1)} %copy-done, bf16[4,2,16,1024]{3,2,1,0:T(8,128)(2,1)} %collective-permute-done.refs_1_, ...), custom_call_target="tpu_custom_call" | custom-call | flops 137438953472 | bytes 2097152 | tf_op jit(solution)/shard_map/regroup/pallas_call | solution.py:272
  60.5 0.4 collective-permute-start.3
  60.9 2.6 %collective-permute-start.4 = (bf16[4,2,16,1024]{3,2,1,0:T(8,128)(2,1)}, bf16[4,2,16,1024]{3,2,1,0:T(8,128)(2,1)S(1)}, u32[]{:S(2)}, u32[]{:S(2)}) collective-permute-start(bf16[4,2,16,1024]{3,2,1,0:T(8,128)(2,1)} %get-tuple-element.36), channel_id=1, source_target_pairs={{0,2},{1,3},{2,0},{3,1},{4,6},{5,7},{6,4},{7,5},{8,10},{9,11},{10,... | collective-permute-start | bytes 786440 | tf_op jit(solution)/shard_map/ppermute | solution.py:301
  63.5 0.0 collective-permute-start.5
  63.5 0.0 collective-permute-done.3.refs_1_
  63.5 0.0 copy-start.2
  63.5 17.5 %collective-permute-done.4.refs_2_ = bf16[4,2,16,1024]{3,2,1,0:T(8,128)(2,1)S(1)} collective-permute-done((bf16[4,2,16,1024]{3,2,1,0:T(8,128)(2,1)}, bf16[4,2,16,1024]{3,2,1,0:T(8,128)(2,1)S(1)}, u32[]{:S(2)}, u32[]{:S(2)}) %collective-permute-start.4) | collective-permute-done | bytes 262176 | tf_op jit(solution)/shard_map/ppermute | solution.py:301
  81.0 0.0 copy-done.2
  81.0 0.0 copy-start.3
  81.0 0.7 copy-done.3
  81.7 5.4 %collective-permute-done.5.refs_3_ = bf16[4,2,16,1024]{3,2,1,0:T(8,128)(2,1)} collective-permute-done((bf16[4,2,16,1024]{3,2,1,0:T(8,128)(2,1)}, bf16[4,2,16,1024]{3,2,1,0:T(8,128)(2,1)}, u32[]{:S(2)}, u32[]{:S(2)}) %collective-permute-start.5) | collective-permute-done | bytes 262176 | tf_op jit(solution)/shard_map/ppermute | solution.py:301
  87.1 40.1 %all-to-all-done.refs_4_ = bf16[16,3,2,16,1024]{4,3,2,1,0:T(8,128)(2,1)S(1)} async-done(((bf16[16,3,2,16,1024]{4,3,2,1,0:T(8,128)(2,1)}), bf16[16,3,2,16,1024]{4,3,2,1,0:T(8,128)(2,1)S(1)}, u32[]{:S(2)}, u32[]{:S(2)}) %all-to-all-start) | async-done | bytes 3145760 | tf_op jit(solution)/shard_map/all_to_all | solution.py:492
  127.2 14.4 %correlate.1 = f32[16,2,16,128,128]{4,3,2,1,0:T(8,128)} custom-call(s32[2,16]{1,0:T(2,128)S(1)} %get-tuple-element.24.blocks, bf16[4,2,16,1024]{3,2,1,0:T(8,128)(2,1)} %get-tuple-element.34.refs_0_, bf16[4,2,16,1024]{3,2,1,0:T(8,128)(2,1)} %copy-done.2, bf16[4,2,16,1024]{3,2,1,0:T(8,128)(2,1)} %copy-done.3, ...), custom_call_target="tpu_custom_call" | custom-call | flops 2147483648 | bytes 37748736 | tf_op jit(solution)/shard_map/correlate/pallas_call | solution.py:439
Async XLA Ops:
  0.0 0.7 copy-start.1
  7.2 25.4 %collective-permute-start.7 = (bf16[3,512,512]{2,1,0:T(8,128)(2,1)S(1)}, bf16[3,512,512]{2,1,0:T(8,128)(2,1)S(1)}, u32[]{:S(2)}, u32[]{:S(2)}) collective-permute-start(bf16[3,512,512]{2,1,0:T(8,128)(2,1)S(1)} %get-tuple-element.28.up.own), channel_id=1, source_target_pairs={{0,1},{1,2},{2,3},{3,4},{4,5},{5,6},{6,7},{7,8},{8,9},{9,10},{10,1... | collective-permute-start | bytes 4718600 | tf_op jit(solution)/shard_map/ppermute | solution.py:30
  15.9 32.1 %collective-permute-start.6 = (bf16[3,512,512]{2,1,0:T(8,128)(2,1)S(1)}, bf16[3,512,512]{2,1,0:T(8,128)(2,1)S(1)}, u32[]{:S(2)}, u32[]{:S(2)}) collective-permute-start(bf16[3,512,512]{2,1,0:T(8,128)(2,1)S(1)} %get-tuple-element.29.down.own), channel_id=1, source_target_pairs={{0,15},{1,0},{2,1},{3,2},{4,3},{5,4},{6,5},{7,6},{8,7},{9,8},{10,9... | collective-permute-start | bytes 4718600 | tf_op jit(solution)/shard_map/ppermute | solution.py:30
  20.7 36.6 %collective-permute-start = (bf16[4,2,16,1024]{3,2,1,0:T(8,128)(2,1)}, bf16[4,2,16,1024]{3,2,1,0:T(8,128)(2,1)}, u32[]{:S(2)}, u32[]{:S(2)}) collective-permute-start(bf16[4,2,16,1024]{3,2,1,0:T(8,128)(2,1)} %get-tuple-element.31), channel_id=1, source_target_pairs={{0,4},{1,5},{2,6},{3,7},{4,0},{5,1},{6,2},{7,3},{8,12},{9,13},{10,... | collective-permute-start | bytes 786440 | tf_op jit(solution)/shard_map/ppermute | solution.py:291
  21.0 36.4 %collective-permute-start.1 = (bf16[4,2,16,1024]{3,2,1,0:T(8,128)(2,1)}, bf16[4,2,16,1024]{3,2,1,0:T(8,128)(2,1)}, u32[]{:S(2)}, u32[]{:S(2)}) collective-permute-start(bf16[4,2,16,1024]{3,2,1,0:T(8,128)(2,1)} %get-tuple-element.32), channel_id=1, source_target_pairs={{0,8},{1,9},{2,10},{3,11},{4,12},{5,13},{6,14},{7,15},{8,0},{9,1},... | collective-permute-start | bytes 786440 | tf_op jit(solution)/shard_map/ppermute | solution.py:291
  23.3 34.1 %collective-permute-start.2 = (bf16[4,2,16,1024]{3,2,1,0:T(8,128)(2,1)}, bf16[4,2,16,1024]{3,2,1,0:T(8,128)(2,1)}, u32[]{:S(2)}, u32[]{:S(2)}) collective-permute-start(bf16[4,2,16,1024]{3,2,1,0:T(8,128)(2,1)} %get-tuple-element.33), channel_id=1, source_target_pairs={{0,12},{1,13},{2,14},{3,15},{4,8},{5,9},{6,10},{7,11},{8,4},{9,5},... | collective-permute-start | bytes 786440 | tf_op jit(solution)/shard_map/ppermute | solution.py:291
  50.4 76.9 %all-to-all-start = ((bf16[16,3,2,16,1024]{4,3,2,1,0:T(8,128)(2,1)}), bf16[16,3,2,16,1024]{4,3,2,1,0:T(8,128)(2,1)S(1)}, u32[]{:S(2)}, u32[]{:S(2)}) async-start(bf16[16,3,2,16,1024]{4,3,2,1,0:T(8,128)(2,1)} %later_spectra.3), calls=%async_computation | async-start | bytes 6291456 | tf_op jit(solution)/shard_map/all_to_all | solution.py:492
  57.3 1.0 copy-start
  60.5 3.0 %collective-permute-start.3 = (bf16[4,2,16,1024]{3,2,1,0:T(8,128)(2,1)}, bf16[4,2,16,1024]{3,2,1,0:T(8,128)(2,1)S(1)}, u32[]{:S(2)}, u32[]{:S(2)}) collective-permute-start(bf16[4,2,16,1024]{3,2,1,0:T(8,128)(2,1)} %get-tuple-element.35), channel_id=1, source_target_pairs={{0,1},{1,0},{2,3},{3,2},{4,5},{5,4},{6,7},{7,6},{8,9},{9,8},{10,11... | collective-permute-start | bytes 786440 | tf_op jit(solution)/shard_map/ppermute | solution.py:301
  60.9 20.1 %collective-permute-start.4 = (bf16[4,2,16,1024]{3,2,1,0:T(8,128)(2,1)}, bf16[4,2,16,1024]{3,2,1,0:T(8,128)(2,1)S(1)}, u32[]{:S(2)}, u32[]{:S(2)}) collective-permute-start(bf16[4,2,16,1024]{3,2,1,0:T(8,128)(2,1)} %get-tuple-element.36), channel_id=1, source_target_pairs={{0,2},{1,3},{2,0},{3,1},{4,6},{5,7},{6,4},{7,5},{8,10},{9,11},{10,... | collective-permute-start | bytes 786440 | tf_op jit(solution)/shard_map/ppermute | solution.py:301
  63.5 23.7 %collective-permute-start.5 = (bf16[4,2,16,1024]{3,2,1,0:T(8,128)(2,1)}, bf16[4,2,16,1024]{3,2,1,0:T(8,128)(2,1)}, u32[]{:S(2)}, u32[]{:S(2)}) collective-permute-start(bf16[4,2,16,1024]{3,2,1,0:T(8,128)(2,1)} %get-tuple-element.37), channel_id=1, source_target_pairs={{0,3},{1,2},{2,1},{3,0},{4,7},{5,6},{6,5},{7,4},{8,11},{9,10},{10,... | collective-permute-start | bytes 786440 | tf_op jit(solution)/shard_map/ppermute | solution.py:301
  63.5 17.5 %copy-start.2 = (bf16[4,2,16,1024]{3,2,1,0:T(8,128)(2,1)}, bf16[4,2,16,1024]{3,2,1,0:T(8,128)(2,1)S(1)}, u32[]{:S(2)}) copy-start(bf16[4,2,16,1024]{3,2,1,0:T(8,128)(2,1)S(1)} %collective-permute-done.3.refs_1_) | copy-start | bytes 786436
  81.0 0.7 copy-start.3

commit v7 on v6

--- a/solution.py
+++ b/solution.py
@@ -100,13 +100,16 @@
         )
 
 
-def left_kernel(blocks, frames, inputs, halo, hot, volts, places, names, panels, come):
+def left_kernel(listing, frames, inputs, halo, hot, volts, places, names, panels, blocks, come):
+    wanted = pltpu.make_async_copy(listing, blocks, come.at[TAPS + 1])
+    wanted.start()
     listed = pltpu.make_async_copy(inputs, names, come.at[TAPS])
     listed.start()
     order = list(range(1, TAPS)) + [0]
     arrive = [pltpu.make_async_copy(frames.at[t], volts.at[t], come.at[t]) for t in order]
     for copy in arrive[:-1]:
         copy.start()
+    wanted.wait()
     listed.wait()
     choose(0, blocks, names, hot, panels)
     for k in range(TAPS - 1):
@@ -122,9 +125,12 @@
     arrive[TAPS - 1].wait()
 
 
-def right_kernel(blocks, volts, inputs, halo, hot, names, panels, come):
+def right_kernel(listing, volts, inputs, halo, hot, names, panels, blocks, come):
+    wanted = pltpu.make_async_copy(listing, blocks, come.at[TAPS + 1])
+    wanted.start()
     listed = pltpu.make_async_copy(inputs, names, come.at[TAPS])
     listed.start()
+    wanted.wait()
     listed.wait()
     choose(1, blocks, names, hot, panels)
     for k in range(TAPS - 1):
@@ -154,24 +160,21 @@
         ]
     return pl.pallas_call(
         right_kernel if side else left_kernel,
-        grid_spec=pltpu.PrefetchScalarGridSpec(
-            num_scalar_prefetch=1,
-            grid=(1,),
-            in_specs=[INSIDE if side else ANYWHERE, ANYWHERE],
-            out_specs=out_specs,
-            scratch_shapes=[
-                pltpu.VMEM((width // PANEL, PANEL), jnp.int32),
-                pltpu.SMEM((TAPS * USED + width // PANEL,), jnp.int32),
-                pltpu.SemaphoreType.DMA((1 + TAPS,)),
-            ],
-        ),
+        in_specs=[ANYWHERE, INSIDE if side else ANYWHERE, ANYWHERE],
+        out_specs=out_specs,
+        scratch_shapes=[
+            pltpu.VMEM((width // PANEL, PANEL), jnp.int32),
+            pltpu.SMEM((TAPS * USED + width // PANEL,), jnp.int32),
+            pltpu.SMEM(block_list.shape, jnp.int32),
+            pltpu.SemaphoreType.DMA((2 + TAPS,)),
+        ],
         out_shape=out_shape,
         compiler_params=pltpu.CompilerParams(vmem_limit_bytes=VMEM // 2),
         cost_estimate=pl.CostEstimate(
             flops=depth * frame * width * WIDTH, bytes_accessed=10 << 20, transcendentals=0
         ),
         name="select",
-    )(block_list, *([frames] if side else pin(frames)), *pin(panel_map.reshape(-1, PANEL)))
+    )(*pin(block_list), *([frames] if side else pin(frames)), *pin(panel_map.reshape(-1, PANEL)))
 
 
 def first_kernel(count, volts, hot0, hot1, up, down, taps, table, orders, *refs):

time: 142 us -> 141 us (level)
  no operation moved by 1% of the time
where the time goes in v7:
time: 141 us
  waiting for transfers between devices  85.6 us (61%)
  Pallas kernels  36.6 us (26%)
  starting transfers between devices  16.4 us (12%)
  local copies, waits for them, and re-layouts  1.65 us (1%)
    all_to_all x1, waiting for transfers between devices, body(): rest = lax.all_to_all(rest, 'tm', split_axis=0, concat_axis=0, tiled=True)  40.1 us
    ppermute x3, waiting for transfers between devices, within_plane(): lax.ppermute(block, 'tm', [(i, i ^ q) for i in range(count)])  23.4 us
    ppermute x2, waiting for transfers between devices, shifted(): return lax.ppermute(block, axis, route)  22 us
    pallas_call x1, Pallas kernels, correlate(): pl.pallas_call(functools.partial(correlate_kernel, 1.0 / (groups * TAPS))...  14.3 us
    pallas_call x2, Pallas kernels, select(): pl.pallas_call(right_kernel if side else left_kernel, in_specs=[ANYWHERE,...  10.4 us
    all_to_all x1, starting transfers between devices, body(): rest = lax.all_to_all(rest, 'tm', split_axis=0, concat_axis=0, tiled=True)  7.44 us
    pallas_call x2, Pallas kernels, later_spectra(): pl.pallas_call(functools.partial(spectra_kernel, side), in_specs=[INSIDE]...  4.89 us
    pallas_call x1, Pallas kernels, first_spectra(): pl.pallas_call(functools.partial(first_kernel, planes), in_specs=[INSIDE]...  4.81 us
  transfers between devices with their start and end apart: 9, of which 5 were waited for; matrix products, arithmetic and copies ran while one was open for 0% of the time, Pallas kernels for 12%

profile of v7, /device:TPU:15, one launch (start us, length us, event | category | flops | bytes accessed | tf_op | source)
XLA Modules:
  0.0 140.5 jit_solution(4957057233178592352)
XLA Ops:
  0.0 6.0 %select.2 = (bf16[3,512,512]{2,1,0:T(8,128)(2,1)S(1)}, bf16[2048,512]{1,0:T(8,128)(2,1)S(1)}, bf16[4,512,2048]{2,1,0:T(8,128)(2,1)S(1)}, s32[2,16]{1,0:T(2,128)S(1)}) custom-call(s32[2,16]{1,0:T(2,128)} %bitcast.6, bf16[4,512,2048]{2,1,0:T(8,128)(2,1)} %bitcast.3, s32[16,128]{1,0:T(8,128)} %bitcast.4), custom_call_target="tpu_custom_call" | custom-call | flops 3221225472 | bytes 10485760 | tf_op jit(solution)/shard_map/select/pallas_call | solution.py:161
  6.0 3.7 %collective-permute-start.7 = (bf16[3,512,512]{2,1,0:T(8,128)(2,1)S(1)}, bf16[3,512,512]{2,1,0:T(8,128)(2,1)S(1)}, u32[]{:S(2)}, u32[]{:S(2)}) collective-permute-start(bf16[3,512,512]{2,1,0:T(8,128)(2,1)S(1)} %get-tuple-element.28.up.own), channel_id=1, source_target_pairs={{0,1},{1,2},{2,3},{3,4},{4,5},{5,6},{6,7},{7,8},{8,9},{9,10},{10,1... | collective-permute-start | bytes 4718600 | tf_op jit(solution)/shard_map/ppermute | solution.py:30
  9.7 4.4 %select.3 = (bf16[3,512,512]{2,1,0:T(8,128)(2,1)S(1)}, bf16[2048,512]{1,0:T(8,128)(2,1)S(1)}) custom-call(s32[2,16]{1,0:T(2,128)} %bitcast.7, bf16[4,512,2048]{2,1,0:T(8,128)(2,1)S(1)} %get-tuple-element.25.volts, s32[16,128]{1,0:T(8,128)} %bitcast.5), custom_call_target="tpu_custom_call" | custom-call | flops 3221225472 | bytes 10485760 | tf_op jit(solution)/shard_map/select/pallas_call | solution.py:161
  14.1 0.1 collective-permute-start.6
  14.2 4.8 %first_spectra.1 = (bf16[512,512]{1,0:T(8,128)(2,1)S(1)}, bf16[512,512]{1,0:T(8,128)(2,1)S(1)}, f32[4,512,128]{2,1,0:T(8,128)S(1)}, bf16[512,512]{1,0:T(8,128)(2...) custom-call(bf16[4,512,2048]{2,1,0:T(8,128)(2,1)S(1)} %get-tuple-ele, ...), custom_call_target="tpu_custom_call" | custom-call | flops 2684354560 | bytes 16777216 | tf_op jit(solution)/shard_map/first_spectra/pallas_call | solution.py:228
  19.0 0.2 collective-permute-start
  19.2 2.3 %collective-permute-start.1 = (bf16[4,2,16,1024]{3,2,1,0:T(8,128)(2,1)}, bf16[4,2,16,1024]{3,2,1,0:T(8,128)(2,1)}, u32[]{:S(2)}, u32[]{:S(2)}) collective-permute-start(bf16[4,2,16,1024]{3,2,1,0:T(8,128)(2,1)} %get-tuple-element.32), channel_id=1, source_target_pairs={{0,8},{1,9},{2,10},{3,11},{4,12},{5,13},{6,14},{7,15},{8,0},{9,1},... | collective-permute-start | bytes 786440 | tf_op jit(solution)/shard_map/ppermute | solution.py:294
  21.6 0.2 collective-permute-start.2
  21.7 11.1 %collective-permute-done.7.halo = bf16[3,512,512]{2,1,0:T(8,128)(2,1)S(1)} collective-permute-done((bf16[3,512,512]{2,1,0:T(8,128)(2,1)S(1)}, bf16[3,512,512]{2,1,0:T(8,128)(2,1)S(1)}, u32[]{:S(2)}, u32[]{:S(2)}) %collective-permute-start.7) | collective-permute-done | bytes 1572896 | tf_op jit(solution)/shard_map/ppermute | solution.py:30
  32.9 2.4 %later_spectra.2.refs_0_ = bf16[16,3,2,16,1024]{4,3,2,1,0:T(8,128)(2,1)} custom-call(bf16[3,512,512]{2,1,0:T(8,128)(2,1)S(1)} %collective-permute-done.7.halo, bf16[3,512,512]{2,1,0:T(8,128)(2,1)S(1)} %get-tuple-element.28.up.own, bf16[512,512]{1,0:T(8,128)(2,1)S(1)} %get-tuple-element.41.kept, f32[4,512,128]{2,1,0:T(8,128)S(1)} %get-tuple-element.39.taps, ...), custom_call_target="tpu_custom_call" | custom-call | flops 80530636800 | bytes 6291456 | tf_op jit(solution)/shard_map/later_spectra/pallas_call | solution.py:346
  35.3 10.9 %collective-permute-done.6.halo = bf16[3,512,512]{2,1,0:T(8,128)(2,1)S(1)} collective-permute-done((bf16[3,512,512]{2,1,0:T(8,128)(2,1)S(1)}, bf16[3,512,512]{2,1,0:T(8,128)(2,1)S(1)}, u32[]{:S(2)}, u32[]{:S(2)}) %collective-permute-start.6) | collective-permute-done | bytes 1572896 | tf_op jit(solution)/shard_map/ppermute | solution.py:30
  46.2 2.4 %later_spectra.3 = bf16[16,3,2,16,1024]{4,3,2,1,0:T(8,128)(2,1)} custom-call(bf16[3,512,512]{2,1,0:T(8,128)(2,1)S(1)} %collective-permute-done.6.halo, bf16[3,512,512]{2,1,0:T(8,128)(2,1)S(1)} %get-tuple-element.29.down.own, bf16[512,512]{1,0:T(8,128)(2,1)S(1)} %get-tuple-element.38.kept, ...), custom_call_target="tpu_custom_call", output_to_operand_aliasing={{}: (5, {})} | custom-call | flops 80530636800 | bytes 6291456 | tf_op jit(solution)/shard_map/later_spectra/pallas_call | solution.py:346
  48.7 7.4 %all-to-all-start = ((bf16[16,3,2,16,1024]{4,3,2,1,0:T(8,128)(2,1)}), bf16[16,3,2,16,1024]{4,3,2,1,0:T(8,128)(2,1)S(1)}, u32[]{:S(2)}, u32[]{:S(2)}) async-start(bf16[16,3,2,16,1024]{4,3,2,1,0:T(8,128)(2,1)} %later_spectra.3), calls=%async_computation | async-start | bytes 6291456 | tf_op jit(solution)/shard_map/all_to_all | solution.py:495
  56.1 0.0 collective-permute-done.refs_1_
  56.1 0.0 collective-permute-done.1.refs_2_
  56.1 0.0 collective-permute-done.2.refs_3_
  56.1 0.0 copy-start
  56.1 0.9 copy-done
  57.1 2.2 %regroup.1 = (bf16[4,2,16,1024]{3,2,1,0:T(8,128)(2,1)}, bf16[4,2,16,1024]{3,2,1,0:T(8,128)(2,1)}, bf16[4,2,16,1024]{3,2,1,0:T(8,128)(2,1)}, bf16[4,2,16,1024]{3,2,1,0:T(8,128)(2,1)}) custom-call(bf16[4,2,16,1024]{3,2,1,0:T(8,128)(2,1)S(1)} %copy-done, bf16[4,2,16,1024]{3,2,1,0:T(8,128)(2,1)} %collective-permute-done.refs_1_, ...), custom_call_target="tpu_custom_call" | custom-call | flops 137438953472 | bytes 2097152 | tf_op jit(solution)/shard_map/regroup/pallas_call | solution.py:275
  59.3 0.4 collective-permute-start.3
  59.7 2.0 %collective-permute-start.4 = (bf16[4,2,16,1024]{3,2,1,0:T(8,128)(2,1)}, bf16[4,2,16,1024]{3,2,1,0:T(8,128)(2,1)S(1)}, u32[]{:S(2)}, u32[]{:S(2)}) collective-permute-start(bf16[4,2,16,1024]{3,2,1,0:T(8,128)(2,1)} %get-tuple-element.36), channel_id=1, source_target_pairs={{0,2},{1,3},{2,0},{3,1},{4,6},{5,7},{6,4},{7,5},{8,10},{9,11},{10,... | collective-permute-start | bytes 786440 | tf_op jit(solution)/shard_map/ppermute | solution.py:304
  61.7 0.0 collective-permute-start.5
  61.8 0.0 collective-permute-done.3.refs_1_
  61.8 0.0 copy-start.1
  61.8 18.0 %collective-permute-done.4.refs_2_ = bf16[4,2,16,1024]{3,2,1,0:T(8,128)(2,1)S(1)} collective-permute-done((bf16[4,2,16,1024]{3,2,1,0:T(8,128)(2,1)}, bf16[4,2,16,1024]{3,2,1,0:T(8,128)(2,1)S(1)}, u32[]{:S(2)}, u32[]{:S(2)}) %collective-permute-start.4) | collective-permute-done | bytes 262176 | tf_op jit(solution)/shard_map/ppermute | solution.py:304
  79.8 0.0 copy-done.1
  79.8 0.0 copy-start.2
  79.8 0.7 copy-done.2
  80.5 5.4 %collective-permute-done.5.refs_3_ = bf16[4,2,16,1024]{3,2,1,0:T(8,128)(2,1)} collective-permute-done((bf16[4,2,16,1024]{3,2,1,0:T(8,128)(2,1)}, bf16[4,2,16,1024]{3,2,1,0:T(8,128)(2,1)}, u32[]{:S(2)}, u32[]{:S(2)}) %collective-permute-start.5) | collective-permute-done | bytes 262176 | tf_op jit(solution)/shard_map/ppermute | solution.py:304
  85.9 40.1 %all-to-all-done.refs_4_ = bf16[16,3,2,16,1024]{4,3,2,1,0:T(8,128)(2,1)S(1)} async-done(((bf16[16,3,2,16,1024]{4,3,2,1,0:T(8,128)(2,1)}), bf16[16,3,2,16,1024]{4,3,2,1,0:T(8,128)(2,1)S(1)}, u32[]{:S(2)}, u32[]{:S(2)}) %all-to-all-start) | async-done | bytes 3145760 | tf_op jit(solution)/shard_map/all_to_all | solution.py:495
  126.0 14.3 %correlate.1 = f32[16,2,16,128,128]{4,3,2,1,0:T(8,128)} custom-call(s32[2,16]{1,0:T(2,128)S(1)} %get-tuple-element.24.blocks, bf16[4,2,16,1024]{3,2,1,0:T(8,128)(2,1)} %get-tuple-element.34.refs_0_, bf16[4,2,16,1024]{3,2,1,0:T(8,128)(2,1)} %copy-done.1, bf16[4,2,16,1024]{3,2,1,0:T(8,128)(2,1)} %copy-done.2, ...), custom_call_target="tpu_custom_call" | custom-call | flops 2147483648 | bytes 37748736 | tf_op jit(solution)/shard_map/correlate/pallas_call | solution.py:442
Async XLA Ops:
  6.0 26.8 %collective-permute-start.7 = (bf16[3,512,512]{2,1,0:T(8,128)(2,1)S(1)}, bf16[3,512,512]{2,1,0:T(8,128)(2,1)S(1)}, u32[]{:S(2)}, u32[]{:S(2)}) collective-permute-start(bf16[3,512,512]{2,1,0:T(8,128)(2,1)S(1)} %get-tuple-element.28.up.own), channel_id=1, source_target_pairs={{0,1},{1,2},{2,3},{3,4},{4,5},{5,6},{6,7},{7,8},{8,9},{9,10},{10,1... | collective-permute-start | bytes 4718600 | tf_op jit(solution)/shard_map/ppermute | solution.py:30
  14.1 32.1 %collective-permute-start.6 = (bf16[3,512,512]{2,1,0:T(8,128)(2,1)S(1)}, bf16[3,512,512]{2,1,0:T(8,128)(2,1)S(1)}, u32[]{:S(2)}, u32[]{:S(2)}) collective-permute-start(bf16[3,512,512]{2,1,0:T(8,128)(2,1)S(1)} %get-tuple-element.29.down.own), channel_id=1, source_target_pairs={{0,15},{1,0},{2,1},{3,2},{4,3},{5,4},{6,5},{7,6},{8,7},{9,8},{10,9... | collective-permute-start | bytes 4718600 | tf_op jit(solution)/shard_map/ppermute | solution.py:30
  19.0 37.1 %collective-permute-start = (bf16[4,2,16,1024]{3,2,1,0:T(8,128)(2,1)}, bf16[4,2,16,1024]{3,2,1,0:T(8,128)(2,1)}, u32[]{:S(2)}, u32[]{:S(2)}) collective-permute-start(bf16[4,2,16,1024]{3,2,1,0:T(8,128)(2,1)} %get-tuple-element.31), channel_id=1, source_target_pairs={{0,4},{1,5},{2,6},{3,7},{4,0},{5,1},{6,2},{7,3},{8,12},{9,13},{10,... | collective-permute-start | bytes 786440 | tf_op jit(solution)/shard_map/ppermute | solution.py:294
  19.2 36.9 %collective-permute-start.1 = (bf16[4,2,16,1024]{3,2,1,0:T(8,128)(2,1)}, bf16[4,2,16,1024]{3,2,1,0:T(8,128)(2,1)}, u32[]{:S(2)}, u32[]{:S(2)}) collective-permute-start(bf16[4,2,16,1024]{3,2,1,0:T(8,128)(2,1)} %get-tuple-element.32), channel_id=1, source_target_pairs={{0,8},{1,9},{2,10},{3,11},{4,12},{5,13},{6,14},{7,15},{8,0},{9,1},... | collective-permute-start | bytes 786440 | tf_op jit(solution)/shard_map/ppermute | solution.py:294
  21.6 34.6 %collective-permute-start.2 = (bf16[4,2,16,1024]{3,2,1,0:T(8,128)(2,1)}, bf16[4,2,16,1024]{3,2,1,0:T(8,128)(2,1)}, u32[]{:S(2)}, u32[]{:S(2)}) collective-permute-start(bf16[4,2,16,1024]{3,2,1,0:T(8,128)(2,1)} %get-tuple-element.33), channel_id=1, source_target_pairs={{0,12},{1,13},{2,14},{3,15},{4,8},{5,9},{6,10},{7,11},{8,4},{9,5},... | collective-permute-start | bytes 786440 | tf_op jit(solution)/shard_map/ppermute | solution.py:294
  48.7 77.4 %all-to-all-start = ((bf16[16,3,2,16,1024]{4,3,2,1,0:T(8,128)(2,1)}), bf16[16,3,2,16,1024]{4,3,2,1,0:T(8,128)(2,1)S(1)}, u32[]{:S(2)}, u32[]{:S(2)}) async-start(bf16[16,3,2,16,1024]{4,3,2,1,0:T(8,128)(2,1)} %later_spectra.3), calls=%async_computation | async-start | bytes 6291456 | tf_op jit(solution)/shard_map/all_to_all | solution.py:495
  56.1 1.0 copy-start
  59.3 2.5 %collective-permute-start.3 = (bf16[4,2,16,1024]{3,2,1,0:T(8,128)(2,1)}, bf16[4,2,16,1024]{3,2,1,0:T(8,128)(2,1)S(1)}, u32[]{:S(2)}, u32[]{:S(2)}) collective-permute-start(bf16[4,2,16,1024]{3,2,1,0:T(8,128)(2,1)} %get-tuple-element.35), channel_id=1, source_target_pairs={{0,1},{1,0},{2,3},{3,2},{4,5},{5,4},{6,7},{7,6},{8,9},{9,8},{10,11... | collective-permute-start | bytes 786440 | tf_op jit(solution)/shard_map/ppermute | solution.py:304
  59.7 20.1 %collective-permute-start.4 = (bf16[4,2,16,1024]{3,2,1,0:T(8,128)(2,1)}, bf16[4,2,16,1024]{3,2,1,0:T(8,128)(2,1)S(1)}, u32[]{:S(2)}, u32[]{:S(2)}) collective-permute-start(bf16[4,2,16,1024]{3,2,1,0:T(8,128)(2,1)} %get-tuple-element.36), channel_id=1, source_target_pairs={{0,2},{1,3},{2,0},{3,1},{4,6},{5,7},{6,4},{7,5},{8,10},{9,11},{10,... | collective-permute-start | bytes 786440 | tf_op jit(solution)/shard_map/ppermute | solution.py:304
  61.7 24.2 %collective-permute-start.5 = (bf16[4,2,16,1024]{3,2,1,0:T(8,128)(2,1)}, bf16[4,2,16,1024]{3,2,1,0:T(8,128)(2,1)}, u32[]{:S(2)}, u32[]{:S(2)}) collective-permute-start(bf16[4,2,16,1024]{3,2,1,0:T(8,128)(2,1)} %get-tuple-element.37), channel_id=1, source_target_pairs={{0,3},{1,2},{2,1},{3,0},{4,7},{5,6},{6,5},{7,4},{8,11},{9,10},{10,... | collective-permute-start | bytes 786440 | tf_op jit(solution)/shard_map/ppermute | solution.py:304
  61.8 18.0 %copy-start.1 = (bf16[4,2,16,1024]{3,2,1,0:T(8,128)(2,1)}, bf16[4,2,16,1024]{3,2,1,0:T(8,128)(2,1)S(1)}, u32[]{:S(2)}) copy-start(bf16[4,2,16,1024]{3,2,1,0:T(8,128)(2,1)S(1)} %collective-permute-done.3.refs_1_) | copy-start | bytes 786436
  79.8 0.7 copy-start.2

commit v8 on v7

--- a/solution.py
+++ b/solution.py
@@ -409,13 +409,13 @@
                         256 + at : 256 + at + width
                     ]
 
-        @pl.loop(0, per)
+        @pl.loop(0, per, unroll=2)
         def _(f):
-            across[...] = plain[f].T
+            across[f % 2] = plain[f].T
             for b in range(blocks.shape[1]):
                 a, w = (pl.multiple_of(blocks[i, b], PANEL) for i in range(2))
                 product = jnp.dot(
-                    across[pl.ds(a, PANEL), :],
+                    across[f % 2, pl.ds(a, PANEL), :],
                     jnp.concatenate(
                         [plain[f, :, pl.ds(w, PANEL)], turned[f, :, pl.ds(w, PANEL)]], axis=1
                     ),
@@ -450,7 +450,7 @@
             scratch_shapes=[
                 pltpu.VMEM((per, keys, WIDTH), jnp.bfloat16),
                 pltpu.VMEM((per, keys, WIDTH), jnp.bfloat16),
-                pltpu.VMEM((WIDTH, keys), jnp.bfloat16),
+                pltpu.VMEM((2, WIDTH, keys), jnp.bfloat16),
                 pltpu.VMEM((parts, per, blocks, 2, PANEL, PANEL), jnp.float32),
                 pltpu.VMEM((PLANE, *first[0].shape), jnp.bfloat16),
                 pltpu.SemaphoreType.DMA((parts, per)),

time: 141 us -> 140 us (level)
  no operation moved by 1% of the time
where the time goes in v8:
time: 140 us
  waiting for transfers between devices  85.6 us (61%)
  Pallas kernels  36.2 us (26%)
  starting transfers between devices  16.4 us (12%)
  local copies, waits for them, and re-layouts  1.65 us (1%)
    all_to_all x1, waiting for transfers between devices, body(): rest = lax.all_to_all(rest, 'tm', split_axis=0, concat_axis=0, tiled=True)  40.1 us
    ppermute x3, waiting for transfers between devices, within_plane(): lax.ppermute(block, 'tm', [(i, i ^ q) for i in range(count)])  23.4 us
    ppermute x2, waiting for transfers between devices, shifted(): return lax.ppermute(block, axis, route)  22 us
    pallas_call x1, Pallas kernels, correlate(): pl.pallas_call(functools.partial(correlate_kernel, 1.0 / (groups * TAPS))...  13.9 us
    pallas_call x2, Pallas kernels, select(): pl.pallas_call(right_kernel if side else left_kernel, in_specs=[ANYWHERE,...  10.4 us
    all_to_all x1, starting transfers between devices, body(): rest = lax.all_to_all(rest, 'tm', split_axis=0, concat_axis=0, tiled=True)  7.44 us
    pallas_call x2, Pallas kernels, later_spectra(): pl.pallas_call(functools.partial(spectra_kernel, side), in_specs=[INSIDE]...  4.89 us
    pallas_call x1, Pallas kernels, first_spectra(): pl.pallas_call(functools.partial(first_kernel, planes), in_specs=[INSIDE]...  4.81 us
  transfers between devices with their start and end apart: 9, of which 5 were waited for; matrix products, arithmetic and copies ran while one was open for 0% of the time, Pallas kernels for 12%

profile of v8, /device:TPU:15, one launch (start us, length us, event | category | flops | bytes accessed | tf_op | source)
XLA Modules:
  0.0 140.1 jit_solution(4265252463148544226)
XLA Ops:
  0.0 6.0 %select.2 = (bf16[3,512,512]{2,1,0:T(8,128)(2,1)S(1)}, bf16[2048,512]{1,0:T(8,128)(2,1)S(1)}, bf16[4,512,2048]{2,1,0:T(8,128)(2,1)S(1)}, s32[2,16]{1,0:T(2,128)S(1)}) custom-call(s32[2,16]{1,0:T(2,128)} %bitcast.6, bf16[4,512,2048]{2,1,0:T(8,128)(2,1)} %bitcast.3, s32[16,128]{1,0:T(8,128)} %bitcast.4), custom_call_target="tpu_custom_call" | custom-call | flops 3221225472 | bytes 10485760 | tf_op jit(solution)/shard_map/select/pallas_call | solution.py:161
  6.0 3.7 %collective-permute-start.7 = (bf16[3,512,512]{2,1,0:T(8,128)(2,1)S(1)}, bf16[3,512,512]{2,1,0:T(8,128)(2,1)S(1)}, u32[]{:S(2)}, u32[]{:S(2)}) collective-permute-start(bf16[3,512,512]{2,1,0:T(8,128)(2,1)S(1)} %get-tuple-element.28.up.own), channel_id=1, source_target_pairs={{0,1},{1,2},{2,3},{3,4},{4,5},{5,6},{6,7},{7,8},{8,9},{9,10},{10,1... | collective-permute-start | bytes 4718600 | tf_op jit(solution)/shard_map/ppermute | solution.py:30
  9.7 4.4 %select.3 = (bf16[3,512,512]{2,1,0:T(8,128)(2,1)S(1)}, bf16[2048,512]{1,0:T(8,128)(2,1)S(1)}) custom-call(s32[2,16]{1,0:T(2,128)} %bitcast.7, bf16[4,512,2048]{2,1,0:T(8,128)(2,1)S(1)} %get-tuple-element.25.volts, s32[16,128]{1,0:T(8,128)} %bitcast.5), custom_call_target="tpu_custom_call" | custom-call | flops 3221225472 | bytes 10485760 | tf_op jit(solution)/shard_map/select/pallas_call | solution.py:161
  14.1 0.1 collective-permute-start.6
  14.2 4.8 %first_spectra.1 = (bf16[512,512]{1,0:T(8,128)(2,1)S(1)}, bf16[512,512]{1,0:T(8,128)(2,1)S(1)}, f32[4,512,128]{2,1,0:T(8,128)S(1)}, bf16[512,512]{1,0:T(8,128)(2...) custom-call(bf16[4,512,2048]{2,1,0:T(8,128)(2,1)S(1)} %get-tuple-ele, ...), custom_call_target="tpu_custom_call" | custom-call | flops 2684354560 | bytes 16777216 | tf_op jit(solution)/shard_map/first_spectra/pallas_call | solution.py:228
  19.0 0.2 collective-permute-start
  19.2 2.3 %collective-permute-start.1 = (bf16[4,2,16,1024]{3,2,1,0:T(8,128)(2,1)}, bf16[4,2,16,1024]{3,2,1,0:T(8,128)(2,1)}, u32[]{:S(2)}, u32[]{:S(2)}) collective-permute-start(bf16[4,2,16,1024]{3,2,1,0:T(8,128)(2,1)} %get-tuple-element.32), channel_id=1, source_target_pairs={{0,8},{1,9},{2,10},{3,11},{4,12},{5,13},{6,14},{7,15},{8,0},{9,1},... | collective-permute-start | bytes 786440 | tf_op jit(solution)/shard_map/ppermute | solution.py:294
  21.6 0.2 collective-permute-start.2
  21.7 11.1 %collective-permute-done.7.halo = bf16[3,512,512]{2,1,0:T(8,128)(2,1)S(1)} collective-permute-done((bf16[3,512,512]{2,1,0:T(8,128)(2,1)S(1)}, bf16[3,512,512]{2,1,0:T(8,128)(2,1)S(1)}, u32[]{:S(2)}, u32[]{:S(2)}) %collective-permute-start.7) | collective-permute-done | bytes 1572896 | tf_op jit(solution)/shard_map/ppermute | solution.py:30
  32.9 2.4 %later_spectra.2.refs_0_ = bf16[16,3,2,16,1024]{4,3,2,1,0:T(8,128)(2,1)} custom-call(bf16[3,512,512]{2,1,0:T(8,128)(2,1)S(1)} %collective-permute-done.7.halo, bf16[3,512,512]{2,1,0:T(8,128)(2,1)S(1)} %get-tuple-element.28.up.own, bf16[512,512]{1,0:T(8,128)(2,1)S(1)} %get-tuple-element.41.kept, f32[4,512,128]{2,1,0:T(8,128)S(1)} %get-tuple-element.39.taps, ...), custom_call_target="tpu_custom_call" | custom-call | flops 80530636800 | bytes 6291456 | tf_op jit(solution)/shard_map/later_spectra/pallas_call | solution.py:346
  35.3 10.9 %collective-permute-done.6.halo = bf16[3,512,512]{2,1,0:T(8,128)(2,1)S(1)} collective-permute-done((bf16[3,512,512]{2,1,0:T(8,128)(2,1)S(1)}, bf16[3,512,512]{2,1,0:T(8,128)(2,1)S(1)}, u32[]{:S(2)}, u32[]{:S(2)}) %collective-permute-start.6) | collective-permute-done | bytes 1572896 | tf_op jit(solution)/shard_map/ppermute | solution.py:30
  46.2 2.4 %later_spectra.3 = bf16[16,3,2,16,1024]{4,3,2,1,0:T(8,128)(2,1)} custom-call(bf16[3,512,512]{2,1,0:T(8,128)(2,1)S(1)} %collective-permute-done.6.halo, bf16[3,512,512]{2,1,0:T(8,128)(2,1)S(1)} %get-tuple-element.29.down.own, bf16[512,512]{1,0:T(8,128)(2,1)S(1)} %get-tuple-element.38.kept, ...), custom_call_target="tpu_custom_call", output_to_operand_aliasing={{}: (5, {})} | custom-call | flops 80530636800 | bytes 6291456 | tf_op jit(solution)/shard_map/later_spectra/pallas_call | solution.py:346
  48.7 7.4 %all-to-all-start = ((bf16[16,3,2,16,1024]{4,3,2,1,0:T(8,128)(2,1)}), bf16[16,3,2,16,1024]{4,3,2,1,0:T(8,128)(2,1)S(1)}, u32[]{:S(2)}, u32[]{:S(2)}) async-start(bf16[16,3,2,16,1024]{4,3,2,1,0:T(8,128)(2,1)} %later_spectra.3), calls=%async_computation | async-start | bytes 6291456 | tf_op jit(solution)/shard_map/all_to_all | solution.py:495
  56.1 0.0 collective-permute-done.refs_1_
  56.1 0.0 collective-permute-done.1.refs_2_
  56.1 0.0 collective-permute-done.2.refs_3_
  56.1 0.0 copy-start
  56.1 0.9 copy-done
  57.1 2.2 %regroup.1 = (bf16[4,2,16,1024]{3,2,1,0:T(8,128)(2,1)}, bf16[4,2,16,1024]{3,2,1,0:T(8,128)(2,1)}, bf16[4,2,16,1024]{3,2,1,0:T(8,128)(2,1)}, bf16[4,2,16,1024]{3,2,1,0:T(8,128)(2,1)}) custom-call(bf16[4,2,16,1024]{3,2,1,0:T(8,128)(2,1)S(1)} %copy-done, bf16[4,2,16,1024]{3,2,1,0:T(8,128)(2,1)} %collective-permute-done.refs_1_, ...), custom_call_target="tpu_custom_call" | custom-call | flops 137438953472 | bytes 2097152 | tf_op jit(solution)/shard_map/regroup/pallas_call | solution.py:275
  59.3 0.4 collective-permute-start.3
  59.7 2.0 %collective-permute-start.4 = (bf16[4,2,16,1024]{3,2,1,0:T(8,128)(2,1)}, bf16[4,2,16,1024]{3,2,1,0:T(8,128)(2,1)S(1)}, u32[]{:S(2)}, u32[]{:S(2)}) collective-permute-start(bf16[4,2,16,1024]{3,2,1,0:T(8,128)(2,1)} %get-tuple-element.36), channel_id=1, source_target_pairs={{0,2},{1,3},{2,0},{3,1},{4,6},{5,7},{6,4},{7,5},{8,10},{9,11},{10,... | collective-permute-start | bytes 786440 | tf_op jit(solution)/shard_map/ppermute | solution.py:304
  61.7 0.0 collective-permute-start.5
  61.8 0.0 collective-permute-done.3.refs_1_
  61.8 0.0 copy-start.1
  61.8 18.0 %collective-permute-done.4.refs_2_ = bf16[4,2,16,1024]{3,2,1,0:T(8,128)(2,1)S(1)} collective-permute-done((bf16[4,2,16,1024]{3,2,1,0:T(8,128)(2,1)}, bf16[4,2,16,1024]{3,2,1,0:T(8,128)(2,1)S(1)}, u32[]{:S(2)}, u32[]{:S(2)}) %collective-permute-start.4) | collective-permute-done | bytes 262176 | tf_op jit(solution)/shard_map/ppermute | solution.py:304
  79.8 0.0 copy-done.1
  79.8 0.0 copy-start.2
  79.8 0.7 copy-done.2
  80.5 5.4 %collective-permute-done.5.refs_3_ = bf16[4,2,16,1024]{3,2,1,0:T(8,128)(2,1)} collective-permute-done((bf16[4,2,16,1024]{3,2,1,0:T(8,128)(2,1)}, bf16[4,2,16,1024]{3,2,1,0:T(8,128)(2,1)}, u32[]{:S(2)}, u32[]{:S(2)}) %collective-permute-start.5) | collective-permute-done | bytes 262176 | tf_op jit(solution)/shard_map/ppermute | solution.py:304
  85.9 40.1 %all-to-all-done.refs_4_ = bf16[16,3,2,16,1024]{4,3,2,1,0:T(8,128)(2,1)S(1)} async-done(((bf16[16,3,2,16,1024]{4,3,2,1,0:T(8,128)(2,1)}), bf16[16,3,2,16,1024]{4,3,2,1,0:T(8,128)(2,1)S(1)}, u32[]{:S(2)}, u32[]{:S(2)}) %all-to-all-start) | async-done | bytes 3145760 | tf_op jit(solution)/shard_map/all_to_all | solution.py:495
  126.0 13.9 %correlate.1 = f32[16,2,16,128,128]{4,3,2,1,0:T(8,128)} custom-call(s32[2,16]{1,0:T(2,128)S(1)} %get-tuple-element.24.blocks, bf16[4,2,16,1024]{3,2,1,0:T(8,128)(2,1)} %get-tuple-element.34.refs_0_, bf16[4,2,16,1024]{3,2,1,0:T(8,128)(2,1)} %copy-done.1, bf16[4,2,16,1024]{3,2,1,0:T(8,128)(2,1)} %copy-done.2, ...), custom_call_target="tpu_custom_call" | custom-call | flops 2147483648 | bytes 37748736 | tf_op jit(solution)/shard_map/correlate/pallas_call | solution.py:442
Async XLA Ops:
  6.0 26.8 %collective-permute-start.7 = (bf16[3,512,512]{2,1,0:T(8,128)(2,1)S(1)}, bf16[3,512,512]{2,1,0:T(8,128)(2,1)S(1)}, u32[]{:S(2)}, u32[]{:S(2)}) collective-permute-start(bf16[3,512,512]{2,1,0:T(8,128)(2,1)S(1)} %get-tuple-element.28.up.own), channel_id=1, source_target_pairs={{0,1},{1,2},{2,3},{3,4},{4,5},{5,6},{6,7},{7,8},{8,9},{9,10},{10,1... | collective-permute-start | bytes 4718600 | tf_op jit(solution)/shard_map/ppermute | solution.py:30
  14.1 32.1 %collective-permute-start.6 = (bf16[3,512,512]{2,1,0:T(8,128)(2,1)S(1)}, bf16[3,512,512]{2,1,0:T(8,128)(2,1)S(1)}, u32[]{:S(2)}, u32[]{:S(2)}) collective-permute-start(bf16[3,512,512]{2,1,0:T(8,128)(2,1)S(1)} %get-tuple-element.29.down.own), channel_id=1, source_target_pairs={{0,15},{1,0},{2,1},{3,2},{4,3},{5,4},{6,5},{7,6},{8,7},{9,8},{10,9... | collective-permute-start | bytes 4718600 | tf_op jit(solution)/shard_map/ppermute | solution.py:30
  19.0 37.1 %collective-permute-start = (bf16[4,2,16,1024]{3,2,1,0:T(8,128)(2,1)}, bf16[4,2,16,1024]{3,2,1,0:T(8,128)(2,1)}, u32[]{:S(2)}, u32[]{:S(2)}) collective-permute-start(bf16[4,2,16,1024]{3,2,1,0:T(8,128)(2,1)} %get-tuple-element.31), channel_id=1, source_target_pairs={{0,4},{1,5},{2,6},{3,7},{4,0},{5,1},{6,2},{7,3},{8,12},{9,13},{10,... | collective-permute-start | bytes 786440 | tf_op jit(solution)/shard_map/ppermute | solution.py:294
  19.2 36.9 %collective-permute-start.1 = (bf16[4,2,16,1024]{3,2,1,0:T(8,128)(2,1)}, bf16[4,2,16,1024]{3,2,1,0:T(8,128)(2,1)}, u32[]{:S(2)}, u32[]{:S(2)}) collective-permute-start(bf16[4,2,16,1024]{3,2,1,0:T(8,128)(2,1)} %get-tuple-element.32), channel_id=1, source_target_pairs={{0,8},{1,9},{2,10},{3,11},{4,12},{5,13},{6,14},{7,15},{8,0},{9,1},... | collective-permute-start | bytes 786440 | tf_op jit(solution)/shard_map/ppermute | solution.py:294
  21.6 34.6 %collective-permute-start.2 = (bf16[4,2,16,1024]{3,2,1,0:T(8,128)(2,1)}, bf16[4,2,16,1024]{3,2,1,0:T(8,128)(2,1)}, u32[]{:S(2)}, u32[]{:S(2)}) collective-permute-start(bf16[4,2,16,1024]{3,2,1,0:T(8,128)(2,1)} %get-tuple-element.33), channel_id=1, source_target_pairs={{0,12},{1,13},{2,14},{3,15},{4,8},{5,9},{6,10},{7,11},{8,4},{9,5},... | collective-permute-start | bytes 786440 | tf_op jit(solution)/shard_map/ppermute | solution.py:294
  48.7 77.4 %all-to-all-start = ((bf16[16,3,2,16,1024]{4,3,2,1,0:T(8,128)(2,1)}), bf16[16,3,2,16,1024]{4,3,2,1,0:T(8,128)(2,1)S(1)}, u32[]{:S(2)}, u32[]{:S(2)}) async-start(bf16[16,3,2,16,1024]{4,3,2,1,0:T(8,128)(2,1)} %later_spectra.3), calls=%async_computation | async-start | bytes 6291456 | tf_op jit(solution)/shard_map/all_to_all | solution.py:495
  56.1 1.0 copy-start
  59.3 2.5 %collective-permute-start.3 = (bf16[4,2,16,1024]{3,2,1,0:T(8,128)(2,1)}, bf16[4,2,16,1024]{3,2,1,0:T(8,128)(2,1)S(1)}, u32[]{:S(2)}, u32[]{:S(2)}) collective-permute-start(bf16[4,2,16,1024]{3,2,1,0:T(8,128)(2,1)} %get-tuple-element.35), channel_id=1, source_target_pairs={{0,1},{1,0},{2,3},{3,2},{4,5},{5,4},{6,7},{7,6},{8,9},{9,8},{10,11... | collective-permute-start | bytes 786440 | tf_op jit(solution)/shard_map/ppermute | solution.py:304
  59.7 20.1 %collective-permute-start.4 = (bf16[4,2,16,1024]{3,2,1,0:T(8,128)(2,1)}, bf16[4,2,16,1024]{3,2,1,0:T(8,128)(2,1)S(1)}, u32[]{:S(2)}, u32[]{:S(2)}) collective-permute-start(bf16[4,2,16,1024]{3,2,1,0:T(8,128)(2,1)} %get-tuple-element.36), channel_id=1, source_target_pairs={{0,2},{1,3},{2,0},{3,1},{4,6},{5,7},{6,4},{7,5},{8,10},{9,11},{10,... | collective-permute-start | bytes 786440 | tf_op jit(solution)/shard_map/ppermute | solution.py:304
  61.7 24.2 %collective-permute-start.5 = (bf16[4,2,16,1024]{3,2,1,0:T(8,128)(2,1)}, bf16[4,2,16,1024]{3,2,1,0:T(8,128)(2,1)}, u32[]{:S(2)}, u32[]{:S(2)}) collective-permute-start(bf16[4,2,16,1024]{3,2,1,0:T(8,128)(2,1)} %get-tuple-element.37), channel_id=1, source_target_pairs={{0,3},{1,2},{2,1},{3,0},{4,7},{5,6},{6,5},{7,4},{8,11},{9,10},{10,... | collective-permute-start | bytes 786440 | tf_op jit(solution)/shard_map/ppermute | solution.py:304
  61.8 18.0 %copy-start.1 = (bf16[4,2,16,1024]{3,2,1,0:T(8,128)(2,1)}, bf16[4,2,16,1024]{3,2,1,0:T(8,128)(2,1)S(1)}, u32[]{:S(2)}) copy-start(bf16[4,2,16,1024]{3,2,1,0:T(8,128)(2,1)S(1)} %collective-permute-done.3.refs_1_) | copy-start | bytes 786436
  79.8 0.7 copy-start.2

commit v9 on v8

--- a/solution.py
+++ b/solution.py
@@ -409,7 +409,7 @@
                         256 + at : 256 + at + width
                     ]
 
-        @pl.loop(0, per, unroll=2)
+        @pl.loop(0, per, unroll=4)
         def _(f):
             across[f % 2] = plain[f].T
             for b in range(blocks.shape[1]):

time: 140 us -> 140 us (level)
  no operation moved by 1% of the time
where the time goes in v9:
time: 140 us
  waiting for transfers between devices  85.6 us (61%)
  Pallas kernels  36.2 us (26%)
  starting transfers between devices  16.4 us (12%)
  local copies, waits for them, and re-layouts  1.65 us (1%)
    all_to_all x1, waiting for transfers between devices, body(): rest = lax.all_to_all(rest, 'tm', split_axis=0, concat_axis=0, tiled=True)  40.1 us
    ppermute x3, waiting for transfers between devices, within_plane(): lax.ppermute(block, 'tm', [(i, i ^ q) for i in range(count)])  23.4 us
    ppermute x2, waiting for transfers between devices, shifted(): return lax.ppermute(block, axis, route)  22 us
    pallas_call x1, Pallas kernels, correlate(): pl.pallas_call(functools.partial(correlate_kernel, 1.0 / (groups * TAPS))...  13.9 us
    pallas_call x2, Pallas kernels, select(): pl.pallas_call(right_kernel if side else left_kernel, in_specs=[ANYWHERE,...  10.4 us
    all_to_all x1, starting transfers between devices, body(): rest = lax.all_to_all(rest, 'tm', split_axis=0, concat_axis=0, tiled=True)  7.44 us
    pallas_call x2, Pallas kernels, later_spectra(): pl.pallas_call(functools.partial(spectra_kernel, side), in_specs=[INSIDE]...  4.89 us
    pallas_call x1, Pallas kernels, first_spectra(): pl.pallas_call(functools.partial(first_kernel, planes), in_specs=[INSIDE]...  4.81 us
  transfers between devices with their start and end apart: 9, of which 5 were waited for; matrix products, arithmetic and copies ran while one was open for 0% of the time, Pallas kernels for 12%

profile of v9, /device:TPU:15, one launch (start us, length us, event | category | flops | bytes accessed | tf_op | source)
XLA Modules:
  0.0 140.1 jit_solution(8012524314974466389)
XLA Ops:
  0.0 6.0 %select.2 = (bf16[3,512,512]{2,1,0:T(8,128)(2,1)S(1)}, bf16[2048,512]{1,0:T(8,128)(2,1)S(1)}, bf16[4,512,2048]{2,1,0:T(8,128)(2,1)S(1)}, s32[2,16]{1,0:T(2,128)S(1)}) custom-call(s32[2,16]{1,0:T(2,128)} %bitcast.6, bf16[4,512,2048]{2,1,0:T(8,128)(2,1)} %bitcast.3, s32[16,128]{1,0:T(8,128)} %bitcast.4), custom_call_target="tpu_custom_call" | custom-call | flops 3221225472 | bytes 10485760 | tf_op jit(solution)/shard_map/select/pallas_call | solution.py:161
  6.0 3.7 %collective-permute-start.7 = (bf16[3,512,512]{2,1,0:T(8,128)(2,1)S(1)}, bf16[3,512,512]{2,1,0:T(8,128)(2,1)S(1)}, u32[]{:S(2)}, u32[]{:S(2)}) collective-permute-start(bf16[3,512,512]{2,1,0:T(8,128)(2,1)S(1)} %get-tuple-element.28.up.own), channel_id=1, source_target_pairs={{0,1},{1,2},{2,3},{3,4},{4,5},{5,6},{6,7},{7,8},{8,9},{9,10},{10,1... | collective-permute-start | bytes 4718600 | tf_op jit(solution)/shard_map/ppermute | solution.py:30
  9.7 4.4 %select.3 = (bf16[3,512,512]{2,1,0:T(8,128)(2,1)S(1)}, bf16[2048,512]{1,0:T(8,128)(2,1)S(1)}) custom-call(s32[2,16]{1,0:T(2,128)} %bitcast.7, bf16[4,512,2048]{2,1,0:T(8,128)(2,1)S(1)} %get-tuple-element.25.volts, s32[16,128]{1,0:T(8,128)} %bitcast.5), custom_call_target="tpu_custom_call" | custom-call | flops 3221225472 | bytes 10485760 | tf_op jit(solution)/shard_map/select/pallas_call | solution.py:161
  14.1 0.1 collective-permute-start.6
  14.2 4.8 %first_spectra.1 = (bf16[512,512]{1,0:T(8,128)(2,1)S(1)}, bf16[512,512]{1,0:T(8,128)(2,1)S(1)}, f32[4,512,128]{2,1,0:T(8,128)S(1)}, bf16[512,512]{1,0:T(8,128)(2...) custom-call(bf16[4,512,2048]{2,1,0:T(8,128)(2,1)S(1)} %get-tuple-ele, ...), custom_call_target="tpu_custom_call" | custom-call | flops 2684354560 | bytes 16777216 | tf_op jit(solution)/shard_map/first_spectra/pallas_call | solution.py:228
  19.0 0.2 collective-permute-start
  19.2 2.3 %collective-permute-start.1 = (bf16[4,2,16,1024]{3,2,1,0:T(8,128)(2,1)}, bf16[4,2,16,1024]{3,2,1,0:T(8,128)(2,1)}, u32[]{:S(2)}, u32[]{:S(2)}) collective-permute-start(bf16[4,2,16,1024]{3,2,1,0:T(8,128)(2,1)} %get-tuple-element.32), channel_id=1, source_target_pairs={{0,8},{1,9},{2,10},{3,11},{4,12},{5,13},{6,14},{7,15},{8,0},{9,1},... | collective-permute-start | bytes 786440 | tf_op jit(solution)/shard_map/ppermute | solution.py:294
  21.6 0.2 collective-permute-start.2
  21.7 11.1 %collective-permute-done.7.halo = bf16[3,512,512]{2,1,0:T(8,128)(2,1)S(1)} collective-permute-done((bf16[3,512,512]{2,1,0:T(8,128)(2,1)S(1)}, bf16[3,512,512]{2,1,0:T(8,128)(2,1)S(1)}, u32[]{:S(2)}, u32[]{:S(2)}) %collective-permute-start.7) | collective-permute-done | bytes 1572896 | tf_op jit(solution)/shard_map/ppermute | solution.py:30
  32.9 2.4 %later_spectra.2.refs_0_ = bf16[16,3,2,16,1024]{4,3,2,1,0:T(8,128)(2,1)} custom-call(bf16[3,512,512]{2,1,0:T(8,128)(2,1)S(1)} %collective-permute-done.7.halo, bf16[3,512,512]{2,1,0:T(8,128)(2,1)S(1)} %get-tuple-element.28.up.own, bf16[512,512]{1,0:T(8,128)(2,1)S(1)} %get-tuple-element.41.kept, f32[4,512,128]{2,1,0:T(8,128)S(1)} %get-tuple-element.39.taps, ...), custom_call_target="tpu_custom_call" | custom-call | flops 80530636800 | bytes 6291456 | tf_op jit(solution)/shard_map/later_spectra/pallas_call | solution.py:346
  35.3 10.9 %collective-permute-done.6.halo = bf16[3,512,512]{2,1,0:T(8,128)(2,1)S(1)} collective-permute-done((bf16[3,512,512]{2,1,0:T(8,128)(2,1)S(1)}, bf16[3,512,512]{2,1,0:T(8,128)(2,1)S(1)}, u32[]{:S(2)}, u32[]{:S(2)}) %collective-permute-start.6) | collective-permute-done | bytes 1572896 | tf_op jit(solution)/shard_map/ppermute | solution.py:30
  46.2 2.4 %later_spectra.3 = bf16[16,3,2,16,1024]{4,3,2,1,0:T(8,128)(2,1)} custom-call(bf16[3,512,512]{2,1,0:T(8,128)(2,1)S(1)} %collective-permute-done.6.halo, bf16[3,512,512]{2,1,0:T(8,128)(2,1)S(1)} %get-tuple-element.29.down.own, bf16[512,512]{1,0:T(8,128)(2,1)S(1)} %get-tuple-element.38.kept, ...), custom_call_target="tpu_custom_call", output_to_operand_aliasing={{}: (5, {})} | custom-call | flops 80530636800 | bytes 6291456 | tf_op jit(solution)/shard_map/later_spectra/pallas_call | solution.py:346
  48.7 7.4 %all-to-all-start = ((bf16[16,3,2,16,1024]{4,3,2,1,0:T(8,128)(2,1)}), bf16[16,3,2,16,1024]{4,3,2,1,0:T(8,128)(2,1)S(1)}, u32[]{:S(2)}, u32[]{:S(2)}) async-start(bf16[16,3,2,16,1024]{4,3,2,1,0:T(8,128)(2,1)} %later_spectra.3), calls=%async_computation | async-start | bytes 6291456 | tf_op jit(solution)/shard_map/all_to_all | solution.py:495
  56.1 0.0 collective-permute-done.refs_1_
  56.1 0.0 collective-permute-done.1.refs_2_
  56.1 0.0 collective-permute-done.2.refs_3_
  56.1 0.0 copy-start
  56.1 0.9 copy-done
  57.1 2.2 %regroup.1 = (bf16[4,2,16,1024]{3,2,1,0:T(8,128)(2,1)}, bf16[4,2,16,1024]{3,2,1,0:T(8,128)(2,1)}, bf16[4,2,16,1024]{3,2,1,0:T(8,128)(2,1)}, bf16[4,2,16,1024]{3,2,1,0:T(8,128)(2,1)}) custom-call(bf16[4,2,16,1024]{3,2,1,0:T(8,128)(2,1)S(1)} %copy-done, bf16[4,2,16,1024]{3,2,1,0:T(8,128)(2,1)} %collective-permute-done.refs_1_, ...), custom_call_target="tpu_custom_call" | custom-call | flops 137438953472 | bytes 2097152 | tf_op jit(solution)/shard_map/regroup/pallas_call | solution.py:275
  59.3 0.4 collective-permute-start.3
  59.7 2.0 %collective-permute-start.4 = (bf16[4,2,16,1024]{3,2,1,0:T(8,128)(2,1)}, bf16[4,2,16,1024]{3,2,1,0:T(8,128)(2,1)S(1)}, u32[]{:S(2)}, u32[]{:S(2)}) collective-permute-start(bf16[4,2,16,1024]{3,2,1,0:T(8,128)(2,1)} %get-tuple-element.36), channel_id=1, source_target_pairs={{0,2},{1,3},{2,0},{3,1},{4,6},{5,7},{6,4},{7,5},{8,10},{9,11},{10,... | collective-permute-start | bytes 786440 | tf_op jit(solution)/shard_map/ppermute | solution.py:304
  61.7 0.0 collective-permute-start.5
  61.8 0.0 collective-permute-done.3.refs_1_
  61.8 0.0 copy-start.1
  61.8 18.0 %collective-permute-done.4.refs_2_ = bf16[4,2,16,1024]{3,2,1,0:T(8,128)(2,1)S(1)} collective-permute-done((bf16[4,2,16,1024]{3,2,1,0:T(8,128)(2,1)}, bf16[4,2,16,1024]{3,2,1,0:T(8,128)(2,1)S(1)}, u32[]{:S(2)}, u32[]{:S(2)}) %collective-permute-start.4) | collective-permute-done | bytes 262176 | tf_op jit(solution)/shard_map/ppermute | solution.py:304
  79.8 0.0 copy-done.1
  79.8 0.0 copy-start.2
  79.8 0.7 copy-done.2
  80.5 5.4 %collective-permute-done.5.refs_3_ = bf16[4,2,16,1024]{3,2,1,0:T(8,128)(2,1)} collective-permute-done((bf16[4,2,16,1024]{3,2,1,0:T(8,128)(2,1)}, bf16[4,2,16,1024]{3,2,1,0:T(8,128)(2,1)}, u32[]{:S(2)}, u32[]{:S(2)}) %collective-permute-start.5) | collective-permute-done | bytes 262176 | tf_op jit(solution)/shard_map/ppermute | solution.py:304
  85.9 40.1 %all-to-all-done.refs_4_ = bf16[16,3,2,16,1024]{4,3,2,1,0:T(8,128)(2,1)S(1)} async-done(((bf16[16,3,2,16,1024]{4,3,2,1,0:T(8,128)(2,1)}), bf16[16,3,2,16,1024]{4,3,2,1,0:T(8,128)(2,1)S(1)}, u32[]{:S(2)}, u32[]{:S(2)}) %all-to-all-start) | async-done | bytes 3145760 | tf_op jit(solution)/shard_map/all_to_all | solution.py:495
  126.0 13.9 %correlate.1 = f32[16,2,16,128,128]{4,3,2,1,0:T(8,128)} custom-call(s32[2,16]{1,0:T(2,128)S(1)} %get-tuple-element.24.blocks, bf16[4,2,16,1024]{3,2,1,0:T(8,128)(2,1)} %get-tuple-element.34.refs_0_, bf16[4,2,16,1024]{3,2,1,0:T(8,128)(2,1)} %copy-done.1, bf16[4,2,16,1024]{3,2,1,0:T(8,128)(2,1)} %copy-done.2, ...), custom_call_target="tpu_custom_call" | custom-call | flops 2147483648 | bytes 37748736 | tf_op jit(solution)/shard_map/correlate/pallas_call | solution.py:442
Async XLA Ops:
  6.0 26.8 %collective-permute-start.7 = (bf16[3,512,512]{2,1,0:T(8,128)(2,1)S(1)}, bf16[3,512,512]{2,1,0:T(8,128)(2,1)S(1)}, u32[]{:S(2)}, u32[]{:S(2)}) collective-permute-start(bf16[3,512,512]{2,1,0:T(8,128)(2,1)S(1)} %get-tuple-element.28.up.own), channel_id=1, source_target_pairs={{0,1},{1,2},{2,3},{3,4},{4,5},{5,6},{6,7},{7,8},{8,9},{9,10},{10,1... | collective-permute-start | bytes 4718600 | tf_op jit(solution)/shard_map/ppermute | solution.py:30
  14.1 32.1 %collective-permute-start.6 = (bf16[3,512,512]{2,1,0:T(8,128)(2,1)S(1)}, bf16[3,512,512]{2,1,0:T(8,128)(2,1)S(1)}, u32[]{:S(2)}, u32[]{:S(2)}) collective-permute-start(bf16[3,512,512]{2,1,0:T(8,128)(2,1)S(1)} %get-tuple-element.29.down.own), channel_id=1, source_target_pairs={{0,15},{1,0},{2,1},{3,2},{4,3},{5,4},{6,5},{7,6},{8,7},{9,8},{10,9... | collective-permute-start | bytes 4718600 | tf_op jit(solution)/shard_map/ppermute | solution.py:30
  19.0 37.1 %collective-permute-start = (bf16[4,2,16,1024]{3,2,1,0:T(8,128)(2,1)}, bf16[4,2,16,1024]{3,2,1,0:T(8,128)(2,1)}, u32[]{:S(2)}, u32[]{:S(2)}) collective-permute-start(bf16[4,2,16,1024]{3,2,1,0:T(8,128)(2,1)} %get-tuple-element.31), channel_id=1, source_target_pairs={{0,4},{1,5},{2,6},{3,7},{4,0},{5,1},{6,2},{7,3},{8,12},{9,13},{10,... | collective-permute-start | bytes 786440 | tf_op jit(solution)/shard_map/ppermute | solution.py:294
  19.2 36.9 %collective-permute-start.1 = (bf16[4,2,16,1024]{3,2,1,0:T(8,128)(2,1)}, bf16[4,2,16,1024]{3,2,1,0:T(8,128)(2,1)}, u32[]{:S(2)}, u32[]{:S(2)}) collective-permute-start(bf16[4,2,16,1024]{3,2,1,0:T(8,128)(2,1)} %get-tuple-element.32), channel_id=1, source_target_pairs={{0,8},{1,9},{2,10},{3,11},{4,12},{5,13},{6,14},{7,15},{8,0},{9,1},... | collective-permute-start | bytes 786440 | tf_op jit(solution)/shard_map/ppermute | solution.py:294
  21.6 34.6 %collective-permute-start.2 = (bf16[4,2,16,1024]{3,2,1,0:T(8,128)(2,1)}, bf16[4,2,16,1024]{3,2,1,0:T(8,128)(2,1)}, u32[]{:S(2)}, u32[]{:S(2)}) collective-permute-start(bf16[4,2,16,1024]{3,2,1,0:T(8,128)(2,1)} %get-tuple-element.33), channel_id=1, source_target_pairs={{0,12},{1,13},{2,14},{3,15},{4,8},{5,9},{6,10},{7,11},{8,4},{9,5},... | collective-permute-start | bytes 786440 | tf_op jit(solution)/shard_map/ppermute | solution.py:294
  48.7 77.4 %all-to-all-start = ((bf16[16,3,2,16,1024]{4,3,2,1,0:T(8,128)(2,1)}), bf16[16,3,2,16,1024]{4,3,2,1,0:T(8,128)(2,1)S(1)}, u32[]{:S(2)}, u32[]{:S(2)}) async-start(bf16[16,3,2,16,1024]{4,3,2,1,0:T(8,128)(2,1)} %later_spectra.3), calls=%async_computation | async-start | bytes 6291456 | tf_op jit(solution)/shard_map/all_to_all | solution.py:495
  56.1 1.0 copy-start
  59.3 2.5 %collective-permute-start.3 = (bf16[4,2,16,1024]{3,2,1,0:T(8,128)(2,1)}, bf16[4,2,16,1024]{3,2,1,0:T(8,128)(2,1)S(1)}, u32[]{:S(2)}, u32[]{:S(2)}) collective-permute-start(bf16[4,2,16,1024]{3,2,1,0:T(8,128)(2,1)} %get-tuple-element.35), channel_id=1, source_target_pairs={{0,1},{1,0},{2,3},{3,2},{4,5},{5,4},{6,7},{7,6},{8,9},{9,8},{10,11... | collective-permute-start | bytes 786440 | tf_op jit(solution)/shard_map/ppermute | solution.py:304
  59.7 20.1 %collective-permute-start.4 = (bf16[4,2,16,1024]{3,2,1,0:T(8,128)(2,1)}, bf16[4,2,16,1024]{3,2,1,0:T(8,128)(2,1)S(1)}, u32[]{:S(2)}, u32[]{:S(2)}) collective-permute-start(bf16[4,2,16,1024]{3,2,1,0:T(8,128)(2,1)} %get-tuple-element.36), channel_id=1, source_target_pairs={{0,2},{1,3},{2,0},{3,1},{4,6},{5,7},{6,4},{7,5},{8,10},{9,11},{10,... | collective-permute-start | bytes 786440 | tf_op jit(solution)/shard_map/ppermute | solution.py:304
  61.7 24.2 %collective-permute-start.5 = (bf16[4,2,16,1024]{3,2,1,0:T(8,128)(2,1)}, bf16[4,2,16,1024]{3,2,1,0:T(8,128)(2,1)}, u32[]{:S(2)}, u32[]{:S(2)}) collective-permute-start(bf16[4,2,16,1024]{3,2,1,0:T(8,128)(2,1)} %get-tuple-element.37), channel_id=1, source_target_pairs={{0,3},{1,2},{2,1},{3,0},{4,7},{5,6},{6,5},{7,4},{8,11},{9,10},{10,... | collective-permute-start | bytes 786440 | tf_op jit(solution)/shard_map/ppermute | solution.py:304
  61.8 18.0 %copy-start.1 = (bf16[4,2,16,1024]{3,2,1,0:T(8,128)(2,1)}, bf16[4,2,16,1024]{3,2,1,0:T(8,128)(2,1)S(1)}, u32[]{:S(2)}) copy-start(bf16[4,2,16,1024]{3,2,1,0:T(8,128)(2,1)S(1)} %collective-permute-done.3.refs_1_) | copy-start | bytes 786436
  79.8 0.7 copy-start.2

commit v10 on v9

--- a/solution.py
+++ b/solution.py
@@ -409,7 +409,7 @@
                         256 + at : 256 + at + width
                     ]
 
-        @pl.loop(0, per, unroll=4)
+        @pl.loop(0, per, unroll=8)
         def _(f):
             across[f % 2] = plain[f].T
             for b in range(blocks.shape[1]):

time: 140 us -> 141 us (level)
  no operation moved by 1% of the time
where the time goes in v10:
time: 141 us; the launch traced here: 140 us
  waiting for transfers between devices  85.6 us (61%)
  Pallas kernels  36.3 us (26%)
  starting transfers between devices  16.4 us (12%)
  local copies, waits for them, and re-layouts  1.65 us (1%)
    all_to_all x1, waiting for transfers between devices, body(): rest = lax.all_to_all(rest, 'tm', split_axis=0, concat_axis=0, tiled=True)  40.1 us
    ppermute x3, waiting for transfers between devices, within_plane(): lax.ppermute(block, 'tm', [(i, i ^ q) for i in range(count)])  23.4 us
    ppermute x2, waiting for transfers between devices, shifted(): return lax.ppermute(block, axis, route)  22 us
    pallas_call x1, Pallas kernels, correlate(): pl.pallas_call(functools.partial(correlate_kernel, 1.0 / (groups * TAPS))...  14 us
    pallas_call x2, Pallas kernels, select(): pl.pallas_call(right_kernel if side else left_kernel, in_specs=[ANYWHERE,...  10.4 us
    all_to_all x1, starting transfers between devices, body(): rest = lax.all_to_all(rest, 'tm', split_axis=0, concat_axis=0, tiled=True)  7.44 us
    pallas_call x2, Pallas kernels, later_spectra(): pl.pallas_call(functools.partial(spectra_kernel, side), in_specs=[INSIDE]...  4.89 us
    pallas_call x1, Pallas kernels, first_spectra(): pl.pallas_call(functools.partial(first_kernel, planes), in_specs=[INSIDE]...  4.81 us
  transfers between devices with their start and end apart: 9, of which 5 were waited for; matrix products, arithmetic and copies ran while one was open for 0% of the time, Pallas kernels for 12%

profile of v10, /device:TPU:15, one launch (start us, length us, event | category | flops | bytes accessed | tf_op | source)
XLA Modules:
  0.0 140.2 jit_solution(5449708598412729892)
XLA Ops:
  0.0 6.0 %select.2 = (bf16[3,512,512]{2,1,0:T(8,128)(2,1)S(1)}, bf16[2048,512]{1,0:T(8,128)(2,1)S(1)}, bf16[4,512,2048]{2,1,0:T(8,128)(2,1)S(1)}, s32[2,16]{1,0:T(2,128)S(1)}) custom-call(s32[2,16]{1,0:T(2,128)} %bitcast.6, bf16[4,512,2048]{2,1,0:T(8,128)(2,1)} %bitcast.3, s32[16,128]{1,0:T(8,128)} %bitcast.4), custom_call_target="tpu_custom_call" | custom-call | flops 3221225472 | bytes 10485760 | tf_op jit(solution)/shard_map/select/pallas_call | solution.py:161
  6.0 3.7 %collective-permute-start.7 = (bf16[3,512,512]{2,1,0:T(8,128)(2,1)S(1)}, bf16[3,512,512]{2,1,0:T(8,128)(2,1)S(1)}, u32[]{:S(2)}, u32[]{:S(2)}) collective-permute-start(bf16[3,512,512]{2,1,0:T(8,128)(2,1)S(1)} %get-tuple-element.28.up.own), channel_id=1, source_target_pairs={{0,1},{1,2},{2,3},{3,4},{4,5},{5,6},{6,7},{7,8},{8,9},{9,10},{10,1... | collective-permute-start | bytes 4718600 | tf_op jit(solution)/shard_map/ppermute | solution.py:30
  9.7 4.4 %select.3 = (bf16[3,512,512]{2,1,0:T(8,128)(2,1)S(1)}, bf16[2048,512]{1,0:T(8,128)(2,1)S(1)}) custom-call(s32[2,16]{1,0:T(2,128)} %bitcast.7, bf16[4,512,2048]{2,1,0:T(8,128)(2,1)S(1)} %get-tuple-element.25.volts, s32[16,128]{1,0:T(8,128)} %bitcast.5), custom_call_target="tpu_custom_call" | custom-call | flops 3221225472 | bytes 10485760 | tf_op jit(solution)/shard_map/select/pallas_call | solution.py:161
  14.1 0.1 collective-permute-start.6
  14.2 4.8 %first_spectra.1 = (bf16[512,512]{1,0:T(8,128)(2,1)S(1)}, bf16[512,512]{1,0:T(8,128)(2,1)S(1)}, f32[4,512,128]{2,1,0:T(8,128)S(1)}, bf16[512,512]{1,0:T(8,128)(2...) custom-call(bf16[4,512,2048]{2,1,0:T(8,128)(2,1)S(1)} %get-tuple-ele, ...), custom_call_target="tpu_custom_call" | custom-call | flops 2684354560 | bytes 16777216 | tf_op jit(solution)/shard_map/first_spectra/pallas_call | solution.py:228
  19.0 0.2 collective-permute-start
  19.2 2.3 %collective-permute-start.1 = (bf16[4,2,16,1024]{3,2,1,0:T(8,128)(2,1)}, bf16[4,2,16,1024]{3,2,1,0:T(8,128)(2,1)}, u32[]{:S(2)}, u32[]{:S(2)}) collective-permute-start(bf16[4,2,16,1024]{3,2,1,0:T(8,128)(2,1)} %get-tuple-element.32), channel_id=1, source_target_pairs={{0,8},{1,9},{2,10},{3,11},{4,12},{5,13},{6,14},{7,15},{8,0},{9,1},... | collective-permute-start | bytes 786440 | tf_op jit(solution)/shard_map/ppermute | solution.py:294
  21.6 0.2 collective-permute-start.2
  21.7 11.1 %collective-permute-done.7.halo = bf16[3,512,512]{2,1,0:T(8,128)(2,1)S(1)} collective-permute-done((bf16[3,512,512]{2,1,0:T(8,128)(2,1)S(1)}, bf16[3,512,512]{2,1,0:T(8,128)(2,1)S(1)}, u32[]{:S(2)}, u32[]{:S(2)}) %collective-permute-start.7) | collective-permute-done | bytes 1572896 | tf_op jit(solution)/shard_map/ppermute | solution.py:30
  32.9 2.4 %later_spectra.2.refs_0_ = bf16[16,3,2,16,1024]{4,3,2,1,0:T(8,128)(2,1)} custom-call(bf16[3,512,512]{2,1,0:T(8,128)(2,1)S(1)} %collective-permute-done.7.halo, bf16[3,512,512]{2,1,0:T(8,128)(2,1)S(1)} %get-tuple-element.28.up.own, bf16[512,512]{1,0:T(8,128)(2,1)S(1)} %get-tuple-element.41.kept, f32[4,512,128]{2,1,0:T(8,128)S(1)} %get-tuple-element.39.taps, ...), custom_call_target="tpu_custom_call" | custom-call | flops 80530636800 | bytes 6291456 | tf_op jit(solution)/shard_map/later_spectra/pallas_call | solution.py:346
  35.3 10.9 %collective-permute-done.6.halo = bf16[3,512,512]{2,1,0:T(8,128)(2,1)S(1)} collective-permute-done((bf16[3,512,512]{2,1,0:T(8,128)(2,1)S(1)}, bf16[3,512,512]{2,1,0:T(8,128)(2,1)S(1)}, u32[]{:S(2)}, u32[]{:S(2)}) %collective-permute-start.6) | collective-permute-done | bytes 1572896 | tf_op jit(solution)/shard_map/ppermute | solution.py:30
  46.2 2.4 %later_spectra.3 = bf16[16,3,2,16,1024]{4,3,2,1,0:T(8,128)(2,1)} custom-call(bf16[3,512,512]{2,1,0:T(8,128)(2,1)S(1)} %collective-permute-done.6.halo, bf16[3,512,512]{2,1,0:T(8,128)(2,1)S(1)} %get-tuple-element.29.down.own, bf16[512,512]{1,0:T(8,128)(2,1)S(1)} %get-tuple-element.38.kept, ...), custom_call_target="tpu_custom_call", output_to_operand_aliasing={{}: (5, {})} | custom-call | flops 80530636800 | bytes 6291456 | tf_op jit(solution)/shard_map/later_spectra/pallas_call | solution.py:346
  48.7 7.4 %all-to-all-start = ((bf16[16,3,2,16,1024]{4,3,2,1,0:T(8,128)(2,1)}), bf16[16,3,2,16,1024]{4,3,2,1,0:T(8,128)(2,1)S(1)}, u32[]{:S(2)}, u32[]{:S(2)}) async-start(bf16[16,3,2,16,1024]{4,3,2,1,0:T(8,128)(2,1)} %later_spectra.3), calls=%async_computation | async-start | bytes 6291456 | tf_op jit(solution)/shard_map/all_to_all | solution.py:495
  56.1 0.0 collective-permute-done.refs_1_
  56.1 0.0 collective-permute-done.1.refs_2_
  56.1 0.0 collective-permute-done.2.refs_3_
  56.1 0.0 copy-start
  56.1 0.9 copy-done
  57.1 2.2 %regroup.1 = (bf16[4,2,16,1024]{3,2,1,0:T(8,128)(2,1)}, bf16[4,2,16,1024]{3,2,1,0:T(8,128)(2,1)}, bf16[4,2,16,1024]{3,2,1,0:T(8,128)(2,1)}, bf16[4,2,16,1024]{3,2,1,0:T(8,128)(2,1)}) custom-call(bf16[4,2,16,1024]{3,2,1,0:T(8,128)(2,1)S(1)} %copy-done, bf16[4,2,16,1024]{3,2,1,0:T(8,128)(2,1)} %collective-permute-done.refs_1_, ...), custom_call_target="tpu_custom_call" | custom-call | flops 137438953472 | bytes 2097152 | tf_op jit(solution)/shard_map/regroup/pallas_call | solution.py:275
  59.3 0.4 collective-permute-start.3
  59.7 2.0 %collective-permute-start.4 = (bf16[4,2,16,1024]{3,2,1,0:T(8,128)(2,1)}, bf16[4,2,16,1024]{3,2,1,0:T(8,128)(2,1)S(1)}, u32[]{:S(2)}, u32[]{:S(2)}) collective-permute-start(bf16[4,2,16,1024]{3,2,1,0:T(8,128)(2,1)} %get-tuple-element.36), channel_id=1, source_target_pairs={{0,2},{1,3},{2,0},{3,1},{4,6},{5,7},{6,4},{7,5},{8,10},{9,11},{10,... | collective-permute-start | bytes 786440 | tf_op jit(solution)/shard_map/ppermute | solution.py:304
  61.7 0.0 collective-permute-start.5
  61.8 0.0 collective-permute-done.3.refs_1_
  61.8 0.0 copy-start.1
  61.8 18.0 %collective-permute-done.4.refs_2_ = bf16[4,2,16,1024]{3,2,1,0:T(8,128)(2,1)S(1)} collective-permute-done((bf16[4,2,16,1024]{3,2,1,0:T(8,128)(2,1)}, bf16[4,2,16,1024]{3,2,1,0:T(8,128)(2,1)S(1)}, u32[]{:S(2)}, u32[]{:S(2)}) %collective-permute-start.4) | collective-permute-done | bytes 262176 | tf_op jit(solution)/shard_map/ppermute | solution.py:304
  79.8 0.0 copy-done.1
  79.8 0.0 copy-start.2
  79.8 0.7 copy-done.2
  80.5 5.4 %collective-permute-done.5.refs_3_ = bf16[4,2,16,1024]{3,2,1,0:T(8,128)(2,1)} collective-permute-done((bf16[4,2,16,1024]{3,2,1,0:T(8,128)(2,1)}, bf16[4,2,16,1024]{3,2,1,0:T(8,128)(2,1)}, u32[]{:S(2)}, u32[]{:S(2)}) %collective-permute-start.5) | collective-permute-done | bytes 262176 | tf_op jit(solution)/shard_map/ppermute | solution.py:304
  85.9 40.1 %all-to-all-done.refs_4_ = bf16[16,3,2,16,1024]{4,3,2,1,0:T(8,128)(2,1)S(1)} async-done(((bf16[16,3,2,16,1024]{4,3,2,1,0:T(8,128)(2,1)}), bf16[16,3,2,16,1024]{4,3,2,1,0:T(8,128)(2,1)S(1)}, u32[]{:S(2)}, u32[]{:S(2)}) %all-to-all-start) | async-done | bytes 3145760 | tf_op jit(solution)/shard_map/all_to_all | solution.py:495
  126.0 14.0 %correlate.1 = f32[16,2,16,128,128]{4,3,2,1,0:T(8,128)} custom-call(s32[2,16]{1,0:T(2,128)S(1)} %get-tuple-element.24.blocks, bf16[4,2,16,1024]{3,2,1,0:T(8,128)(2,1)} %get-tuple-element.34.refs_0_, bf16[4,2,16,1024]{3,2,1,0:T(8,128)(2,1)} %copy-done.1, bf16[4,2,16,1024]{3,2,1,0:T(8,128)(2,1)} %copy-done.2, ...), custom_call_target="tpu_custom_call" | custom-call | flops 2147483648 | bytes 37748736 | tf_op jit(solution)/shard_map/correlate/pallas_call | solution.py:442
Async XLA Ops:
  6.0 26.8 %collective-permute-start.7 = (bf16[3,512,512]{2,1,0:T(8,128)(2,1)S(1)}, bf16[3,512,512]{2,1,0:T(8,128)(2,1)S(1)}, u32[]{:S(2)}, u32[]{:S(2)}) collective-permute-start(bf16[3,512,512]{2,1,0:T(8,128)(2,1)S(1)} %get-tuple-element.28.up.own), channel_id=1, source_target_pairs={{0,1},{1,2},{2,3},{3,4},{4,5},{5,6},{6,7},{7,8},{8,9},{9,10},{10,1... | collective-permute-start | bytes 4718600 | tf_op jit(solution)/shard_map/ppermute | solution.py:30
  14.1 32.1 %collective-permute-start.6 = (bf16[3,512,512]{2,1,0:T(8,128)(2,1)S(1)}, bf16[3,512,512]{2,1,0:T(8,128)(2,1)S(1)}, u32[]{:S(2)}, u32[]{:S(2)}) collective-permute-start(bf16[3,512,512]{2,1,0:T(8,128)(2,1)S(1)} %get-tuple-element.29.down.own), channel_id=1, source_target_pairs={{0,15},{1,0},{2,1},{3,2},{4,3},{5,4},{6,5},{7,6},{8,7},{9,8},{10,9... | collective-permute-start | bytes 4718600 | tf_op jit(solution)/shard_map/ppermute | solution.py:30
  19.0 37.1 %collective-permute-start = (bf16[4,2,16,1024]{3,2,1,0:T(8,128)(2,1)}, bf16[4,2,16,1024]{3,2,1,0:T(8,128)(2,1)}, u32[]{:S(2)}, u32[]{:S(2)}) collective-permute-start(bf16[4,2,16,1024]{3,2,1,0:T(8,128)(2,1)} %get-tuple-element.31), channel_id=1, source_target_pairs={{0,4},{1,5},{2,6},{3,7},{4,0},{5,1},{6,2},{7,3},{8,12},{9,13},{10,... | collective-permute-start | bytes 786440 | tf_op jit(solution)/shard_map/ppermute | solution.py:294
  19.2 36.9 %collective-permute-start.1 = (bf16[4,2,16,1024]{3,2,1,0:T(8,128)(2,1)}, bf16[4,2,16,1024]{3,2,1,0:T(8,128)(2,1)}, u32[]{:S(2)}, u32[]{:S(2)}) collective-permute-start(bf16[4,2,16,1024]{3,2,1,0:T(8,128)(2,1)} %get-tuple-element.32), channel_id=1, source_target_pairs={{0,8},{1,9},{2,10},{3,11},{4,12},{5,13},{6,14},{7,15},{8,0},{9,1},... | collective-permute-start | bytes 786440 | tf_op jit(solution)/shard_map/ppermute | solution.py:294
  21.6 34.6 %collective-permute-start.2 = (bf16[4,2,16,1024]{3,2,1,0:T(8,128)(2,1)}, bf16[4,2,16,1024]{3,2,1,0:T(8,128)(2,1)}, u32[]{:S(2)}, u32[]{:S(2)}) collective-permute-start(bf16[4,2,16,1024]{3,2,1,0:T(8,128)(2,1)} %get-tuple-element.33), channel_id=1, source_target_pairs={{0,12},{1,13},{2,14},{3,15},{4,8},{5,9},{6,10},{7,11},{8,4},{9,5},... | collective-permute-start | bytes 786440 | tf_op jit(solution)/shard_map/ppermute | solution.py:294
  48.7 77.4 %all-to-all-start = ((bf16[16,3,2,16,1024]{4,3,2,1,0:T(8,128)(2,1)}), bf16[16,3,2,16,1024]{4,3,2,1,0:T(8,128)(2,1)S(1)}, u32[]{:S(2)}, u32[]{:S(2)}) async-start(bf16[16,3,2,16,1024]{4,3,2,1,0:T(8,128)(2,1)} %later_spectra.3), calls=%async_computation | async-start | bytes 6291456 | tf_op jit(solution)/shard_map/all_to_all | solution.py:495
  56.1 1.0 copy-start
  59.3 2.5 %collective-permute-start.3 = (bf16[4,2,16,1024]{3,2,1,0:T(8,128)(2,1)}, bf16[4,2,16,1024]{3,2,1,0:T(8,128)(2,1)S(1)}, u32[]{:S(2)}, u32[]{:S(2)}) collective-permute-start(bf16[4,2,16,1024]{3,2,1,0:T(8,128)(2,1)} %get-tuple-element.35), channel_id=1, source_target_pairs={{0,1},{1,0},{2,3},{3,2},{4,5},{5,4},{6,7},{7,6},{8,9},{9,8},{10,11... | collective-permute-start | bytes 786440 | tf_op jit(solution)/shard_map/ppermute | solution.py:304
  59.7 20.1 %collective-permute-start.4 = (bf16[4,2,16,1024]{3,2,1,0:T(8,128)(2,1)}, bf16[4,2,16,1024]{3,2,1,0:T(8,128)(2,1)S(1)}, u32[]{:S(2)}, u32[]{:S(2)}) collective-permute-start(bf16[4,2,16,1024]{3,2,1,0:T(8,128)(2,1)} %get-tuple-element.36), channel_id=1, source_target_pairs={{0,2},{1,3},{2,0},{3,1},{4,6},{5,7},{6,4},{7,5},{8,10},{9,11},{10,... | collective-permute-start | bytes 786440 | tf_op jit(solution)/shard_map/ppermute | solution.py:304
  61.7 24.2 %collective-permute-start.5 = (bf16[4,2,16,1024]{3,2,1,0:T(8,128)(2,1)}, bf16[4,2,16,1024]{3,2,1,0:T(8,128)(2,1)}, u32[]{:S(2)}, u32[]{:S(2)}) collective-permute-start(bf16[4,2,16,1024]{3,2,1,0:T(8,128)(2,1)} %get-tuple-element.37), channel_id=1, source_target_pairs={{0,3},{1,2},{2,1},{3,0},{4,7},{5,6},{6,5},{7,4},{8,11},{9,10},{10,... | collective-permute-start | bytes 786440 | tf_op jit(solution)/shard_map/ppermute | solution.py:304
  61.8 18.0 %copy-start.1 = (bf16[4,2,16,1024]{3,2,1,0:T(8,128)(2,1)}, bf16[4,2,16,1024]{3,2,1,0:T(8,128)(2,1)S(1)}, u32[]{:S(2)}) copy-start(bf16[4,2,16,1024]{3,2,1,0:T(8,128)(2,1)S(1)} %collective-permute-done.3.refs_1_) | copy-start | bytes 786436
  79.8 0.7 copy-start.2
